TPU v7x, 512 devices: a whole 4x8x8 slice. The times are simulated.
512 devices in a mesh: week: 32 (over z_hi, y, core), markov: 16 (over x, z_lo).
Axes of the slice: x: 4, y: 8, z: 8 (z_hi: 2, z_lo: 4; z = z_hi * 4 + z_lo), core: 2. Of those that a mesh axis runs over, the one named last changes fastest.
Arguments:
- trial_states: float32 [32, 16, 32, 2048], P('week', 'markov'), may hold values from -6 to 6
- successor: int32 [32, 16, 32, 1], P('week', 'markov'), may hold values from 0 to 15; in each aligned block of 32 rows (0 to 31, 32 to 63, ..., all dimensions but the last counted through in order) at most 4 rows name the same one
- inflow: float32 [32, 16, 2048], P('week', 'markov'), may hold values from -6 to 6
- unit_cost: float32 [32, 16, 2048], P('week', 'markov'), may hold values from -3 to 3
- curvature: float32 [32, 16, 2048], P('week', 'markov'), may hold values from 0.5 to 8
- target: float32 [32, 16, 2048], P('week', 'markov'), may hold values from -6 to 6
- release_cap: float32 [32, 16, 2048], P('week', 'markov'), may hold values from 0.3 to 3
- block_values: float32 [32, 16, 16, 2, 128, 128], P('week', 'markov'), may hold values from -0.1875 to 0.1875
- block_cols: int32 [32, 16, 16, 2], P('week', 'markov'), may hold values from 0 to 15
Outputs:
- cut_slope: float32 [32, 16, 32, 2048], P('week', 'markov')
- cut_intercept: float32 [32, 16, 32], P('week', 'markov')
Inputs may be any that keep to these rules, and one draw needn't show every extreme that they name: Among the 32 rows of one node, at most 4 name the same successor state, and in every draw some node has exactly 4 rows naming one state.
All inputs are finite; a program needn't handle non-finite values.
Results may differ from a plain program's by a relative error of at most 0.0003.
Values sent between devices are 32-bit elements; how exact they have to be, the bound alone decides.
No kernel may reach another device: no remote copies, remote signals or barrier semaphores. Data moves between devices by JAX's collectives and lax.ppermute only.
A program may use at most 64 MiB of HBM per device.

v0:
```python
import jax
import jax.numpy as jnp
from jax import lax
from jax.sharding import PartitionSpec as P

ITERS = 4


highest = lax.Precision.HIGHEST
dual_step = 0.5
primal_step = 0.5


def shifted(value, axis, steps):
    count = lax.axis_size(axis)
    pairs = [(source, (source + steps) % count) for source in range(count)]
    return lax.ppermute(value, axis, pairs)


def solve_rows(rows, inflow, unit_cost, curvature, target, release_cap, block_values, block_cols):
    count, width = rows.shape
    nblk, kblk, bsize = (block_values.shape[0], block_values.shape[1], block_values.shape[2])
    picker = (block_cols[:, :, None] == jnp.arange(nblk, dtype=jnp.int32)[None, None, :]).astype(
        jnp.float32
    )

    def apply_fwd(field):
        split = field.reshape(count, nblk, bsize)
        taken = jnp.einsum("rjb,nkj->rnkb", split, picker, precision=highest)
        mixed = jnp.einsum("rnkb,nkcb->rnc", taken, block_values, precision=highest)
        return field + mixed.reshape(count, width)

    base = rows + inflow[None, :] - target[None, :]
    shrink = curvature / (curvature + dual_step)
    release = jnp.zeros((count, width), jnp.float32)
    extrap = jnp.zeros((count, width), jnp.float32)
    dual = jnp.zeros((count, width), jnp.float32)
    for sweep_index in range(ITERS):
        dual = (dual + dual_step * (base - apply_fwd(extrap))) * shrink[None, :]
        apply_split = dual.reshape(count, nblk, bsize)
        spread = jnp.einsum("rnc,nkcb->rnkb", apply_split, block_values, precision=highest)
        summed = jnp.einsum("rnkb,nkj->rjb", spread, picker, precision=highest)
        fresh = jnp.clip(
            release + primal_step * (dual + summed.reshape(count, width) - unit_cost[None, :]),
            0.0,
            release_cap[None, :],
        )
        extrap = 2.0 * fresh - release
        release = fresh
    storage = rows + inflow[None, :] - apply_fwd(release)
    gap = storage - target[None, :]
    value = jnp.mean(unit_cost[None, :] * release + 0.5 * curvature[None, :] * gap * gap, axis=1)
    icpt = value - jnp.mean(dual * rows, axis=1)
    return (dual, icpt)


def slot_numbers(dest_row, states, capacity):
    marked = (dest_row[:, None] == jnp.arange(states, dtype=jnp.int32)[None, :]).astype(jnp.int32)
    ranked = jnp.sum(jnp.cumsum(marked, axis=0) * marked, axis=1) - 1
    return dest_row * capacity + ranked


def on_device(
    trial_states,
    successor,
    inflow,
    unit_cost,
    curvature,
    target,
    release_cap,
    block_values,
    block_cols,
):
    states = lax.axis_size("markov")
    tr_rows = trial_states.shape[2]
    width = trial_states.shape[3]
    capacity = 2 * tr_rows // states
    own_rows = trial_states.reshape(tr_rows, width)
    own_dest = successor.reshape(tr_rows)
    node_data = (
        inflow.reshape(width),
        unit_cost.reshape(width),
        curvature.reshape(width),
        target.reshape(width),
        release_cap.reshape(width),
        block_values[0, 0],
        block_cols[0, 0],
    )
    slot_values = slot_numbers(own_dest, states, capacity).astype(jnp.float32)
    placer = (
        slot_values[None, :] == jnp.arange(states * capacity, dtype=jnp.float32)[:, None]
    ).astype(jnp.float32)
    packed = jnp.dot(placer, own_rows, precision=highest).reshape(states, capacity, width)
    arrived = lax.all_to_all(packed, "markov", split_axis=0, concat_axis=0, tiled=True)
    arrived = shifted(arrived, "week", 1)
    count = arrived.shape[1]
    slopes, icpts = solve_rows(arrived.reshape(-1, width), *node_data)
    slopes, icpts = (slopes.reshape(states, count, width), icpts.reshape(states, count))
    slopes, icpts = shifted((slopes, icpts), "week", -1)
    slopes, icpts = (
        lax.all_to_all(slopes, "markov", split_axis=0, concat_axis=0, tiled=True),
        lax.all_to_all(icpts, "markov", split_axis=0, concat_axis=0, tiled=True),
    )
    mine = jnp.einsum("qt,qr->tr", placer, slopes.reshape(-1, width), precision=highest)
    mine_icpt = jnp.einsum("qt,q->t", placer, icpts.reshape(-1), precision=highest)
    return (mine.reshape(1, 1, tr_rows, width), mine_icpt.reshape(1, 1, tr_rows))


def solution(mesh):
    return jax.shard_map(
        on_device,
        mesh=mesh,
        in_specs=(
            P("week", "markov", None, None),
            P("week", "markov", None, None),
            P("week", "markov", None),
            P("week", "markov", None),
            P("week", "markov", None),
            P("week", "markov", None),
            P("week", "markov", None),
            P("week", "markov", None, None, None, None),
            P("week", "markov", None, None),
        ),
        out_specs=(P("week", "markov", None, None), P("week", "markov", None)),
        check_vma=False,
    )
```

profile of v0, /device:TPU:57, one launch (start us, length us, event | category | flops | bytes accessed | tf_op | source)
XLA Modules:
  0.0 148.0 jit_solution(10006494290308423872)
XLA Ops:
  0.7 0.9 fusion.132
  1.6 0.8 select_reduce_fusion
  3.1 1.4 fusion.114
  4.5 1.2 copy.40
  5.6 9.6 %all-to-all-start = ((f32[16,4,2048]{2,1,0:T(4,128)}), f32[16,4,2048]{2,1,0:T(4,128)}, u32[]{:S(2)}, u32[]{:S(2)}) async-start(f32[16,4,2048]{2,1,0:T(4,128)} %copy.40), calls=%async_computation | async-start | bytes 1048576 | tf_op jit(solution)/shard_map/all_to_all | solution.py:94
  15.3 1.4 convolution_bitcast_fusion.5
  16.7 14.4 %all-to-all-done = f32[16,4,2048]{2,1,0:T(4,128)} async-done(((f32[16,4,2048]{2,1,0:T(4,128)}), f32[16,4,2048]{2,1,0:T(4,128)}, u32[]{:S(2)}, u32[]{:S(2)}) %all-to-all-start) | async-done | bytes 524320 | tf_op jit(solution)/shard_map/all_to_all | solution.py:94
  31.0 8.8 %collective-permute-start = (f32[16,4,2048]{2,1,0:T(4,128)}, f32[16,4,2048]{2,1,0:T(4,128)}, u32[]{:S(2)}, u32[]{:S(2)}) collective-permute-start(f32[16,4,2048]{2,1,0:T(4,128)} %all-to-all-done), channel_id=1, source_target_pairs={{0,16},{16,32},{32,48},{48,64},{64,80},{80,96},{96,112},{112,128},... | collective-permute-start | bytes 1572872 | tf_op jit(solution)/shard_map/ppermute | solution.py:17
  39.8 3.7 %fusion.30 = f32[64,16,128]{2,0,1:T(8,128)S(1)} fusion(f32[1,1,16,2,128,128]{5,4,3,2,1,0:T(8,128)S(1)} %copy-done, f32[64,16,2,128]{3,1,0,2:T(8,128)} %convolution_bitcast_fusion.5), kind=kOutput, calls=%fused_computation.28 | convolution fusion | flops 402653184 | bytes 3670016 | tf_op jit(solution)/shard_map/rnkb,nkcb->rnc/dot_general | solution.py:30
  43.8 1.0 reshape.690
  44.8 4.6 %collective-permute-done = f32[16,4,2048]{2,1,0:T(4,128)} collective-permute-done((f32[16,4,2048]{2,1,0:T(4,128)}, f32[16,4,2048]{2,1,0:T(4,128)}, u32[]{:S(2)}, u32[]{:S(2)}) %collective-permute-start) | collective-permute-done | bytes 524320 | tf_op jit(solution)/shard_map/ppermute | solution.py:17
  49.4 1.3 reshape.692
  50.8 1.4 fusion.18
  52.2 1.1 fusion.63
  53.9 0.8 convolution_bitcast_fusion.4
  54.7 3.3 %add_multiply_fusion.3 = (f32[64,16,128]{2,0,1:T(8,128)S(1)}, f32[64,16,128]{2,0,1:T(8,128)}) fusion(f32[16,128]{1,0:T(8,128)S(1)} %get-tuple-element.10, f32[16,128]{1,0:T(8,128)S(1)} %bitcast.264, f32[16,128]{1,0:T(8,128)S(1)} %bitcast.272, f32[64,16,128]{2,1,0:T(8,128)S(1)} %reshape.692, f32[64,16,128]{2,0,1:T(8,128)S(1)} %get-tuple-element.7, ...), kind=kOutput, calls=%fused_computation.96 | convolution fusion | flops 403963904 | bytes 5799936 | tf_op jit(solution)/shard_map/rnkb,nkcb->rnc/dot_general | solution.py:30
  58.0 1.3 fusion.21
  59.3 1.1 fusion.60
  61.3 1.0 convolution_bitcast_fusion.3
  62.3 3.3 %add_multiply_fusion.2 = (f32[64,16,128]{2,0,1:T(8,128)S(1)}, f32[64,16,128]{2,0,1:T(8,128)}) fusion(f32[64,16,128]{2,0,1:T(8,128)S(1)} %get-tuple-element.13, f32[64,16,128]{2,0,1:T(8,128)S(1)} %get-tuple-element.4, f32[16,128]{1,0:T(8,128)S(1)} %get-tuple-element.10, f32[16,128]{1,0:T(8,128)S(1)} %bitcast.265, f32[16,128]{1,0:T(8,128)S(1)} %bitcast.273, ...), kind=kOutput, calls=%fused_computation.94 | convolution fusion | flops 403570688 | bytes 5791744 | tf_op jit(solution)/shard_map/rnkb,nkcb->rnc/dot_general | solution.py:30
  65.6 1.3 fusion.24
  66.9 1.1 fusion.57
  68.3 0.8 convolution_bitcast_fusion.2
  69.2 2.5 %fusion.39 = f32[64,16,128]{2,0,1:T(8,128)S(1)} fusion(f32[1,1,16,2,128,128]{5,4,3,2,1,0:T(8,128)S(1)} %copy-done, f32[64,16,2,128]{3,1,0,2:T(8,128)S(1)} %convolution_bitcast_fusion.2), kind=kOutput, calls=%fused_computation.31 | convolution fusion | flops 402653184 | bytes 3670016 | tf_op jit(solution)/shard_map/rnkb,nkcb->rnc/dot_general | solution.py:30
  71.7 1.5 %fusion.27 = f32[64,16,2,128]{3,0,2,1:T(8,128)S(1)} fusion(f32[1,1,16,2,128,128]{5,4,3,2,1,0:T(8,128)S(1)} %copy-done, f32[64,16,128]{2,0,1:T(8,128)S(1)} %get-tuple-element.15, f32[64,16,128]{2,0,1:T(8,128)S(1)} %multiply_subtract_fusion, f32[64,16,128]{2,0,1:T(8,128)S(1)} %fusion.39, f32[16,128]{1,0:T(8,128)S(1)} %get-tuple-element.10, ...), kind=kOutput, calls=%fused_computation.22 | convolution fusion | flops 403570688 | bytes 5267456 | tf_op jit(solution)/shard_map/rnc,nkcb->rnkb/dot_general | solution.py:41
  73.3 1.1 copy.65
  74.4 1.1 convolution_bitcast_fusion.6
  75.5 0.8 fusion.89
  76.3 0.8 copy-done.5
  77.1 2.0 %convolution_bitcast_fusion.1 = f32[64,16,2,128]{3,1,0,2:T(8,128)} fusion(f32[64,16,128]{2,0,1:T(8,128)S(1)} %fusion.89, s32[16,2]{0,1:T(2,128)S(1)} %bitcast.297), kind=kOutput, calls=%fused_computation.23 | convolution fusion | flops 50332160 | bytes 1572992 | tf_op jit(solution)/shard_map/rjb,nkj->rnkb/dot_general | solution.py:29
  79.1 2.0 %reshape.699 = f32[16,4,2048]{2,1,0:T(4,128)} reshape(f32[64,16,128]{2,1,0:T(8,128)} %copy.65) | data formatting | bytes 1048576 | tf_op jit(solution)/shard_map/reshape | solution.py:31
  81.1 1.0 reshape.698
  82.1 2.2 %copy.58 = f32[64,16,128]{2,1,0:T(8,128)} copy(f32[64,16,128]{2,0,1:T(8,128)} %get-tuple-element.16) | data formatting | bytes 1048576 | tf_op jit(solution)/shard_map/rnkb,nkcb->rnc/transpose | solution.py:30
  84.3 2.0 %reshape.697 = f32[16,4,2048]{2,1,0:T(4,128)} reshape(f32[64,16,128]{2,1,0:T(8,128)} %copy.58) | data formatting | bytes 1048576 | tf_op jit(solution)/shard_map/reshape | solution.py:31
  86.3 1.0 reshape.696
  87.3 2.2 %copy.51 = f32[64,16,128]{2,1,0:T(8,128)} copy(f32[64,16,128]{2,0,1:T(8,128)} %get-tuple-element.14) | data formatting | bytes 1048576 | tf_op jit(solution)/shard_map/rnkb,nkcb->rnc/transpose | solution.py:30
  89.5 2.0 %reshape.695 = f32[16,4,2048]{2,1,0:T(4,128)} reshape(f32[64,16,128]{2,1,0:T(8,128)} %copy.51) | data formatting | bytes 1048576 | tf_op jit(solution)/shard_map/reshape | solution.py:31
  91.5 1.0 reshape.694
  92.5 3.9 %multiply_reduce_fusion = (f32[16,4]{1,0:T(8,128)S(1)}, f32[16,4,2048]{2,1,0:T(4,128)S(1)}) fusion(f32[16,4,2048]{2,1,0:T(4,128)} %collective-permute-done, f32[16,4,2048]{2,1,0:T(4,128)} %reshape.699, f32[16,4,2048]{2,1,0:T(4,128)} %reshape.698, f32[16,4,2048]{2,1,0:T(4,128)} %reshape.697, f32[16,4,2048]{2,1,0:T(4,128)} %reshape.696, ...), kind=kLoop, calls=%fused_computation.90 | loop fusion | flops 5636032 | bytes 4768000 | tf_op jit(solution)/shard_map/reduce_sum | solution.py:53
  96.4 1.9 %collective-permute-start.1 = (f32[16,4,2048]{2,1,0:T(4,128)S(1)}, f32[16,4,2048]{2,1,0:T(4,128)}, u32[]{:S(2)}, u32[]{:S(2)}) collective-permute-start(f32[16,4,2048]{2,1,0:T(4,128)S(1)} %get-tuple-element.3), channel_id=1, source_target_pairs={{0,496},{16,0},{32,16},{48,32},{64,48},{80,64},{96,80},{112,96},{1... | collective-permute-start | bytes 1572872 | tf_op jit(solution)/shard_map/ppermute | solution.py:17
  98.3 2.6 %fusion.75 = f32[64]{0:T(128)S(1)} fusion(f32[64,16,128]{2,0,1:T(8,128)S(1)} %copy-done.6, f32[1,1,16,2,128,128]{5,4,3,2,1,0:T(8,128)S(1)} %copy-done, f32[64,16,2,128]{3,1,0,2:T(8,128)S(1)} %copy-done.7, f32[64,16,128]{2,1,0:T(8,128)S(1)} %reshape.692, f32[16,128]{1,0:T(8,128)S(1)} %get-tuple-element.8, f32[16,128]{1,0:T(8,128)S(1)} %bitcast.283, ...), kind=kOutput, calls=%fused_computation.52 | convolution fusion | flops 403832768 | bytes 4227328 | tf_op jit(solution)/shard_map/rnkb,nkcb->rnc/dot_general | solution.py:30
  101.2 1.9 %collective-permute-start.2 = (f32[16,4]{0,1:T(4,128)S(1)}, f32[16,4]{0,1:T(4,128)S(1)}, u32[]{:S(2)}, u32[]{:S(2)}) collective-permute-start(f32[16,4]{0,1:T(4,128)S(1)} %multiply_subtract_fusion.2), channel_id=1, source_target_pairs={{0,496},{16,0},{32,16},{48,32},{64,48},{80,64},{96,80},{112,96},{1... | collective-permute-start | bytes 776 | tf_op jit(solution)/shard_map/ppermute | solution.py:17
  103.1 16.7 %collective-permute-done.2 = f32[16,4]{0,1:T(4,128)S(1)} collective-permute-done((f32[16,4]{0,1:T(4,128)S(1)}, f32[16,4]{0,1:T(4,128)S(1)}, u32[]{:S(2)}, u32[]{:S(2)}) %collective-permute-start.2) | collective-permute-done | bytes 288 | tf_op jit(solution)/shard_map/ppermute | solution.py:17
  119.9 12.2 %all_to_all.19 = f32[16,1,4]{2,1,0:T(1,128)S(1)} all-to-all(f32[16,1,4]{2,1,0:T(1,128)S(1)} %copy.73), channel_id=1, replica_groups=mesh['week'=32,'markov'=16] {'markov'}, dimensions={0} | all-to-all | bytes 512 | tf_op jit(solution)/shard_map/all_to_all | solution.py:102
  132.1 3.6 %all-to-all-start.1 = ((f32[16,4,2048]{2,1,0:T(4,128)}), f32[16,4,2048]{2,1,0:T(4,128)S(1)}, u32[]{:S(2)}, u32[]{:S(2)}) async-start(f32[16,4,2048]{2,1,0:T(4,128)} %collective-permute-done.1), calls=%async_computation.1 | async-start | bytes 1048576 | tf_op jit(solution)/shard_map/all_to_all | solution.py:101
  136.2 0.7 reduce.5
  137.6 9.2 %all-to-all-done.1 = f32[16,4,2048]{2,1,0:T(4,128)S(1)} async-done(((f32[16,4,2048]{2,1,0:T(4,128)}), f32[16,4,2048]{2,1,0:T(4,128)S(1)}, u32[]{:S(2)}, u32[]{:S(2)}) %all-to-all-start.1) | async-done | bytes 524320 | tf_op jit(solution)/shard_map/all_to_all | solution.py:101
  146.9 1.0 convolution_bitcast_fusion
  (47 shorter events, 4.5 us)
Async XLA Ops:
  0.6 39.2 %copy-start = (f32[1,1,16,2,128,128]{5,4,3,2,1,0:T(8,128)S(1)}, f32[1,1,16,2,128,128]{5,4,3,2,1,0:T(8,128)}, u32[]{:S(2)}) copy-start(f32[1,1,16,2,128,128]{5,4,3,2,1,0:T(8,128)} %param.16) | copy-start | bytes 6291460
  0.6 14.6 %copy-start.12 = (s32[1,1,16,2]{2,3,1,0:T(2,128)S(1)}, s32[1,1,16,2]{2,3,1,0:T(2,128)}, u32[]{:S(2)}) copy-start(s32[1,1,16,2]{2,3,1,0:T(2,128)} %param.17) | copy-start | bytes 388
  5.6 25.4 %all-to-all-start = ((f32[16,4,2048]{2,1,0:T(4,128)}), f32[16,4,2048]{2,1,0:T(4,128)}, u32[]{:S(2)}, u32[]{:S(2)}) async-start(f32[16,4,2048]{2,1,0:T(4,128)} %copy.40), calls=%async_computation | async-start | bytes 1048576 | tf_op jit(solution)/shard_map/all_to_all | solution.py:94
  16.7 28.1 %copy-start.13 = (f32[1,1,2048]{2,1,0:T(1,128)S(1)}, f32[1,1,2048]{2,1,0:T(1,128)}, u32[]{:S(2)}) copy-start(f32[1,1,2048]{2,1,0:T(1,128)} %param.13) | copy-start | bytes 24580
  31.0 18.4 %collective-permute-start = (f32[16,4,2048]{2,1,0:T(4,128)}, f32[16,4,2048]{2,1,0:T(4,128)}, u32[]{:S(2)}, u32[]{:S(2)}) collective-permute-start(f32[16,4,2048]{2,1,0:T(4,128)} %all-to-all-done), channel_id=1, source_target_pairs={{0,16},{16,32},{32,48},{48,64},{64,80},{80,96},{96,112},{112,128},... | collective-permute-start | bytes 1572872 | tf_op jit(solution)/shard_map/ppermute | solution.py:17
  43.5 7.3 %copy-start.8 = (f32[1,1,2048]{2,1,0:T(1,128)S(1)}, f32[1,1,2048]{2,1,0:T(1,128)}, u32[]{:S(2)}) copy-start(f32[1,1,2048]{2,1,0:T(1,128)} %param.14) | copy-start | bytes 24580
  43.5 7.3 %copy-start.9 = (f32[1,1,2048]{2,1,0:T(1,128)S(1)}, f32[1,1,2048]{2,1,0:T(1,128)}, u32[]{:S(2)}) copy-start(f32[1,1,2048]{2,1,0:T(1,128)} %param.11) | copy-start | bytes 24580
  50.8 2.6 %copy-start.10 = (f32[1,1,2048]{2,1,0:T(1,128)S(1)}, f32[1,1,2048]{2,1,0:T(1,128)}, u32[]{:S(2)}) copy-start(f32[1,1,2048]{2,1,0:T(1,128)} %param.12) | copy-start | bytes 24580
  50.8 2.6 %copy-start.11 = (f32[1,1,2048]{2,1,0:T(1,128)S(1)}, f32[1,1,2048]{2,1,0:T(1,128)}, u32[]{:S(2)}) copy-start(f32[1,1,2048]{2,1,0:T(1,128)} %param.15) | copy-start | bytes 24580
  53.4 1.3 copy-start.3
  60.4 0.8 copy-start.1
  76.2 0.8 copy-start.5
  82.1 4.2 %copy-start.2 = (f32[16,64,128,1]{2,0,3,1:T(8,128)S(1)}, f32[16,64,128,1]{2,0,3,1:T(8,128)}, u32[]{:S(2)}) copy-start(f32[16,64,128,1]{2,0,3,1:T(8,128)} %copy-done.1) | copy-start | bytes 1572868
  87.3 4.2 %copy-start.4 = (f32[16,64,128,1]{2,0,3,1:T(8,128)S(1)}, f32[16,64,128,1]{2,0,3,1:T(8,128)}, u32[]{:S(2)}) copy-start(f32[16,64,128,1]{2,0,3,1:T(8,128)} %copy-done.3) | copy-start | bytes 1572868
  92.5 5.8 %copy-start.6 = (f32[64,16,128]{2,0,1:T(8,128)S(1)}, f32[64,16,128]{2,0,1:T(8,128)}, u32[]{:S(2)}) copy-start(f32[64,16,128]{2,0,1:T(8,128)} %copy-done.5) | copy-start | bytes 1572868
  92.5 5.8 %copy-start.7 = (f32[64,16,2,128]{3,1,0,2:T(8,128)S(1)}, f32[64,16,2,128]{3,1,0,2:T(8,128)}, u32[]{:S(2)}) copy-start(f32[64,16,2,128]{3,1,0,2:T(8,128)} %convolution_bitcast_fusion.1) | copy-start | bytes 3145732
  96.4 35.7 %collective-permute-start.1 = (f32[16,4,2048]{2,1,0:T(4,128)S(1)}, f32[16,4,2048]{2,1,0:T(4,128)}, u32[]{:S(2)}, u32[]{:S(2)}) collective-permute-start(f32[16,4,2048]{2,1,0:T(4,128)S(1)} %get-tuple-element.3), channel_id=1, source_target_pairs={{0,496},{16,0},{32,16},{48,32},{64,48},{80,64},{96,80},{112,96},{1... | collective-permute-start | bytes 1572872 | tf_op jit(solution)/shard_map/ppermute | solution.py:17
  101.2 18.6 %collective-permute-start.2 = (f32[16,4]{0,1:T(4,128)S(1)}, f32[16,4]{0,1:T(4,128)S(1)}, u32[]{:S(2)}, u32[]{:S(2)}) collective-permute-start(f32[16,4]{0,1:T(4,128)S(1)} %multiply_subtract_fusion.2), channel_id=1, source_target_pairs={{0,496},{16,0},{32,16},{48,32},{64,48},{80,64},{96,80},{112,96},{1... | collective-permute-start | bytes 776 | tf_op jit(solution)/shard_map/ppermute | solution.py:17
  132.1 14.7 %all-to-all-start.1 = ((f32[16,4,2048]{2,1,0:T(4,128)}), f32[16,4,2048]{2,1,0:T(4,128)S(1)}, u32[]{:S(2)}, u32[]{:S(2)}) async-start(f32[16,4,2048]{2,1,0:T(4,128)} %collective-permute-done.1), calls=%async_computation.1 | async-start | bytes 1048576 | tf_op jit(solution)/shard_map/all_to_all | solution.py:101
where the time goes:
time: 149 us; the launch traced here: 148 us
  waiting for transfers between devices  44.8 us (30%)
  matrix products  34.6 us (23%)
  starting transfers between devices  25.8 us (17%)
  local copies, waits for them, and re-layouts  20.7 us (14%)
  blocking collectives  12.2 us (8%)
  other arithmetic  8.83 us (6%)
    ppermute x3, waiting for transfers between devices, shifted(): return lax.ppermute(value, axis, pairs)  21.3 us
    dot_general x5, matrix products, apply_fwd(): mixed = jnp.einsum('rnkb,nkcb->rnc', taken, block_values, precision=highest)  15.5 us
    all_to_all x1, waiting for transfers between devices, on_device(): lax.all_to_all(packed, 'markov', split_axis=0, concat_axis=0, tiled=True)  14.4 us
    ppermute x3, starting transfers between devices, shifted(): return lax.ppermute(value, axis, pairs)  12.6 us
    all_to_all x1, blocking collectives, on_device(): lax.all_to_all(icpts, 'markov', split_axis=0, concat_axis=0, tiled=True)  12.2 us
    all_to_all x1, starting transfers between devices, on_device(): lax.all_to_all(packed, 'markov', split_axis=0, concat_axis=0, tiled=True)  9.6 us
    all_to_all x1, waiting for transfers between devices, on_device(): lax.all_to_all(slopes, 'markov', split_axis=0, concat_axis=0, tiled=True)  9.18 us
    reshape x4, local copies, waits for them, and re-layouts, apply_fwd(): return field + mixed.reshape(count, width)  6.99 us
  transfers between devices with their start and end apart: 5, of which 4 were waited for; matrix products, arithmetic and copies ran while one was open for 8% of the time, Pallas kernels for 0%

commit v1 on v0

v1 whole, which is shorter than its diff:
```python
import functools

import jax
import jax.numpy as jnp
from jax import lax
from jax.experimental import pallas as pl
from jax.experimental.pallas import tpu as pltpu
from jax.sharding import PartitionSpec as P

ITERS = 4
BS = 128

highest = lax.Precision.HIGHEST
dual_step = 0.5
primal_step = 0.5


def shifted(value, axis, steps):
    count = lax.axis_size(axis)
    pairs = [(source, (source + steps) % count) for source in range(count)]
    return lax.ppermute(value, axis, pairs)


def mat_nt(a, b):
    return lax.dot_general(a, b, (((1,), (1,)), ((), ())), precision=highest,
                           preferred_element_type=jnp.float32)


def mat_nn(a, b):
    return lax.dot_general(a, b, (((1,), (0,)), ((), ())), precision=highest,
                           preferred_element_type=jnp.float32)


def solve_kernel(nblk, kblk, cols_ref, rows_ref, xi_ref, c_ref, q_ref, g_ref, h_ref, bv_ref,
                 out_ref, base_s, p_s, u_s, v_s, acc_s):
    width = nblk * BS

    def lanes(n):
        return slice(n * BS, (n + 1) * BS)

    def col(n, k):
        return cols_ref[n * kblk + k]

    def apply_fwd(field_s, n):
        total = field_s[n]
        for k in range(kblk):
            total = total + mat_nt(field_s[col(n, k)], bv_ref[n, k])
        return total

    for n in range(nblk):
        s = lanes(n)
        base_s[n] = rows_ref[:, s] + xi_ref[:, s] - g_ref[:, s]
        u_s[n] = jnp.zeros(u_s.shape[1:], jnp.float32)

    for sweep in range(ITERS):
        for n in range(nblk):
            s = lanes(n)
            q = q_ref[:, s]
            shrink = q / (q + dual_step)
            if sweep == 0:
                p_s[n] = (dual_step * base_s[n]) * shrink
            else:
                p_s[n] = (p_s[n] + dual_step * (base_s[n] - apply_fwd(v_s, n))) * shrink
        for n in range(nblk):
            acc_s[n] = jnp.zeros(acc_s.shape[1:], jnp.float32)
        for n in range(nblk):
            pn = p_s[n]
            for k in range(kblk):
                c = col(n, k)
                acc_s[c] = acc_s[c] + mat_nn(pn, bv_ref[n, k])
        for n in range(nblk):
            s = lanes(n)
            u_old = u_s[n]
            fresh = jnp.clip(u_old + primal_step * (p_s[n] + acc_s[n] - c_ref[:, s]), 0.0, h_ref[:, s])
            v_s[n] = 2.0 * fresh - u_old
            u_s[n] = fresh

    value = jnp.zeros((rows_ref.shape[0], 1), jnp.float32)
    cross = jnp.zeros((rows_ref.shape[0], 1), jnp.float32)
    for n in range(nblk):
        s = lanes(n)
        rows = rows_ref[:, s]
        un = u_s[n]
        gap = rows + xi_ref[:, s] - apply_fwd(u_s, n) - g_ref[:, s]
        term = c_ref[:, s] * un + 0.5 * q_ref[:, s] * gap * gap
        value = value + jnp.sum(term, axis=1, keepdims=True)
        pn = p_s[n]
        cross = cross + jnp.sum(pn * rows, axis=1, keepdims=True)
        out_ref[:, s] = pn
    icpt = (value - cross) / width
    out_ref[:, width:] = jnp.broadcast_to(icpt, (rows_ref.shape[0], BS))


def solve_block(rows, inflow, unit_cost, curvature, target, release_cap, block_values, block_cols):
    count, width = rows.shape
    nblk, kblk = block_values.shape[0], block_values.shape[1]
    vec = lambda a: a.reshape(1, width)
    vspec = pl.BlockSpec(memory_space=pltpu.VMEM)
    field = pltpu.VMEM((nblk, count, BS), jnp.float32)
    flops = 2 * count * nblk * kblk * BS * BS * (2 * ITERS + 1) * 6
    return pl.pallas_call(
        functools.partial(solve_kernel, nblk, kblk),
        out_shape=jax.ShapeDtypeStruct((count, width + BS), jnp.float32),
        in_specs=[pl.BlockSpec(memory_space=pltpu.SMEM)] + [vspec] * 7,
        out_specs=vspec,
        scratch_shapes=[field] * 5,
        compiler_params=pltpu.CompilerParams(vmem_limit_bytes=48 * 1024 * 1024),
        cost_estimate=pl.CostEstimate(flops=flops, transcendentals=0,
                                      bytes_accessed=4 * (block_values.size + 3 * rows.size)),
        name="sddp_solve",
    )(block_cols.reshape(-1), rows, vec(inflow), vec(unit_cost), vec(curvature), vec(target),
      vec(release_cap), block_values)


def on_device(trial_states, successor, inflow, unit_cost, curvature, target, release_cap,
              block_values, block_cols):
    states = lax.axis_size("markov")
    tr_rows = trial_states.shape[2]
    width = trial_states.shape[3]
    capacity = 2 * tr_rows // states
    slots = states * capacity
    own_rows = trial_states.reshape(tr_rows, width)
    own_dest = successor.reshape(tr_rows)
    rows, dest = shifted((own_rows, own_dest), "week", 1)
    marked = (dest[:, None] == jnp.arange(states, dtype=jnp.int32)[None, :]).astype(jnp.int32)
    ranked = jnp.sum(jnp.cumsum(marked, axis=0) * marked, axis=1) - 1
    slot_ids = dest * capacity + ranked
    hit = slot_ids[None, :] == jnp.arange(slots, dtype=jnp.int32)[:, None]
    source = jnp.sum(jnp.where(hit, jnp.arange(tr_rows, dtype=jnp.int32)[None, :], 0), axis=1)
    filled = jnp.any(hit, axis=1)
    packed = jnp.where(filled[:, None], jnp.take(rows, source, axis=0), 0.0)
    arrived = lax.all_to_all(packed.reshape(states, capacity, width), "markov", 0, 0, tiled=True)
    solved = solve_block(arrived.reshape(slots, width), inflow.reshape(width),
                         unit_cost.reshape(width), curvature.reshape(width), target.reshape(width),
                         release_cap.reshape(width), block_values[0, 0], block_cols[0, 0])
    back = lax.all_to_all(solved.reshape(states, capacity, -1), "markov", 0, 0, tiled=True)
    mine = jnp.take(back.reshape(slots, -1), slot_ids, axis=0)
    mine = shifted(mine, "week", -1)
    return (mine[:, :width].reshape(1, 1, tr_rows, width),
            mine[:, width].reshape(1, 1, tr_rows))


def solution(mesh):
    return jax.shard_map(
        on_device,
        mesh=mesh,
        in_specs=(
            P("week", "markov", None, None),
            P("week", "markov", None, None),
            P("week", "markov", None),
            P("week", "markov", None),
            P("week", "markov", None),
            P("week", "markov", None),
            P("week", "markov", None),
            P("week", "markov", None, None, None, None),
            P("week", "markov", None, None),
        ),
        out_specs=(P("week", "markov", None, None), P("week", "markov", None)),
        check_vma=False,
    )
```

time: 149 us -> 106 us (0.71)
  matrix products: 34.6 us -> 0 us
  Pallas kernels: 0 us -> 25.3 us
  local copies, waits for them, and re-layouts: 20.7 us -> 4.64 us
  blocking collectives: 12.2 us -> 0 us
  other arithmetic: 8.83 us -> 1.64 us
  waiting for transfers between devices: 44.8 us -> 47.5 us
    dot_general x21 -> x0, matrix products: 34.6 us -> none  [the longest x5 15.5 us: apply_fwd(): mixed = jnp.einsum('rnkb,nkcb->rnc', taken, block_values, precision=highest)]
    pallas_call x0 -> x1, Pallas kernels: none -> 25.3 us  [solve_block(): pl.pallas_call(functools.partial(solve_kernel, nblk, kblk), out_shape=jax...]
    all_to_all x1 -> x0, blocking collectives: 12.2 us -> none  [on_device(): lax.all_to_all(icpts, 'markov', split_axis=0, concat_axis=0, tiled=True)]
    reshape x10 -> x4, local copies, waits for them, and re-layouts: 11.5 us -> 2.05 us  [the longest x1 0.96 us: on_device(): solved.reshape(states, capacity, -1)]
    all_to_all x2, waiting for transfers between devices: 23.5 us -> 32.5 us  [the longest x1 17.4 us: on_device(): lax.all_to_all(solved.reshape(states, capacity, -1), 'markov', 0, 0, tile...]
    ppermute x3, waiting for transfers between devices: 21.3 us -> 15 us  [shifted(): return lax.ppermute(value, axis, pairs)]
    transpose x4 -> x0, local copies, waits for them, and re-layouts: 5.81 us -> none  [apply_fwd(): mixed = jnp.einsum('rnkb,nkcb->rnc', taken, block_values, precision=highest)]
    reduce_sum x2, other arithmetic: 4.73 us -> 0.27 us  [the longest x1 0.18 us: on_device(): ranked = jnp.sum(jnp.cumsum(marked, axis=0) * marked, axis=1) - 1]
  transfers between devices with their start and end apart: 5 -> 5, of which waited for: 4 -> 4; matrix products, arithmetic and copies ran while one was open for 8% -> 1% of each run, Pallas kernels for 0% -> 0%
where the time goes in v1:
time: 106 us; the launch traced here: 105 us
  waiting for transfers between devices  47.5 us (45%)
  Pallas kernels  25.3 us (24%)
  starting transfers between devices  25.2 us (24%)
  local copies, waits for them, and re-layouts  4.64 us (4%)
  other arithmetic  1.64 us (2%)
    pallas_call x1, Pallas kernels, solve_block(): pl.pallas_call(functools.partial(solve_kernel, nblk, kblk), out_shape=jax...  25.3 us
    all_to_all x1, waiting for transfers between devices, on_device(): lax.all_to_all(solved.reshape(states, capacity, -1), 'markov', 0, 0, tile...  17.4 us
    all_to_all x1, waiting for transfers between devices, on_device(): lax.all_to_all(packed.reshape(states, capacity, width), 'markov', 0, 0, t...  15.2 us
    ppermute x3, waiting for transfers between devices, shifted(): return lax.ppermute(value, axis, pairs)  15 us
    ppermute x3, starting transfers between devices, shifted(): return lax.ppermute(value, axis, pairs)  15 us
    all_to_all x1, starting transfers between devices, on_device(): lax.all_to_all(packed.reshape(states, capacity, width), 'markov', 0, 0, t...  6.65 us
    all_to_all x1, starting transfers between devices, on_device(): lax.all_to_all(solved.reshape(states, capacity, -1), 'markov', 0, 0, tile...  3.58 us
  transfers between devices with their start and end apart: 5, of which 4 were waited for; matrix products, arithmetic and copies ran while one was open for 1% of the time, Pallas kernels for 0%

profile of v1, /device:TPU:57, one launch (start us, length us, event | category | flops | bytes accessed | tf_op | source)
XLA Modules:
  0.0 105.2 jit_solution(6704064571077032837)
XLA Ops:
  0.6 10.4 %collective-permute-start = (s32[32]{0:T(128)}, s32[32]{0:T(128)S(1)}, u32[]{:S(2)}, u32[]{:S(2)}) collective-permute-start(s32[32]{0:T(128)} %bitcast.25), channel_id=1, source_target_pairs={{0,16},{16,32},{32,48},{48,64},{64,80},{80,96},{96,112},{112,128},... | collective-permute-start | bytes 392 | tf_op jit(solution)/shard_map/ppermute | solution.py:21
  11.0 1.9 %collective-permute-start.1 = (f32[32,2048]{1,0:T(8,128)}, f32[32,2048]{1,0:T(8,128)S(1)}, u32[]{:S(2)}, u32[]{:S(2)}) collective-permute-start(f32[32,2048]{1,0:T(8,128)} %bitcast.24), channel_id=1, source_target_pairs={{0,16},{16,32},{32,48},{48,64},{64,80},{80,96},{96,112},{112,128},... | collective-permute-start | bytes 786440 | tf_op jit(solution)/shard_map/ppermute | solution.py:21
  13.0 0.0 collective-permute-done
  13.0 0.1 fusion.1
  13.0 0.1 reduce_window_sum.11
  13.1 0.2 select_reduce_fusion.1
  13.3 0.1 select_reduce_fusion
  13.4 0.1 fusion
  13.5 0.1 reduce_sum.24
  13.6 0.1 broadcast_in_dim.55
  13.7 3.5 %collective-permute-done.1 = f32[32,2048]{1,0:T(8,128)S(1)} collective-permute-done((f32[32,2048]{1,0:T(8,128)}, f32[32,2048]{1,0:T(8,128)S(1)}, u32[]{:S(2)}, u32[]{:S(2)}) %collective-permute-start.1) | collective-permute-done | bytes 262176 | tf_op jit(solution)/shard_map/ppermute | solution.py:21
  17.2 0.8 gather_fusion
  17.9 0.0 copy-start.6
  17.9 0.0 copy-start
  17.9 0.0 copy-start.1
  18.0 0.0 copy-start.2
  18.0 0.0 copy-start.3
  18.0 0.0 copy-start.4
  18.0 0.0 copy-start.5
  18.0 0.1 gather.11
  18.2 1.0 select_select_fusion
  19.2 6.7 %all-to-all-start = ((f32[16,4,2048]{2,1,0:T(4,128)}), f32[16,4,2048]{2,1,0:T(4,128)S(1)}, u32[]{:S(2)}, u32[]{:S(2)}) async-start(f32[16,4,2048]{2,1,0:T(4,128)} %select_select_fusion), calls=%async_computation | async-start | bytes 1048576 | tf_op jit(solution)/shard_map/all_to_all | solution.py:132
  25.8 0.0 copy-done.6
  25.9 0.1 copy.13
  25.9 0.1 reshape_squeeze.6.cols_ref
  26.0 15.2 %all-to-all-done = f32[16,4,2048]{2,1,0:T(4,128)S(1)} async-done(((f32[16,4,2048]{2,1,0:T(4,128)}), f32[16,4,2048]{2,1,0:T(4,128)S(1)}, u32[]{:S(2)}, u32[]{:S(2)}) %all-to-all-start) | async-done | bytes 524320 | tf_op jit(solution)/shard_map/all_to_all | solution.py:132
  41.2 0.2 reshape.62.rows_ref
  41.4 0.0 copy-done
  41.4 0.0 copy-done.1
  41.4 0.0 copy-done.2
  41.4 0.0 copy-done.3
  41.4 0.0 copy-done.4
  41.4 0.0 copy-done.5
  41.5 25.3 %sddp_solve.1 = f32[64,2176]{1,0:T(8,128)S(1)} custom-call(s32[32]{0:T(128)S(1)} %reshape_squeeze.6.cols_ref, f32[64,2048]{1,0:T(8,128)S(1)} %reshape.62.rows_ref, f32[1,2048]{1,0:T(1,128)S(1)} %bitcast.18, f32[1,2048]{1,0:T(1,128)S(1)} %bitcast.19, f32[1,2048]{1,0:T(1,128)S(1)} %bitcast.20, f32[1,2048]{1,0:T(1,128)S(1)} %bitcast.21, ...), custom_call_target="tpu_custom_call" | custom-call | flops 3623878656 | bytes 3670016 | tf_op jit(solution)/shard_map/sddp_solve/pallas_call | solution.py:101
  66.7 1.0 reshape.63
  67.7 3.6 %all-to-all-start.1 = ((f32[16,4,2176]{2,1,0:T(4,128)}), f32[16,4,2176]{2,1,0:T(4,128)S(1)}, u32[]{:S(2)}, u32[]{:S(2)}) async-start(f32[16,4,2176]{2,1,0:T(4,128)} %reshape.63), calls=%async_computation.1 | async-start | bytes 1114112 | tf_op jit(solution)/shard_map/all_to_all | solution.py:136
  71.3 17.4 %all-to-all-done.1 = f32[16,4,2176]{2,1,0:T(4,128)S(1)} async-done(((f32[16,4,2176]{2,1,0:T(4,128)}), f32[16,4,2176]{2,1,0:T(4,128)S(1)}, u32[]{:S(2)}, u32[]{:S(2)}) %all-to-all-start.1) | async-done | bytes 557088 | tf_op jit(solution)/shard_map/all_to_all | solution.py:136
  88.7 0.2 reshape.64
  88.9 0.7 gather_fusion.1
  89.5 0.1 broadcast_select_fusion
  89.6 2.6 %collective-permute-start.2 = (f32[32,2176]{1,0:T(8,128)S(1)}, f32[32,2176]{1,0:T(8,128)S(1)}, u32[]{:S(2)}, u32[]{:S(2)}) collective-permute-start(f32[32,2176]{1,0:T(8,128)S(1)} %broadcast_select_fusion), channel_id=1, source_target_pairs={{0,496},{16,0},{32,16},{48,32},{64,48},{80,64},{96,80},{112,96},{1... | collective-permute-start | bytes 835592 | tf_op jit(solution)/shard_map/ppermute | solution.py:21
  92.3 11.5 %collective-permute-done.2 = f32[32,2176]{1,0:T(8,128)S(1)} collective-permute-done((f32[32,2176]{1,0:T(8,128)S(1)}, f32[32,2176]{1,0:T(8,128)S(1)}, u32[]{:S(2)}, u32[]{:S(2)}) %collective-permute-start.2) | collective-permute-done | bytes 278560 | tf_op jit(solution)/shard_map/ppermute | solution.py:21
  103.8 0.7 slice_bitcast_fusion
  104.5 0.6 slice_reduce_fusion
  (6 shorter events, 0.0 us)
Async XLA Ops:
  0.6 12.3 %collective-permute-start = (s32[32]{0:T(128)}, s32[32]{0:T(128)S(1)}, u32[]{:S(2)}, u32[]{:S(2)}) collective-permute-start(s32[32]{0:T(128)} %bitcast.25), channel_id=1, source_target_pairs={{0,16},{16,32},{32,48},{48,64},{64,80},{80,96},{96,112},{112,128},... | collective-permute-start | bytes 392 | tf_op jit(solution)/shard_map/ppermute | solution.py:21
  11.0 6.1 %collective-permute-start.1 = (f32[32,2048]{1,0:T(8,128)}, f32[32,2048]{1,0:T(8,128)S(1)}, u32[]{:S(2)}, u32[]{:S(2)}) collective-permute-start(f32[32,2048]{1,0:T(8,128)} %bitcast.24), channel_id=1, source_target_pairs={{0,16},{16,32},{32,48},{48,64},{64,80},{80,96},{96,112},{112,128},... | collective-permute-start | bytes 786440 | tf_op jit(solution)/shard_map/ppermute | solution.py:21
  17.9 7.9 %copy-start.6 = (s32[1,1,16,2]{2,3,1,0:T(2,128)S(1)}, s32[1,1,16,2]{2,3,1,0:T(2,128)}, u32[]{:S(2)}) copy-start(s32[1,1,16,2]{2,3,1,0:T(2,128)} %param.17) | copy-start | bytes 388
  17.9 23.5 %copy-start = (f32[1,1,16,2,128,128]{5,4,3,2,1,0:T(8,128)S(1)}, f32[1,1,16,2,128,128]{5,4,3,2,1,0:T(8,128)}, u32[]{:S(2)}) copy-start(f32[1,1,16,2,128,128]{5,4,3,2,1,0:T(8,128)} %param.16) | copy-start | bytes 6291460
  17.9 23.5 %copy-start.1 = (f32[1,1,2048]{2,1,0:T(1,128)S(1)}, f32[1,1,2048]{2,1,0:T(1,128)}, u32[]{:S(2)}) copy-start(f32[1,1,2048]{2,1,0:T(1,128)} %param.11) | copy-start | bytes 24580
  18.0 23.5 %copy-start.2 = (f32[1,1,2048]{2,1,0:T(1,128)S(1)}, f32[1,1,2048]{2,1,0:T(1,128)}, u32[]{:S(2)}) copy-start(f32[1,1,2048]{2,1,0:T(1,128)} %param.12) | copy-start | bytes 24580
  18.0 23.5 %copy-start.3 = (f32[1,1,2048]{2,1,0:T(1,128)S(1)}, f32[1,1,2048]{2,1,0:T(1,128)}, u32[]{:S(2)}) copy-start(f32[1,1,2048]{2,1,0:T(1,128)} %param.13) | copy-start | bytes 24580
  18.0 23.5 %copy-start.4 = (f32[1,1,2048]{2,1,0:T(1,128)S(1)}, f32[1,1,2048]{2,1,0:T(1,128)}, u32[]{:S(2)}) copy-start(f32[1,1,2048]{2,1,0:T(1,128)} %param.14) | copy-start | bytes 24580
  18.0 23.5 %copy-start.5 = (f32[1,1,2048]{2,1,0:T(1,128)S(1)}, f32[1,1,2048]{2,1,0:T(1,128)}, u32[]{:S(2)}) copy-start(f32[1,1,2048]{2,1,0:T(1,128)} %param.15) | copy-start | bytes 24580
  19.2 22.0 %all-to-all-start = ((f32[16,4,2048]{2,1,0:T(4,128)}), f32[16,4,2048]{2,1,0:T(4,128)S(1)}, u32[]{:S(2)}, u32[]{:S(2)}) async-start(f32[16,4,2048]{2,1,0:T(4,128)} %select_select_fusion), calls=%async_computation | async-start | bytes 1048576 | tf_op jit(solution)/shard_map/all_to_all | solution.py:132
  67.7 21.0 %all-to-all-start.1 = ((f32[16,4,2176]{2,1,0:T(4,128)}), f32[16,4,2176]{2,1,0:T(4,128)S(1)}, u32[]{:S(2)}, u32[]{:S(2)}) async-start(f32[16,4,2176]{2,1,0:T(4,128)} %reshape.63), calls=%async_computation.1 | async-start | bytes 1114112 | tf_op jit(solution)/shard_map/all_to_all | solution.py:136
  89.6 14.2 %collective-permute-start.2 = (f32[32,2176]{1,0:T(8,128)S(1)}, f32[32,2176]{1,0:T(8,128)S(1)}, u32[]{:S(2)}, u32[]{:S(2)}) collective-permute-start(f32[32,2176]{1,0:T(8,128)S(1)} %broadcast_select_fusion), channel_id=1, source_target_pairs={{0,496},{16,0},{32,16},{48,32},{64,48},{80,64},{96,80},{112,96},{1... | collective-permute-start | bytes 835592 | tf_op jit(solution)/shard_map/ppermute | solution.py:21

commit v2 on v1

--- a/solution.py
+++ b/solution.py
@@ -10,7 +10,6 @@
 ITERS = 4
 BS = 128
 
-highest = lax.Precision.HIGHEST
 dual_step = 0.5
 primal_step = 0.5
 
@@ -21,19 +20,24 @@
     return lax.ppermute(value, axis, pairs)
 
 
-def mat_nt(a, b):
-    return lax.dot_general(a, b, (((1,), (1,)), ((), ())), precision=highest,
-                           preferred_element_type=jnp.float32)
+def dotb(a, b):
+    return lax.dot_general(a, b, (((1,), (0,)), ((), ())), preferred_element_type=jnp.float32)
 
 
-def mat_nn(a, b):
-    return lax.dot_general(a, b, (((1,), (0,)), ((), ())), precision=highest,
-                           preferred_element_type=jnp.float32)
+def split(x):
+    hi = x.astype(jnp.bfloat16)
+    return hi, (x - hi.astype(jnp.float32)).astype(jnp.bfloat16)
+
+
+def mm(x, wh, wl):
+    xh, xl = split(x)
+    return dotb(xh, wh) + dotb(xl, wh) + dotb(xh, wl)
 
 
 def solve_kernel(nblk, kblk, cols_ref, rows_ref, xi_ref, c_ref, q_ref, g_ref, h_ref, bv_ref,
-                 out_ref, base_s, p_s, u_s, v_s, acc_s):
+                 out_ref, base_s, p_s, u_s, v_s, acc_s, fh, fl, ah, al):
     width = nblk * BS
+    rows_n = rows_ref.shape[0]
 
     def lanes(n):
         return slice(n * BS, (n + 1) * BS)
@@ -41,11 +45,17 @@
     def col(n, k):
         return cols_ref[n * kblk + k]
 
-    def apply_fwd(field_s, n):
-        total = field_s[n]
-        for k in range(kblk):
-            total = total + mat_nt(field_s[col(n, k)], bv_ref[n, k])
-        return total
+    for n in range(nblk):
+        hi, lo = split(jnp.concatenate([bv_ref[n, k].T for k in range(kblk)], axis=0))
+        fh[n] = hi
+        fl[n] = lo
+        hi, lo = split(jnp.concatenate([bv_ref[n, k] for k in range(kblk)], axis=1))
+        ah[n] = hi
+        al[n] = lo
+
+    def mixed_fwd(field_s, n):
+        x = jnp.concatenate([field_s[col(n, k)] for k in range(kblk)], axis=1)
+        return mm(x, fh[n], fl[n])
 
     for n in range(nblk):
         s = lanes(n)
@@ -60,14 +70,15 @@
             if sweep == 0:
                 p_s[n] = (dual_step * base_s[n]) * shrink
             else:
-                p_s[n] = (p_s[n] + dual_step * (base_s[n] - apply_fwd(v_s, n))) * shrink
+                av = v_s[n] + mixed_fwd(v_s, n)
+                p_s[n] = (p_s[n] + dual_step * (base_s[n] - av)) * shrink
         for n in range(nblk):
             acc_s[n] = jnp.zeros(acc_s.shape[1:], jnp.float32)
         for n in range(nblk):
-            pn = p_s[n]
+            r = mm(p_s[n], ah[n], al[n])
             for k in range(kblk):
                 c = col(n, k)
-                acc_s[c] = acc_s[c] + mat_nn(pn, bv_ref[n, k])
+                acc_s[c] = acc_s[c] + r[:, k * BS:(k + 1) * BS]
         for n in range(nblk):
             s = lanes(n)
             u_old = u_s[n]
@@ -75,20 +86,20 @@
             v_s[n] = 2.0 * fresh - u_old
             u_s[n] = fresh
 
-    value = jnp.zeros((rows_ref.shape[0], 1), jnp.float32)
-    cross = jnp.zeros((rows_ref.shape[0], 1), jnp.float32)
+    value = jnp.zeros((rows_n, 1), jnp.float32)
+    cross = jnp.zeros((rows_n, 1), jnp.float32)
     for n in range(nblk):
         s = lanes(n)
         rows = rows_ref[:, s]
         un = u_s[n]
-        gap = rows + xi_ref[:, s] - apply_fwd(u_s, n) - g_ref[:, s]
+        gap = rows + xi_ref[:, s] - (un + mixed_fwd(u_s, n)) - g_ref[:, s]
         term = c_ref[:, s] * un + 0.5 * q_ref[:, s] * gap * gap
         value = value + jnp.sum(term, axis=1, keepdims=True)
         pn = p_s[n]
         cross = cross + jnp.sum(pn * rows, axis=1, keepdims=True)
         out_ref[:, s] = pn
     icpt = (value - cross) / width
-    out_ref[:, width:] = jnp.broadcast_to(icpt, (rows_ref.shape[0], BS))
+    out_ref[:, width:] = jnp.broadcast_to(icpt, (rows_n, BS))
 
 
 def solve_block(rows, inflow, unit_cost, curvature, target, release_cap, block_values, block_cols):
@@ -97,13 +108,16 @@
     vec = lambda a: a.reshape(1, width)
     vspec = pl.BlockSpec(memory_space=pltpu.VMEM)
     field = pltpu.VMEM((nblk, count, BS), jnp.float32)
-    flops = 2 * count * nblk * kblk * BS * BS * (2 * ITERS + 1) * 6
+    scratch = [field] * 5
+    scratch += [pltpu.VMEM((nblk, kblk * BS, BS), jnp.bfloat16)] * 2
+    scratch += [pltpu.VMEM((nblk, BS, kblk * BS), jnp.bfloat16)] * 2
+    flops = 2 * count * nblk * kblk * BS * BS * (2 * ITERS) * 3
     return pl.pallas_call(
         functools.partial(solve_kernel, nblk, kblk),
         out_shape=jax.ShapeDtypeStruct((count, width + BS), jnp.float32),
         in_specs=[pl.BlockSpec(memory_space=pltpu.SMEM)] + [vspec] * 7,
         out_specs=vspec,
-        scratch_shapes=[field] * 5,
+        scratch_shapes=scratch,
         compiler_params=pltpu.CompilerParams(vmem_limit_bytes=48 * 1024 * 1024),
         cost_estimate=pl.CostEstimate(flops=flops, transcendentals=0,
                                       bytes_accessed=4 * (block_values.size + 3 * rows.size)),
@@ -121,7 +135,9 @@
     slots = states * capacity
     own_rows = trial_states.reshape(tr_rows, width)
     own_dest = successor.reshape(tr_rows)
-    rows, dest = shifted((own_rows, own_dest), "week", 1)
+    tag = jnp.broadcast_to(own_dest.astype(jnp.float32)[:, None], (tr_rows, BS))
+    sent = shifted(jnp.concatenate([own_rows, tag], axis=1), "week", 1)
+    rows, dest = sent[:, :width], sent[:, width].astype(jnp.int32)
     marked = (dest[:, None] == jnp.arange(states, dtype=jnp.int32)[None, :]).astype(jnp.int32)
     ranked = jnp.sum(jnp.cumsum(marked, axis=0) * marked, axis=1) - 1
     slot_ids = dest * capacity + ranked

time: 106 us -> 86 us (0.81)
  Pallas kernels: 25.3 us -> 5.83 us
  starting transfers between devices: 25.2 us -> 22.9 us
  other arithmetic: 1.64 us -> 3.63 us
    pallas_call x1, Pallas kernels: 25.3 us -> 5.83 us  [solve_block(): pl.pallas_call(functools.partial(solve_kernel, nblk, kblk), out_shape=jax...]
    ppermute x3 -> x2, starting transfers between devices: 15 us -> 12.8 us  [shifted(): return lax.ppermute(value, axis, pairs)]
    ppermute x3 -> x2, waiting for transfers between devices: 15 us -> 15.8 us  [shifted(): return lax.ppermute(value, axis, pairs)]
  transfers between devices with their start and end apart: 5 -> 4, of which waited for: 4 -> 4; matrix products, arithmetic and copies ran while one was open for 1% -> 0% of each run, Pallas kernels for 0% -> 0%
where the time goes in v2:
time: 86 us; the launch traced here: 85.6 us
  waiting for transfers between devices  47.5 us (55%)
  starting transfers between devices  22.9 us (27%)
  Pallas kernels  5.83 us (7%)
  local copies, waits for them, and re-layouts  4.81 us (6%)
  other arithmetic  3.63 us (4%)
  between operations  0.88 us (1%)
    all_to_all x1, waiting for transfers between devices, on_device(): lax.all_to_all(solved.reshape(states, capacity, -1), 'markov', 0, 0, tile...  17.5 us
    ppermute x2, waiting for transfers between devices, shifted(): return lax.ppermute(value, axis, pairs)  15.8 us
    all_to_all x1, waiting for transfers between devices, on_device(): lax.all_to_all(packed.reshape(states, capacity, width), 'markov', 0, 0, t...  14.2 us
    ppermute x2, starting transfers between devices, shifted(): return lax.ppermute(value, axis, pairs)  12.8 us
    all_to_all x1, starting transfers between devices, on_device(): lax.all_to_all(packed.reshape(states, capacity, width), 'markov', 0, 0, t...  6.57 us
    pallas_call x1, Pallas kernels, solve_block(): pl.pallas_call(functools.partial(solve_kernel, nblk, kblk), out_shape=jax...  5.83 us
    all_to_all x1, starting transfers between devices, on_device(): lax.all_to_all(solved.reshape(states, capacity, -1), 'markov', 0, 0, tile...  3.58 us
  transfers between devices with their start and end apart: 4, of which 4 were waited for; matrix products, arithmetic and copies ran while one was open for 0% of the time, Pallas kernels for 0%

profile of v2, /device:TPU:57, one launch (start us, length us, event | category | flops | bytes accessed | tf_op | source)
XLA Modules:
  0.0 85.6 jit_solution(14401739859849724056)
XLA Ops:
  0.6 0.7 convert_bitcast_fusion
  1.3 0.1 broadcast_in_dim.58
  1.4 1.0 %pad_maximum_fusion = f32[32,2176]{1,0:T(8,128)S(1)} fusion(f32[32,128]{1,0:T(8,128)S(1)} %broadcast_in_dim.58, f32[32,2048]{1,0:T(8,128)} %bitcast.26), kind=kLoop, calls=%fused_computation.3 | loop fusion | flops 69632 | bytes 557056 | tf_op jit(solution)/shard_map/concatenate | solution.py:139
  2.3 10.4 %collective-permute-start = (f32[32,2176]{1,0:T(8,128)S(1)}, f32[32,2176]{1,0:T(8,128)S(1)}, u32[]{:S(2)}, u32[]{:S(2)}) collective-permute-start(f32[32,2176]{1,0:T(8,128)S(1)} %pad_maximum_fusion), channel_id=1, source_target_pairs={{0,16},{16,32},{32,48},{48,64},{64,80},{80,96},{96,112},{112,128},... | collective-permute-start | bytes 835592 | tf_op jit(solution)/shard_map/ppermute | solution.py:20
  12.7 4.2 %collective-permute-done = f32[32,2176]{1,0:T(8,128)S(1)} collective-permute-done((f32[32,2176]{1,0:T(8,128)S(1)}, f32[32,2176]{1,0:T(8,128)S(1)}, u32[]{:S(2)}, u32[]{:S(2)}) %collective-permute-start) | collective-permute-done | bytes 278560 | tf_op jit(solution)/shard_map/ppermute | solution.py:20
  17.0 0.1 fusion.2
  17.1 0.1 fusion.1
  17.2 0.1 reduce_window_sum.11
  17.2 0.2 select_reduce_fusion.1
  17.4 0.1 copy.15
  17.5 0.1 fusion.5
  17.6 0.1 select_reduce_fusion
  17.7 0.1 fusion
  17.8 0.1 reduce_sum.24
  17.9 0.1 broadcast_in_dim.60
  18.1 0.8 gather_fusion
  18.8 0.0 copy-start.6
  18.8 0.0 copy-start
  18.8 0.0 copy-start.1
  18.9 0.0 copy-start.2
  18.9 0.0 copy-start.3
  18.9 0.0 copy-start.4
  18.9 0.0 copy-start.5
  18.9 0.1 gather.11
  19.1 1.0 %select_select_fusion = f32[16,4,2048]{2,1,0:T(4,128)} fusion(f32[16,4,2048]{2,1,0:T(4,128)S(1)} %gather.11, pred[16,4]{1,0:T(8,128)(4,1)S(1)} %compare_and_fusion, pred[16,4]{1,0:T(8,128)(4,1)S(1)} %broadcast_in_dim.60), kind=kLoop, calls=%fused_computation.2 | loop fusion | flops 262144 | bytes 1048704 | tf_op jit(solution)/shard_map/jit(_where)/select_n | solution.py:147
  20.1 6.6 %all-to-all-start = ((f32[16,4,2048]{2,1,0:T(4,128)}), f32[16,4,2048]{2,1,0:T(4,128)S(1)}, u32[]{:S(2)}, u32[]{:S(2)}) async-start(f32[16,4,2048]{2,1,0:T(4,128)} %select_select_fusion), calls=%async_computation | async-start | bytes 1048576 | tf_op jit(solution)/shard_map/all_to_all | solution.py:148
  26.7 0.0 copy-done.6
  26.7 0.1 copy.16
  26.8 0.1 reshape_squeeze.6.cols_ref
  26.8 14.2 %all-to-all-done = f32[16,4,2048]{2,1,0:T(4,128)S(1)} async-done(((f32[16,4,2048]{2,1,0:T(4,128)}), f32[16,4,2048]{2,1,0:T(4,128)S(1)}, u32[]{:S(2)}, u32[]{:S(2)}) %all-to-all-start) | async-done | bytes 524320 | tf_op jit(solution)/shard_map/all_to_all | solution.py:148
  41.1 0.2 reshape.85.rows_ref
  41.2 0.0 copy-done
  41.3 0.0 copy-done.1
  41.3 0.0 copy-done.2
  41.3 0.0 copy-done.3
  41.3 0.0 copy-done.4
  41.3 5.8 %sddp_solve.1 = f32[64,2176]{1,0:T(8,128)S(1)} custom-call(s32[32]{0:T(128)S(1)} %reshape_squeeze.6.cols_ref, f32[64,2048]{1,0:T(8,128)S(1)} %reshape.85.rows_ref, f32[1,2048]{1,0:T(1,128)S(1)} %bitcast.21, f32[1,2048]{1,0:T(1,128)S(1)} %bitcast.22, f32[1,2048]{1,0:T(1,128)S(1)} %bitcast.23, f32[1,2048]{1,0:T(1,128)S(1)} %bitcast.24, ...), custom_call_target="tpu_custom_call" | custom-call | flops 1610612736 | bytes 3670016 | tf_op jit(solution)/shard_map/sddp_solve/pallas_call | solution.py:115
  47.1 0.9 %reshape.86 = f32[16,4,2176]{2,1,0:T(4,128)} reshape(f32[64,2176]{1,0:T(8,128)S(1)} %sddp_solve.1) | data formatting | bytes 1114112 | tf_op jit(solution)/shard_map/reshape | solution.py:152
  48.1 3.6 %all-to-all-start.1 = ((f32[16,4,2176]{2,1,0:T(4,128)}), f32[16,4,2176]{2,1,0:T(4,128)S(1)}, u32[]{:S(2)}, u32[]{:S(2)}) async-start(f32[16,4,2176]{2,1,0:T(4,128)} %reshape.86), calls=%async_computation.1 | async-start | bytes 1114112 | tf_op jit(solution)/shard_map/all_to_all | solution.py:152
  51.7 0.1 and_reduce_fusion
  51.8 17.5 %all-to-all-done.1 = f32[16,4,2176]{2,1,0:T(4,128)S(1)} async-done(((f32[16,4,2176]{2,1,0:T(4,128)}), f32[16,4,2176]{2,1,0:T(4,128)S(1)}, u32[]{:S(2)}, u32[]{:S(2)}) %all-to-all-start.1) | async-done | bytes 557088 | tf_op jit(solution)/shard_map/all_to_all | solution.py:152
  69.3 0.2 reshape.87
  69.5 0.7 gather_fusion.1
  70.2 0.1 broadcast_select_fusion
  70.3 2.4 %collective-permute-start.1 = (f32[32,2176]{1,0:T(8,128)S(1)}, f32[32,2176]{1,0:T(8,128)S(1)}, u32[]{:S(2)}, u32[]{:S(2)}) collective-permute-start(f32[32,2176]{1,0:T(8,128)S(1)} %broadcast_select_fusion), channel_id=1, source_target_pairs={{0,496},{16,0},{32,16},{48,32},{64,48},{80,64},{96,80},{112,96},{1... | collective-permute-start | bytes 835592 | tf_op jit(solution)/shard_map/ppermute | solution.py:20
  72.7 11.6 %collective-permute-done.1 = f32[32,2176]{1,0:T(8,128)S(1)} collective-permute-done((f32[32,2176]{1,0:T(8,128)S(1)}, f32[32,2176]{1,0:T(8,128)S(1)}, u32[]{:S(2)}, u32[]{:S(2)}) %collective-permute-start.1) | collective-permute-done | bytes 278560 | tf_op jit(solution)/shard_map/ppermute | solution.py:20
  84.2 0.6 slice_reduce_fusion
  84.9 0.7 slice_bitcast_fusion
  (8 shorter events, 0.1 us)
Async XLA Ops:
  2.3 14.6 %collective-permute-start = (f32[32,2176]{1,0:T(8,128)S(1)}, f32[32,2176]{1,0:T(8,128)S(1)}, u32[]{:S(2)}, u32[]{:S(2)}) collective-permute-start(f32[32,2176]{1,0:T(8,128)S(1)} %pad_maximum_fusion), channel_id=1, source_target_pairs={{0,16},{16,32},{32,48},{48,64},{64,80},{80,96},{96,112},{112,128},... | collective-permute-start | bytes 835592 | tf_op jit(solution)/shard_map/ppermute | solution.py:20
  18.8 7.8 %copy-start.6 = (s32[1,1,16,2]{2,3,1,0:T(2,128)S(1)}, s32[1,1,16,2]{2,3,1,0:T(2,128)}, u32[]{:S(2)}) copy-start(s32[1,1,16,2]{2,3,1,0:T(2,128)} %param.17) | copy-start | bytes 388
  18.8 22.4 %copy-start = (f32[1,1,16,2,128,128]{5,4,3,2,1,0:T(8,128)S(1)}, f32[1,1,16,2,128,128]{5,4,3,2,1,0:T(8,128)}, u32[]{:S(2)}) copy-start(f32[1,1,16,2,128,128]{5,4,3,2,1,0:T(8,128)} %param.16) | copy-start | bytes 6291460
  18.8 22.4 %copy-start.1 = (f32[1,1,2048]{2,1,0:T(1,128)S(1)}, f32[1,1,2048]{2,1,0:T(1,128)}, u32[]{:S(2)}) copy-start(f32[1,1,2048]{2,1,0:T(1,128)} %param.11) | copy-start | bytes 24580
  18.9 22.4 %copy-start.2 = (f32[1,1,2048]{2,1,0:T(1,128)S(1)}, f32[1,1,2048]{2,1,0:T(1,128)}, u32[]{:S(2)}) copy-start(f32[1,1,2048]{2,1,0:T(1,128)} %param.12) | copy-start | bytes 24580
  18.9 22.4 %copy-start.3 = (f32[1,1,2048]{2,1,0:T(1,128)S(1)}, f32[1,1,2048]{2,1,0:T(1,128)}, u32[]{:S(2)}) copy-start(f32[1,1,2048]{2,1,0:T(1,128)} %param.13) | copy-start | bytes 24580
  18.9 22.4 %copy-start.4 = (f32[1,1,2048]{2,1,0:T(1,128)S(1)}, f32[1,1,2048]{2,1,0:T(1,128)}, u32[]{:S(2)}) copy-start(f32[1,1,2048]{2,1,0:T(1,128)} %param.14) | copy-start | bytes 24580
  18.9 22.4 %copy-start.5 = (f32[1,1,2048]{2,1,0:T(1,128)S(1)}, f32[1,1,2048]{2,1,0:T(1,128)}, u32[]{:S(2)}) copy-start(f32[1,1,2048]{2,1,0:T(1,128)} %param.15) | copy-start | bytes 24580
  20.1 21.0 %all-to-all-start = ((f32[16,4,2048]{2,1,0:T(4,128)}), f32[16,4,2048]{2,1,0:T(4,128)S(1)}, u32[]{:S(2)}, u32[]{:S(2)}) async-start(f32[16,4,2048]{2,1,0:T(4,128)} %select_select_fusion), calls=%async_computation | async-start | bytes 1048576 | tf_op jit(solution)/shard_map/all_to_all | solution.py:148
  48.1 21.3 %all-to-all-start.1 = ((f32[16,4,2176]{2,1,0:T(4,128)}), f32[16,4,2176]{2,1,0:T(4,128)S(1)}, u32[]{:S(2)}, u32[]{:S(2)}) async-start(f32[16,4,2176]{2,1,0:T(4,128)} %reshape.86), calls=%async_computation.1 | async-start | bytes 1114112 | tf_op jit(solution)/shard_map/all_to_all | solution.py:152
  70.3 13.9 %collective-permute-start.1 = (f32[32,2176]{1,0:T(8,128)S(1)}, f32[32,2176]{1,0:T(8,128)S(1)}, u32[]{:S(2)}, u32[]{:S(2)}) collective-permute-start(f32[32,2176]{1,0:T(8,128)S(1)} %broadcast_select_fusion), channel_id=1, source_target_pairs={{0,496},{16,0},{32,16},{48,32},{64,48},{80,64},{96,80},{112,96},{1... | collective-permute-start | bytes 835592 | tf_op jit(solution)/shard_map/ppermute | solution.py:20

commit v3 on v2

--- a/solution.py
+++ b/solution.py
@@ -34,8 +34,34 @@
     return dotb(xh, wh) + dotb(xl, wh) + dotb(xh, wl)
 
 
-def solve_kernel(nblk, kblk, cols_ref, rows_ref, xi_ref, c_ref, q_ref, g_ref, h_ref, bv_ref,
-                 out_ref, base_s, p_s, u_s, v_s, acc_s, fh, fl, ah, al):
+def split_kernel(nblk, kblk, bv_ref, fh, fl, ah, al):
+    for n in range(nblk):
+        hi, lo = split(jnp.concatenate([bv_ref[n, k].T for k in range(kblk)], axis=0))
+        fh[n] = hi
+        fl[n] = lo
+        hi, lo = split(jnp.concatenate([bv_ref[n, k] for k in range(kblk)], axis=1))
+        ah[n] = hi
+        al[n] = lo
+
+
+def split_blocks(block_values):
+    nblk, kblk = block_values.shape[0], block_values.shape[1]
+    vspec = pl.BlockSpec(memory_space=pltpu.VMEM)
+    fwd = jax.ShapeDtypeStruct((nblk, kblk * BS, BS), jnp.bfloat16)
+    adj = jax.ShapeDtypeStruct((nblk, BS, kblk * BS), jnp.bfloat16)
+    return pl.pallas_call(
+        functools.partial(split_kernel, nblk, kblk),
+        out_shape=(fwd, fwd, adj, adj),
+        in_specs=[vspec],
+        out_specs=(vspec,) * 4,
+        cost_estimate=pl.CostEstimate(flops=4 * block_values.size, transcendentals=0,
+                                      bytes_accessed=8 * block_values.size),
+        name="sddp_split",
+    )(block_values)
+
+
+def solve_kernel(nblk, kblk, cols_ref, rows_ref, xi_ref, c_ref, q_ref, g_ref, h_ref,
+                 fh, fl, ah, al, out_ref, base_s, p_s, u_s, v_s, acc_s):
     width = nblk * BS
     rows_n = rows_ref.shape[0]
 
@@ -44,14 +70,6 @@
 
     def col(n, k):
         return cols_ref[n * kblk + k]
-
-    for n in range(nblk):
-        hi, lo = split(jnp.concatenate([bv_ref[n, k].T for k in range(kblk)], axis=0))
-        fh[n] = hi
-        fl[n] = lo
-        hi, lo = split(jnp.concatenate([bv_ref[n, k] for k in range(kblk)], axis=1))
-        ah[n] = hi
-        al[n] = lo
 
     def mixed_fwd(field_s, n):
         x = jnp.concatenate([field_s[col(n, k)] for k in range(kblk)], axis=1)
@@ -108,22 +126,19 @@
     vec = lambda a: a.reshape(1, width)
     vspec = pl.BlockSpec(memory_space=pltpu.VMEM)
     field = pltpu.VMEM((nblk, count, BS), jnp.float32)
-    scratch = [field] * 5
-    scratch += [pltpu.VMEM((nblk, kblk * BS, BS), jnp.bfloat16)] * 2
-    scratch += [pltpu.VMEM((nblk, BS, kblk * BS), jnp.bfloat16)] * 2
     flops = 2 * count * nblk * kblk * BS * BS * (2 * ITERS) * 3
     return pl.pallas_call(
         functools.partial(solve_kernel, nblk, kblk),
         out_shape=jax.ShapeDtypeStruct((count, width + BS), jnp.float32),
-        in_specs=[pl.BlockSpec(memory_space=pltpu.SMEM)] + [vspec] * 7,
+        in_specs=[pl.BlockSpec(memory_space=pltpu.SMEM)] + [vspec] * 10,
         out_specs=vspec,
-        scratch_shapes=scratch,
+        scratch_shapes=[field] * 5,
         compiler_params=pltpu.CompilerParams(vmem_limit_bytes=48 * 1024 * 1024),
         cost_estimate=pl.CostEstimate(flops=flops, transcendentals=0,
                                       bytes_accessed=4 * (block_values.size + 3 * rows.size)),
         name="sddp_solve",
     )(block_cols.reshape(-1), rows, vec(inflow), vec(unit_cost), vec(curvature), vec(target),
-      vec(release_cap), block_values)
+      vec(release_cap), *split_blocks(block_values))
 
 
 def on_device(trial_states, successor, inflow, unit_cost, curvature, target, release_cap,
@@ -143,14 +158,13 @@
     slot_ids = dest * capacity + ranked
     hit = slot_ids[None, :] == jnp.arange(slots, dtype=jnp.int32)[:, None]
     source = jnp.sum(jnp.where(hit, jnp.arange(tr_rows, dtype=jnp.int32)[None, :], 0), axis=1)
-    filled = jnp.any(hit, axis=1)
-    packed = jnp.where(filled[:, None], jnp.take(rows, source, axis=0), 0.0)
+    packed = jnp.take(rows, source, axis=0, mode="clip")
     arrived = lax.all_to_all(packed.reshape(states, capacity, width), "markov", 0, 0, tiled=True)
     solved = solve_block(arrived.reshape(slots, width), inflow.reshape(width),
                          unit_cost.reshape(width), curvature.reshape(width), target.reshape(width),
                          release_cap.reshape(width), block_values[0, 0], block_cols[0, 0])
     back = lax.all_to_all(solved.reshape(states, capacity, -1), "markov", 0, 0, tiled=True)
-    mine = jnp.take(back.reshape(slots, -1), slot_ids, axis=0)
+    mine = jnp.take(back.reshape(slots, -1), slot_ids, axis=0, mode="clip")
     mine = shifted(mine, "week", -1)
     return (mine[:, :width].reshape(1, 1, tr_rows, width),
             mine[:, width].reshape(1, 1, tr_rows))

time: 86 us -> 90.2 us (1.049)
  local copies, waits for them, and re-layouts: 4.81 us -> 10.3 us
  waiting for transfers between devices: 47.5 us -> 43.5 us
  Pallas kernels: 5.83 us -> 9.61 us
  other arithmetic: 3.63 us -> 2.29 us
    unnamed x15 -> x21, local copies, waits for them, and re-layouts: 0.13 us -> 5 us
    all_to_all x1, waiting for transfers between devices: 14.2 us -> 10.1 us  [on_device(): lax.all_to_all(packed.reshape(states, capacity, width), 'markov', 0, 0, t...]
    pallas_call x0 -> x1, Pallas kernels: none -> 4.15 us  [split_blocks(): pl.pallas_call(functools.partial(split_kernel, nblk, kblk), out_shape=(fw...]
    select_n x4 -> x0, other arithmetic: 1.25 us -> none  [the longest x2 1.03 us: on_device(): packed = jnp.where(filled[:, None], jnp.take(rows, source, axis=0), 0.0)]
    reshape x1 -> x2, local copies, waits for them, and re-layouts: 0.19 us -> 1.13 us  [the longest x1 0.94 us: on_device(): packed.reshape(states, capacity, width)]
  transfers between devices with their start and end apart: 4 -> 4, of which waited for: 4 -> 4; matrix products, arithmetic and copies ran while one was open for 0% -> 0% of each run, Pallas kernels for 0% -> 5%
where the time goes in v3:
time: 90.2 us; the launch traced here: 89.6 us
  waiting for transfers between devices  43.5 us (48%)
  starting transfers between devices  23.1 us (26%)
  local copies, waits for them, and re-layouts  10.3 us (11%)
  Pallas kernels  9.61 us (11%)
  other arithmetic  2.29 us (3%)
    all_to_all x1, waiting for transfers between devices, on_device(): lax.all_to_all(solved.reshape(states, capacity, -1), 'markov', 0, 0, tile...  17.6 us
    ppermute x2, waiting for transfers between devices, shifted(): return lax.ppermute(value, axis, pairs)  15.8 us
    ppermute x2, starting transfers between devices, shifted(): return lax.ppermute(value, axis, pairs)  12.8 us
    all_to_all x1, waiting for transfers between devices, on_device(): lax.all_to_all(packed.reshape(states, capacity, width), 'markov', 0, 0, t...  10.1 us
    all_to_all x1, starting transfers between devices, on_device(): lax.all_to_all(packed.reshape(states, capacity, width), 'markov', 0, 0, t...  6.71 us
    pallas_call x1, Pallas kernels, solve_block(): pl.pallas_call(functools.partial(solve_kernel, nblk, kblk), out_shape=jax...  5.46 us
    unnamed x21, local copies, waits for them, and re-layouts  5 us
    pallas_call x1, Pallas kernels, split_blocks(): pl.pallas_call(functools.partial(split_kernel, nblk, kblk), out_shape=(fw...  4.15 us
  transfers between devices with their start and end apart: 4, of which 4 were waited for; matrix products, arithmetic and copies ran while one was open for 0% of the time, Pallas kernels for 5%

profile of v3, /device:TPU:57, one launch (start us, length us, event | category | flops | bytes accessed | tf_op | source)
XLA Modules:
  0.0 89.6 jit_solution(1303835075493072646)
XLA Ops:
  0.6 0.7 convert_bitcast_fusion
  1.3 0.1 broadcast_in_dim.19
  1.4 1.0 %pad_maximum_fusion = f32[32,2176]{1,0:T(8,128)S(1)} fusion(f32[32,128]{1,0:T(8,128)S(1)} %broadcast_in_dim.19, f32[32,2048]{1,0:T(8,128)} %bitcast.22), kind=kLoop, calls=%fused_computation.2 | loop fusion | flops 69632 | bytes 557056 | tf_op jit(solution)/shard_map/concatenate | solution.py:154
  2.3 10.4 %collective-permute-start = (f32[32,2176]{1,0:T(8,128)S(1)}, f32[32,2176]{1,0:T(8,128)S(1)}, u32[]{:S(2)}, u32[]{:S(2)}) collective-permute-start(f32[32,2176]{1,0:T(8,128)S(1)} %pad_maximum_fusion), channel_id=1, source_target_pairs={{0,16},{16,32},{32,48},{48,64},{64,80},{80,96},{96,112},{112,128},... | collective-permute-start | bytes 835592 | tf_op jit(solution)/shard_map/ppermute | solution.py:20
  12.7 4.2 %collective-permute-done = f32[32,2176]{1,0:T(8,128)S(1)} collective-permute-done((f32[32,2176]{1,0:T(8,128)S(1)}, f32[32,2176]{1,0:T(8,128)S(1)}, u32[]{:S(2)}, u32[]{:S(2)}) %collective-permute-start) | collective-permute-done | bytes 278560 | tf_op jit(solution)/shard_map/ppermute | solution.py:20
  17.0 0.1 fusion.1
  17.1 0.1 fusion
  17.2 0.1 reduce_window_sum.11
  17.2 0.2 select_reduce_fusion.1
  17.4 0.1 copy.16
  17.5 0.1 add_reduce_fusion
  17.6 0.1 select_reduce_fusion
  17.8 0.8 gather_fusion
  18.5 0.0 copy-start.9
  18.5 0.9 %reshape.52 = f32[16,4,2048]{2,1,0:T(4,128)} reshape(f32[64,2048]{1,0:T(8,128)S(1)} %gather_fusion) | data formatting | bytes 1048576 | tf_op jit(solution)/shard_map/reshape | solution.py:162
  19.5 0.0 copy-start.4
  19.5 0.0 copy-start.5
  19.5 0.0 copy-start.6
  19.5 0.0 copy-start.7
  19.5 0.0 copy-start.8
  19.5 6.7 %all-to-all-start = ((f32[16,4,2048]{2,1,0:T(4,128)}), f32[16,4,2048]{2,1,0:T(4,128)S(1)}, u32[]{:S(2)}, u32[]{:S(2)}) async-start(f32[16,4,2048]{2,1,0:T(4,128)} %reshape.52), calls=%async_computation | async-start | bytes 1048576 | tf_op jit(solution)/shard_map/all_to_all | solution.py:162
  26.2 0.0 copy-done.9
  26.2 0.1 copy.15
  26.3 0.1 reshape_squeeze.6.cols_ref
  26.4 4.2 %sddp_split.1 = (bf16[16,256,128]{2,1,0:T(8,128)(2,1)}, bf16[16,256,128]{2,1,0:T(8,128)(2,1)}, bf16[16,128,256]{2,1,0:T(8,128)(2,1)}, bf16[16,128,256]{2,1,0:T(8,128)(2,1)}) custom-call(f32[16,2,128,128]{3,2,1,0:T(8,128)} %bitcast.21), custom_call_target="tpu_custom_call" | custom-call | flops 2097152 | bytes 4194304 | tf_op jit(solution)/shard_map/sddp_split/pallas_call | solution.py:52
  30.5 10.1 %all-to-all-done = f32[16,4,2048]{2,1,0:T(4,128)S(1)} async-done(((f32[16,4,2048]{2,1,0:T(4,128)}), f32[16,4,2048]{2,1,0:T(4,128)S(1)}, u32[]{:S(2)}, u32[]{:S(2)}) %all-to-all-start) | async-done | bytes 524320 | tf_op jit(solution)/shard_map/all_to_all | solution.py:162
  40.6 0.2 reshape.53.rows_ref
  40.8 0.0 copy-done.4
  40.8 0.0 copy-done.5
  40.8 0.0 copy-done.6
  40.8 0.0 copy-done.7
  40.8 0.0 copy-done.8
  40.8 0.0 copy-start
  40.9 1.2 %copy-done = bf16[16,256,128]{2,1,0:T(8,128)(2,1)S(1)} copy-done((bf16[16,256,128]{2,1,0:T(8,128)(2,1)S(1)}, bf16[16,256,128]{2,1,0:T(8,128)(2,1)}, u32[]{:S(2)}) %copy-start) | copy-done | bytes 1048600
  42.1 0.0 copy-start.1
  42.1 1.2 %copy-done.1 = bf16[16,256,128]{2,1,0:T(8,128)(2,1)S(1)} copy-done((bf16[16,256,128]{2,1,0:T(8,128)(2,1)S(1)}, bf16[16,256,128]{2,1,0:T(8,128)(2,1)}, u32[]{:S(2)}) %copy-start.1) | copy-done | bytes 1048600
  43.3 1.2 %copy-done.2 = bf16[16,128,256]{2,1,0:T(8,128)(2,1)S(1)} copy-done((bf16[16,128,256]{2,1,0:T(8,128)(2,1)S(1)}, bf16[16,128,256]{2,1,0:T(8,128)(2,1)}, u32[]{:S(2)}) %copy-start.2) | copy-done | bytes 1048600
  44.5 1.2 %copy-done.3 = bf16[16,128,256]{2,1,0:T(8,128)(2,1)S(1)} copy-done((bf16[16,128,256]{2,1,0:T(8,128)(2,1)S(1)}, bf16[16,128,256]{2,1,0:T(8,128)(2,1)}, u32[]{:S(2)}) %copy-start.3) | copy-done | bytes 1048600
  45.7 5.5 %sddp_solve.1 = f32[64,2176]{1,0:T(8,128)S(1)} custom-call(s32[32]{0:T(128)S(1)} %reshape_squeeze.6.cols_ref, f32[64,2048]{1,0:T(8,128)S(1)} %reshape.53.rows_ref, f32[1,2048]{1,0:T(1,128)S(1)} %bitcast.16, f32[1,2048]{1,0:T(1,128)S(1)} %bitcast.17, f32[1,2048]{1,0:T(1,128)S(1)} %bitcast.18, f32[1,2048]{1,0:T(1,128)S(1)} %bitcast.19, ...), custom_call_target="tpu_custom_call" | custom-call | flops 1610612736 | bytes 3670016 | tf_op jit(solution)/shard_map/sddp_solve/pallas_call | solution.py:130
  51.2 0.9 %reshape.54 = f32[16,4,2176]{2,1,0:T(4,128)} reshape(f32[64,2176]{1,0:T(8,128)S(1)} %sddp_solve.1) | data formatting | bytes 1114112 | tf_op jit(solution)/shard_map/reshape | solution.py:166
  52.2 3.6 %all-to-all-start.1 = ((f32[16,4,2176]{2,1,0:T(4,128)}), f32[16,4,2176]{2,1,0:T(4,128)S(1)}, u32[]{:S(2)}, u32[]{:S(2)}) async-start(f32[16,4,2176]{2,1,0:T(4,128)} %reshape.54), calls=%async_computation.1 | async-start | bytes 1114112 | tf_op jit(solution)/shard_map/all_to_all | solution.py:166
  55.8 17.6 %all-to-all-done.1 = f32[16,4,2176]{2,1,0:T(4,128)S(1)} async-done(((f32[16,4,2176]{2,1,0:T(4,128)}), f32[16,4,2176]{2,1,0:T(4,128)S(1)}, u32[]{:S(2)}, u32[]{:S(2)}) %all-to-all-start.1) | async-done | bytes 557088 | tf_op jit(solution)/shard_map/all_to_all | solution.py:166
  73.4 0.2 reshape.55
  73.6 0.7 gather_fusion.1
  74.3 2.4 %collective-permute-start.1 = (f32[32,2176]{1,0:T(8,128)S(1)}, f32[32,2176]{1,0:T(8,128)S(1)}, u32[]{:S(2)}, u32[]{:S(2)}) collective-permute-start(f32[32,2176]{1,0:T(8,128)S(1)} %gather_fusion.1), channel_id=1, source_target_pairs={{0,496},{16,0},{32,16},{48,32},{64,48},{80,64},{96,80},{112,96},{1... | collective-permute-start | bytes 835592 | tf_op jit(solution)/shard_map/ppermute | solution.py:20
  76.7 11.6 %collective-permute-done.1 = f32[32,2176]{1,0:T(8,128)S(1)} collective-permute-done((f32[32,2176]{1,0:T(8,128)S(1)}, f32[32,2176]{1,0:T(8,128)S(1)}, u32[]{:S(2)}, u32[]{:S(2)}) %collective-permute-start.1) | collective-permute-done | bytes 278560 | tf_op jit(solution)/shard_map/ppermute | solution.py:20
  88.2 0.7 slice_bitcast_fusion
  88.9 0.6 slice_reduce_fusion
  (7 shorter events, 0.0 us)
Async XLA Ops:
  2.3 14.6 %collective-permute-start = (f32[32,2176]{1,0:T(8,128)S(1)}, f32[32,2176]{1,0:T(8,128)S(1)}, u32[]{:S(2)}, u32[]{:S(2)}) collective-permute-start(f32[32,2176]{1,0:T(8,128)S(1)} %pad_maximum_fusion), channel_id=1, source_target_pairs={{0,16},{16,32},{32,48},{48,64},{64,80},{80,96},{96,112},{112,128},... | collective-permute-start | bytes 835592 | tf_op jit(solution)/shard_map/ppermute | solution.py:20
  18.5 7.7 %copy-start.9 = (s32[1,1,16,2]{2,3,1,0:T(2,128)S(1)}, s32[1,1,16,2]{2,3,1,0:T(2,128)}, u32[]{:S(2)}) copy-start(s32[1,1,16,2]{2,3,1,0:T(2,128)} %param.17) | copy-start | bytes 388
  19.5 21.3 %copy-start.4 = (f32[1,1,2048]{2,1,0:T(1,128)S(1)}, f32[1,1,2048]{2,1,0:T(1,128)}, u32[]{:S(2)}) copy-start(f32[1,1,2048]{2,1,0:T(1,128)} %param.11) | copy-start | bytes 24580
  19.5 21.3 %copy-start.5 = (f32[1,1,2048]{2,1,0:T(1,128)S(1)}, f32[1,1,2048]{2,1,0:T(1,128)}, u32[]{:S(2)}) copy-start(f32[1,1,2048]{2,1,0:T(1,128)} %param.12) | copy-start | bytes 24580
  19.5 21.3 %copy-start.6 = (f32[1,1,2048]{2,1,0:T(1,128)S(1)}, f32[1,1,2048]{2,1,0:T(1,128)}, u32[]{:S(2)}) copy-start(f32[1,1,2048]{2,1,0:T(1,128)} %param.13) | copy-start | bytes 24580
  19.5 21.4 %copy-start.7 = (f32[1,1,2048]{2,1,0:T(1,128)S(1)}, f32[1,1,2048]{2,1,0:T(1,128)}, u32[]{:S(2)}) copy-start(f32[1,1,2048]{2,1,0:T(1,128)} %param.14) | copy-start | bytes 24580
  19.5 21.4 %copy-start.8 = (f32[1,1,2048]{2,1,0:T(1,128)S(1)}, f32[1,1,2048]{2,1,0:T(1,128)}, u32[]{:S(2)}) copy-start(f32[1,1,2048]{2,1,0:T(1,128)} %param.15) | copy-start | bytes 24580
  19.5 21.1 %all-to-all-start = ((f32[16,4,2048]{2,1,0:T(4,128)}), f32[16,4,2048]{2,1,0:T(4,128)S(1)}, u32[]{:S(2)}, u32[]{:S(2)}) async-start(f32[16,4,2048]{2,1,0:T(4,128)} %reshape.52), calls=%async_computation | async-start | bytes 1048576 | tf_op jit(solution)/shard_map/all_to_all | solution.py:162
  40.8 1.2 %copy-start = (bf16[16,256,128]{2,1,0:T(8,128)(2,1)S(1)}, bf16[16,256,128]{2,1,0:T(8,128)(2,1)}, u32[]{:S(2)}) copy-start(bf16[16,256,128]{2,1,0:T(8,128)(2,1)} %get-tuple-element.6.fh) | copy-start | bytes 3145732
  42.1 1.2 %copy-start.1 = (bf16[16,256,128]{2,1,0:T(8,128)(2,1)S(1)}, bf16[16,256,128]{2,1,0:T(8,128)(2,1)}, u32[]{:S(2)}) copy-start(bf16[16,256,128]{2,1,0:T(8,128)(2,1)} %get-tuple-element.7.fl) | copy-start | bytes 3145732
  43.3 1.2 %copy-start.2 = (bf16[16,128,256]{2,1,0:T(8,128)(2,1)S(1)}, bf16[16,128,256]{2,1,0:T(8,128)(2,1)}, u32[]{:S(2)}) copy-start(bf16[16,128,256]{2,1,0:T(8,128)(2,1)} %get-tuple-element.8.ah) | copy-start | bytes 3145732
  44.5 1.2 %copy-start.3 = (bf16[16,128,256]{2,1,0:T(8,128)(2,1)S(1)}, bf16[16,128,256]{2,1,0:T(8,128)(2,1)}, u32[]{:S(2)}) copy-start(bf16[16,128,256]{2,1,0:T(8,128)(2,1)} %get-tuple-element.9.al) | copy-start | bytes 3145732
  52.2 21.2 %all-to-all-start.1 = ((f32[16,4,2176]{2,1,0:T(4,128)}), f32[16,4,2176]{2,1,0:T(4,128)S(1)}, u32[]{:S(2)}, u32[]{:S(2)}) async-start(f32[16,4,2176]{2,1,0:T(4,128)} %reshape.54), calls=%async_computation.1 | async-start | bytes 1114112 | tf_op jit(solution)/shard_map/all_to_all | solution.py:166
  74.3 14.0 %collective-permute-start.1 = (f32[32,2176]{1,0:T(8,128)S(1)}, f32[32,2176]{1,0:T(8,128)S(1)}, u32[]{:S(2)}, u32[]{:S(2)}) collective-permute-start(f32[32,2176]{1,0:T(8,128)S(1)} %gather_fusion.1), channel_id=1, source_target_pairs={{0,496},{16,0},{32,16},{48,32},{64,48},{80,64},{96,80},{112,96},{1... | collective-permute-start | bytes 835592 | tf_op jit(solution)/shard_map/ppermute | solution.py:20

commit v4 on v2

--- a/solution.py
+++ b/solution.py
@@ -133,25 +133,24 @@
     width = trial_states.shape[3]
     capacity = 2 * tr_rows // states
     slots = states * capacity
-    own_rows = trial_states.reshape(tr_rows, width)
-    own_dest = successor.reshape(tr_rows)
-    tag = jnp.broadcast_to(own_dest.astype(jnp.float32)[:, None], (tr_rows, BS))
-    sent = shifted(jnp.concatenate([own_rows, tag], axis=1), "week", 1)
-    rows, dest = sent[:, :width], sent[:, width].astype(jnp.int32)
+    nblk, kblk = block_cols.shape[2], block_cols.shape[3]
+    rows = trial_states.reshape(tr_rows, width)
+    dest = successor.reshape(tr_rows)
+    vectors = jnp.stack([a.reshape(width) for a in (inflow, unit_cost, curvature, target, release_cap)])
+    cols = jnp.zeros((1, width), jnp.float32).at[0, :nblk * kblk].set(
+        block_cols.reshape(-1).astype(jnp.float32))
+    node_blocks, node_small = shifted((block_values[0, 0], jnp.concatenate([vectors, cols])), "week", -1)
     marked = (dest[:, None] == jnp.arange(states, dtype=jnp.int32)[None, :]).astype(jnp.int32)
     ranked = jnp.sum(jnp.cumsum(marked, axis=0) * marked, axis=1) - 1
     slot_ids = dest * capacity + ranked
     hit = slot_ids[None, :] == jnp.arange(slots, dtype=jnp.int32)[:, None]
     source = jnp.sum(jnp.where(hit, jnp.arange(tr_rows, dtype=jnp.int32)[None, :], 0), axis=1)
-    filled = jnp.any(hit, axis=1)
-    packed = jnp.where(filled[:, None], jnp.take(rows, source, axis=0), 0.0)
+    packed = jnp.take(rows, source, axis=0, mode="clip")
     arrived = lax.all_to_all(packed.reshape(states, capacity, width), "markov", 0, 0, tiled=True)
-    solved = solve_block(arrived.reshape(slots, width), inflow.reshape(width),
-                         unit_cost.reshape(width), curvature.reshape(width), target.reshape(width),
-                         release_cap.reshape(width), block_values[0, 0], block_cols[0, 0])
+    node_cols = node_small[5, :nblk * kblk].astype(jnp.int32).reshape(nblk, kblk)
+    solved = solve_block(arrived.reshape(slots, width), *node_small[:5], node_blocks, node_cols)
     back = lax.all_to_all(solved.reshape(states, capacity, -1), "markov", 0, 0, tiled=True)
-    mine = jnp.take(back.reshape(slots, -1), slot_ids, axis=0)
-    mine = shifted(mine, "week", -1)
+    mine = jnp.take(back.reshape(slots, -1), slot_ids, axis=0, mode="clip")
     return (mine[:, :width].reshape(1, 1, tr_rows, width),
             mine[:, width].reshape(1, 1, tr_rows))
 

time: 86 us -> 111 us (1.29)
  waiting for transfers between devices: 47.5 us -> 75 us
  starting transfers between devices: 22.9 us -> 18.8 us
    ppermute x2, waiting for transfers between devices: 15.8 us -> 36.6 us  [shifted(): return lax.ppermute(value, axis, pairs)]
    all_to_all x1, waiting for transfers between devices: 14.2 us -> 21.9 us  [on_device(): lax.all_to_all(packed.reshape(states, capacity, width), 'markov', 0, 0, t...]
    ppermute x2, starting transfers between devices: 12.8 us -> 5.69 us  [shifted(): return lax.ppermute(value, axis, pairs)]
    all_to_all x1, starting transfers between devices: 6.57 us -> 9.55 us  [on_device(): lax.all_to_all(packed.reshape(states, capacity, width), 'markov', 0, 0, t...]
    another operation x0 -> x2, other arithmetic: none -> 1.29 us
    select_n x4 -> x0, other arithmetic: 1.25 us -> none  [the longest x2 1.03 us: on_device(): packed = jnp.where(filled[:, None], jnp.take(rows, source, axis=0), 0.0)]
  transfers between devices with their start and end apart: 4 -> 4, of which waited for: 4 -> 3; matrix products, arithmetic and copies ran while one was open for 0% -> 5% of each run, Pallas kernels for 0% -> 0%
where the time goes in v4:
time: 111 us; the launch traced here: 110 us
  waiting for transfers between devices  75 us (68%)
  starting transfers between devices  18.8 us (17%)
  Pallas kernels  5.84 us (5%)
  local copies, waits for them, and re-layouts  5.38 us (5%)
  other arithmetic  3.69 us (3%)
    ppermute x2, waiting for transfers between devices, shifted(): return lax.ppermute(value, axis, pairs)  36.6 us
    all_to_all x1, waiting for transfers between devices, on_device(): lax.all_to_all(packed.reshape(states, capacity, width), 'markov', 0, 0, t...  21.9 us
    all_to_all x1, waiting for transfers between devices, on_device(): lax.all_to_all(solved.reshape(states, capacity, -1), 'markov', 0, 0, tile...  16.5 us
    all_to_all x1, starting transfers between devices, on_device(): lax.all_to_all(packed.reshape(states, capacity, width), 'markov', 0, 0, t...  9.55 us
    pallas_call x1, Pallas kernels, solve_block(): pl.pallas_call(functools.partial(solve_kernel, nblk, kblk), out_shape=jax...  5.84 us
    ppermute x2, starting transfers between devices, shifted(): return lax.ppermute(value, axis, pairs)  5.69 us
    all_to_all x1, starting transfers between devices, on_device(): lax.all_to_all(solved.reshape(states, capacity, -1), 'markov', 0, 0, tile...  3.58 us
  transfers between devices with their start and end apart: 4, of which 3 were waited for; matrix products, arithmetic and copies ran while one was open for 5% of the time, Pallas kernels for 0%

profile of v4, /device:TPU:57, one launch (start us, length us, event | category | flops | bytes accessed | tf_op | source)
XLA Modules:
  0.0 109.6 jit_solution(12775997897690605595)
XLA Ops:
  0.6 0.0 copy-start
  0.6 2.7 %collective-permute-start.1 = (f32[16,2,128,128]{3,2,1,0:T(8,128)}, f32[16,2,128,128]{3,2,1,0:T(8,128)S(1)}, u32[]{:S(2)}, u32[]{:S(2)}) collective-permute-start(f32[16,2,128,128]{3,2,1,0:T(8,128)} %bitcast.33), channel_id=1, source_target_pairs={{0,496},{16,0},{32,16},{48,32},{64,48},{80,64},{96,80},{112,96},{1... | collective-permute-start | bytes 6291464 | tf_op jit(solution)/shard_map/ppermute | solution.py:20
  3.4 0.7 fusion
  4.1 0.1 reduce_window_sum.11
  4.2 0.8 select_reduce_fusion.1
  5.0 0.7 multiply_add_fusion
  5.7 0.1 select_reduce_fusion
  5.8 0.0 copy-done
  5.8 0.8 gather_fusion
  6.5 0.0 copy-start.7
  6.5 0.0 copy-start.1
  6.5 0.0 copy-start.2
  6.6 0.0 copy-start.3
  6.6 0.0 copy-start.4
  6.6 0.0 copy-start.5
  6.6 0.9 reshape.107
  7.5 9.5 %all-to-all-start = ((f32[16,4,2048]{2,1,0:T(4,128)}), f32[16,4,2048]{2,1,0:T(4,128)S(1)}, u32[]{:S(2)}, u32[]{:S(2)}) async-start(f32[16,4,2048]{2,1,0:T(4,128)} %reshape.107), calls=%async_computation | async-start | bytes 1048576 | tf_op jit(solution)/shard_map/all_to_all | solution.py:149
  17.1 0.6 compare_reduce_fusion
  17.7 0.0 copy-done.7
  17.7 0.6 convert_select_fusion
  18.4 0.1 copy.13
  18.5 0.1 reshape.104
  18.6 0.0 copy-done.1
  18.6 0.0 copy-done.2
  18.6 0.0 copy-done.3
  18.6 0.0 copy-done.4
  18.6 0.0 copy-done.5
  18.6 0.1 concatenate.5
  18.7 3.0 %collective-permute-start = (f32[6,2048]{1,0:T(8,128)S(1)}, f32[6,2048]{1,0:T(8,128)S(1)}, u32[]{:S(2)}, u32[]{:S(2)}) collective-permute-start(f32[6,2048]{1,0:T(8,128)S(1)} %concatenate.5), channel_id=1, source_target_pairs={{0,496},{16,0},{32,16},{48,32},{64,48},{80,64},{96,80},{112,96},{1... | collective-permute-start | bytes 147464 | tf_op jit(solution)/shard_map/ppermute | solution.py:20
  21.7 36.6 %collective-permute-done = f32[6,2048]{1,0:T(8,128)S(1)} collective-permute-done((f32[6,2048]{1,0:T(8,128)S(1)}, f32[6,2048]{1,0:T(8,128)S(1)}, u32[]{:S(2)}, u32[]{:S(2)}) %collective-permute-start) | collective-permute-done | bytes 49184 | tf_op jit(solution)/shard_map/ppermute | solution.py:20
  58.3 21.9 %all-to-all-done = f32[16,4,2048]{2,1,0:T(4,128)S(1)} async-done(((f32[16,4,2048]{2,1,0:T(4,128)}), f32[16,4,2048]{2,1,0:T(4,128)S(1)}, u32[]{:S(2)}, u32[]{:S(2)}) %all-to-all-start) | async-done | bytes 524320 | tf_op jit(solution)/shard_map/all_to_all | solution.py:149
  80.2 0.2 reshape.108.rows_ref
  80.4 0.0 collective-permute-done.1.bv_ref
  80.4 5.8 %sddp_solve.1 = f32[64,2176]{1,0:T(8,128)S(1)} custom-call(s32[32]{0:T(128)S(1)} %fusion.1.cols_ref, f32[64,2048]{1,0:T(8,128)S(1)} %reshape.108.rows_ref, f32[1,2048]{1,0:T(1,128)S(1)} %get-tuple-element.18.xi_ref, f32[1,2048]{1,0:T(1,128)S(1)} %get-tuple-element.17.c_ref, f32[1,2048]{1,0:T(1,128)S(1)} %get-tuple-element.16.q_ref, ...), custom_call_target="tpu_custom_call" | custom-call | flops 1610612736 | bytes 3670016 | tf_op jit(solution)/shard_map/sddp_solve/pallas_call | solution.py:115
  86.3 0.0 copy-start.6
  86.3 1.0 reshape.109
  87.2 3.6 %all-to-all-start.1 = ((f32[16,4,2176]{2,1,0:T(4,128)}), f32[16,4,2176]{2,1,0:T(4,128)S(1)}, u32[]{:S(2)}, u32[]{:S(2)}) async-start(f32[16,4,2176]{2,1,0:T(4,128)} %reshape.109), calls=%async_computation.1 | async-start | bytes 1114112 | tf_op jit(solution)/shard_map/all_to_all | solution.py:152
  90.8 0.0 copy-done.6
  90.9 16.5 %all-to-all-done.1 = f32[16,4,2176]{2,1,0:T(4,128)S(1)} async-done(((f32[16,4,2176]{2,1,0:T(4,128)}), f32[16,4,2176]{2,1,0:T(4,128)S(1)}, u32[]{:S(2)}, u32[]{:S(2)}) %all-to-all-start.1) | async-done | bytes 557088 | tf_op jit(solution)/shard_map/all_to_all | solution.py:152
  107.3 0.2 reshape.110
  107.5 0.7 gather_fusion.1
  108.2 0.7 slice_bitcast_fusion
  108.9 0.6 slice_reduce_fusion
  (6 shorter events, 0.1 us)
Async XLA Ops:
  0.6 5.1 %copy-start = (f32[1,1,32,2048]{3,2,1,0:T(8,128)S(1)}, f32[1,1,32,2048]{3,2,1,0:T(8,128)}, u32[]{:S(2)}) copy-start(f32[1,1,32,2048]{3,2,1,0:T(8,128)} %param.11) | copy-start | bytes 786436
  0.6 79.8 %collective-permute-start.1 = (f32[16,2,128,128]{3,2,1,0:T(8,128)}, f32[16,2,128,128]{3,2,1,0:T(8,128)S(1)}, u32[]{:S(2)}, u32[]{:S(2)}) collective-permute-start(f32[16,2,128,128]{3,2,1,0:T(8,128)} %bitcast.33), channel_id=1, source_target_pairs={{0,496},{16,0},{32,16},{48,32},{64,48},{80,64},{96,80},{112,96},{1... | collective-permute-start | bytes 6291464 | tf_op jit(solution)/shard_map/ppermute | solution.py:20
  6.5 11.2 %copy-start.7 = (s32[1,1,16,2]{2,3,1,0:T(2,128)S(1)}, s32[1,1,16,2]{2,3,1,0:T(2,128)}, u32[]{:S(2)}) copy-start(s32[1,1,16,2]{2,3,1,0:T(2,128)} %param.19) | copy-start | bytes 388
  6.5 12.0 %copy-start.1 = (f32[1,1,2048]{2,1,0:T(1,128)S(1)}, f32[1,1,2048]{2,1,0:T(1,128)}, u32[]{:S(2)}) copy-start(f32[1,1,2048]{2,1,0:T(1,128)} %param.13) | copy-start | bytes 24580
  6.5 12.0 %copy-start.2 = (f32[1,1,2048]{2,1,0:T(1,128)S(1)}, f32[1,1,2048]{2,1,0:T(1,128)}, u32[]{:S(2)}) copy-start(f32[1,1,2048]{2,1,0:T(1,128)} %param.14) | copy-start | bytes 24580
  6.6 12.0 %copy-start.3 = (f32[1,1,2048]{2,1,0:T(1,128)S(1)}, f32[1,1,2048]{2,1,0:T(1,128)}, u32[]{:S(2)}) copy-start(f32[1,1,2048]{2,1,0:T(1,128)} %param.15) | copy-start | bytes 24580
  6.6 12.0 %copy-start.4 = (f32[1,1,2048]{2,1,0:T(1,128)S(1)}, f32[1,1,2048]{2,1,0:T(1,128)}, u32[]{:S(2)}) copy-start(f32[1,1,2048]{2,1,0:T(1,128)} %param.16) | copy-start | bytes 24580
  6.6 12.0 %copy-start.5 = (f32[1,1,2048]{2,1,0:T(1,128)S(1)}, f32[1,1,2048]{2,1,0:T(1,128)}, u32[]{:S(2)}) copy-start(f32[1,1,2048]{2,1,0:T(1,128)} %param.17) | copy-start | bytes 24580
  7.5 72.7 %all-to-all-start = ((f32[16,4,2048]{2,1,0:T(4,128)}), f32[16,4,2048]{2,1,0:T(4,128)S(1)}, u32[]{:S(2)}, u32[]{:S(2)}) async-start(f32[16,4,2048]{2,1,0:T(4,128)} %reshape.107), calls=%async_computation | async-start | bytes 1048576 | tf_op jit(solution)/shard_map/all_to_all | solution.py:149
  18.7 39.6 %collective-permute-start = (f32[6,2048]{1,0:T(8,128)S(1)}, f32[6,2048]{1,0:T(8,128)S(1)}, u32[]{:S(2)}, u32[]{:S(2)}) collective-permute-start(f32[6,2048]{1,0:T(8,128)S(1)} %concatenate.5), channel_id=1, source_target_pairs={{0,496},{16,0},{32,16},{48,32},{64,48},{80,64},{96,80},{112,96},{1... | collective-permute-start | bytes 147464 | tf_op jit(solution)/shard_map/ppermute | solution.py:20
  86.3 4.6 %copy-start.6 = (s32[1,1,32,1]{2,3,1,0:T(1,128)S(1)}, s32[1,1,32,1]{2,3,1,0:T(1,128)}, u32[]{:S(2)}) copy-start(s32[1,1,32,1]{2,3,1,0:T(1,128)} %param.12) | copy-start | bytes 388
  87.2 20.1 %all-to-all-start.1 = ((f32[16,4,2176]{2,1,0:T(4,128)}), f32[16,4,2176]{2,1,0:T(4,128)S(1)}, u32[]{:S(2)}, u32[]{:S(2)}) async-start(f32[16,4,2176]{2,1,0:T(4,128)} %reshape.109), calls=%async_computation.1 | async-start | bytes 1114112 | tf_op jit(solution)/shard_map/all_to_all | solution.py:152

commit v5 on v2

--- a/solution.py
+++ b/solution.py
@@ -143,14 +143,13 @@
     slot_ids = dest * capacity + ranked
     hit = slot_ids[None, :] == jnp.arange(slots, dtype=jnp.int32)[:, None]
     source = jnp.sum(jnp.where(hit, jnp.arange(tr_rows, dtype=jnp.int32)[None, :], 0), axis=1)
-    filled = jnp.any(hit, axis=1)
-    packed = jnp.where(filled[:, None], jnp.take(rows, source, axis=0), 0.0)
+    packed = jnp.take(rows, source, axis=0, mode="clip")
     arrived = lax.all_to_all(packed.reshape(states, capacity, width), "markov", 0, 0, tiled=True)
     solved = solve_block(arrived.reshape(slots, width), inflow.reshape(width),
                          unit_cost.reshape(width), curvature.reshape(width), target.reshape(width),
                          release_cap.reshape(width), block_values[0, 0], block_cols[0, 0])
     back = lax.all_to_all(solved.reshape(states, capacity, -1), "markov", 0, 0, tiled=True)
-    mine = jnp.take(back.reshape(slots, -1), slot_ids, axis=0)
+    mine = jnp.take(back.reshape(slots, -1), slot_ids, axis=0, mode="clip")
     mine = shifted(mine, "week", -1)
     return (mine[:, :width].reshape(1, 1, tr_rows, width),
             mine[:, width].reshape(1, 1, tr_rows))

time: 86 us -> 85.3 us (level)
  other arithmetic: 3.63 us -> 2.29 us
    select_n x4 -> x0, other arithmetic: 1.25 us -> none  [the longest x2 1.03 us: on_device(): packed = jnp.where(filled[:, None], jnp.take(rows, source, axis=0), 0.0)]
    reshape x1 -> x2, local copies, waits for them, and re-layouts: 0.19 us -> 1.13 us  [the longest x1 0.94 us: on_device(): packed.reshape(states, capacity, width)]
where the time goes in v5:
time: 85.3 us; the launch traced here: 84.9 us
  waiting for transfers between devices  47.6 us (56%)
  starting transfers between devices  22.9 us (27%)
  Pallas kernels  5.8 us (7%)
  local copies, waits for them, and re-layouts  5.42 us (6%)
  other arithmetic  2.29 us (3%)
    all_to_all x1, waiting for transfers between devices, on_device(): lax.all_to_all(solved.reshape(states, capacity, -1), 'markov', 0, 0, tile...  17.6 us
    ppermute x2, waiting for transfers between devices, shifted(): return lax.ppermute(value, axis, pairs)  15.8 us
    all_to_all x1, waiting for transfers between devices, on_device(): lax.all_to_all(packed.reshape(states, capacity, width), 'markov', 0, 0, t...  14.2 us
    ppermute x2, starting transfers between devices, shifted(): return lax.ppermute(value, axis, pairs)  12.8 us
    all_to_all x1, starting transfers between devices, on_device(): lax.all_to_all(packed.reshape(states, capacity, width), 'markov', 0, 0, t...  6.57 us
    pallas_call x1, Pallas kernels, solve_block(): pl.pallas_call(functools.partial(solve_kernel, nblk, kblk), out_shape=jax...  5.8 us
    all_to_all x1, starting transfers between devices, on_device(): lax.all_to_all(solved.reshape(states, capacity, -1), 'markov', 0, 0, tile...  3.58 us
  transfers between devices with their start and end apart: 4, of which 4 were waited for; matrix products, arithmetic and copies ran while one was open for 0% of the time, Pallas kernels for 0%

profile of v5, /device:TPU:57, one launch (start us, length us, event | category | flops | bytes accessed | tf_op | source)
XLA Modules:
  0.0 84.9 jit_solution(2303534582858247268)
XLA Ops:
  0.6 0.7 convert_bitcast_fusion
  1.3 0.1 broadcast_in_dim.19
  1.4 1.0 %pad_maximum_fusion = f32[32,2176]{1,0:T(8,128)S(1)} fusion(f32[32,128]{1,0:T(8,128)S(1)} %broadcast_in_dim.19, f32[32,2048]{1,0:T(8,128)} %bitcast.22), kind=kLoop, calls=%fused_computation.2 | loop fusion | flops 69632 | bytes 557056 | tf_op jit(solution)/shard_map/concatenate | solution.py:139
  2.3 10.4 %collective-permute-start = (f32[32,2176]{1,0:T(8,128)S(1)}, f32[32,2176]{1,0:T(8,128)S(1)}, u32[]{:S(2)}, u32[]{:S(2)}) collective-permute-start(f32[32,2176]{1,0:T(8,128)S(1)} %pad_maximum_fusion), channel_id=1, source_target_pairs={{0,16},{16,32},{32,48},{48,64},{64,80},{80,96},{96,112},{112,128},... | collective-permute-start | bytes 835592 | tf_op jit(solution)/shard_map/ppermute | solution.py:20
  12.7 4.2 %collective-permute-done = f32[32,2176]{1,0:T(8,128)S(1)} collective-permute-done((f32[32,2176]{1,0:T(8,128)S(1)}, f32[32,2176]{1,0:T(8,128)S(1)}, u32[]{:S(2)}, u32[]{:S(2)}) %collective-permute-start) | collective-permute-done | bytes 278560 | tf_op jit(solution)/shard_map/ppermute | solution.py:20
  17.0 0.1 fusion.1
  17.1 0.1 fusion
  17.2 0.1 reduce_window_sum.11
  17.2 0.2 select_reduce_fusion.1
  17.4 0.1 copy.16
  17.5 0.1 add_reduce_fusion
  17.6 0.1 select_reduce_fusion
  17.8 0.0 copy-start.6
  17.8 0.8 gather_fusion
  18.5 0.0 copy-start
  18.5 0.0 copy-start.1
  18.6 0.0 copy-start.2
  18.6 0.0 copy-start.3
  18.6 0.0 copy-start.4
  18.6 0.0 copy-start.5
  18.6 0.9 %reshape.52 = f32[16,4,2048]{2,1,0:T(4,128)} reshape(f32[64,2048]{1,0:T(8,128)S(1)} %gather_fusion) | data formatting | bytes 1048576 | tf_op jit(solution)/shard_map/reshape | solution.py:147
  19.5 6.6 %all-to-all-start = ((f32[16,4,2048]{2,1,0:T(4,128)}), f32[16,4,2048]{2,1,0:T(4,128)S(1)}, u32[]{:S(2)}, u32[]{:S(2)}) async-start(f32[16,4,2048]{2,1,0:T(4,128)} %reshape.52), calls=%async_computation | async-start | bytes 1048576 | tf_op jit(solution)/shard_map/all_to_all | solution.py:147
  26.1 0.0 copy-done.6
  26.1 0.1 copy.15
  26.2 0.1 reshape_squeeze.6.cols_ref
  26.3 14.2 %all-to-all-done = f32[16,4,2048]{2,1,0:T(4,128)S(1)} async-done(((f32[16,4,2048]{2,1,0:T(4,128)}), f32[16,4,2048]{2,1,0:T(4,128)S(1)}, u32[]{:S(2)}, u32[]{:S(2)}) %all-to-all-start) | async-done | bytes 524320 | tf_op jit(solution)/shard_map/all_to_all | solution.py:147
  40.5 0.2 reshape.53.rows_ref
  40.7 0.0 copy-done
  40.7 0.0 copy-done.1
  40.7 0.0 copy-done.2
  40.7 0.0 copy-done.3
  40.7 0.0 copy-done.4
  40.7 0.0 copy-done.5
  40.8 5.8 %sddp_solve.1 = f32[64,2176]{1,0:T(8,128)S(1)} custom-call(s32[32]{0:T(128)S(1)} %reshape_squeeze.6.cols_ref, f32[64,2048]{1,0:T(8,128)S(1)} %reshape.53.rows_ref, f32[1,2048]{1,0:T(1,128)S(1)} %bitcast.17, f32[1,2048]{1,0:T(1,128)S(1)} %bitcast.18, f32[1,2048]{1,0:T(1,128)S(1)} %bitcast.19, f32[1,2048]{1,0:T(1,128)S(1)} %bitcast.20, ...), custom_call_target="tpu_custom_call" | custom-call | flops 1610612736 | bytes 3670016 | tf_op jit(solution)/shard_map/sddp_solve/pallas_call | solution.py:115
  46.6 0.9 %reshape.54 = f32[16,4,2176]{2,1,0:T(4,128)} reshape(f32[64,2176]{1,0:T(8,128)S(1)} %sddp_solve.1) | data formatting | bytes 1114112 | tf_op jit(solution)/shard_map/reshape | solution.py:151
  47.5 3.6 %all-to-all-start.1 = ((f32[16,4,2176]{2,1,0:T(4,128)}), f32[16,4,2176]{2,1,0:T(4,128)S(1)}, u32[]{:S(2)}, u32[]{:S(2)}) async-start(f32[16,4,2176]{2,1,0:T(4,128)} %reshape.54), calls=%async_computation.1 | async-start | bytes 1114112 | tf_op jit(solution)/shard_map/all_to_all | solution.py:151
  51.1 17.6 %all-to-all-done.1 = f32[16,4,2176]{2,1,0:T(4,128)S(1)} async-done(((f32[16,4,2176]{2,1,0:T(4,128)}), f32[16,4,2176]{2,1,0:T(4,128)S(1)}, u32[]{:S(2)}, u32[]{:S(2)}) %all-to-all-start.1) | async-done | bytes 557088 | tf_op jit(solution)/shard_map/all_to_all | solution.py:151
  68.7 0.2 reshape.55
  68.9 0.7 gather_fusion.1
  69.6 2.4 %collective-permute-start.1 = (f32[32,2176]{1,0:T(8,128)S(1)}, f32[32,2176]{1,0:T(8,128)S(1)}, u32[]{:S(2)}, u32[]{:S(2)}) collective-permute-start(f32[32,2176]{1,0:T(8,128)S(1)} %gather_fusion.1), channel_id=1, source_target_pairs={{0,496},{16,0},{32,16},{48,32},{64,48},{80,64},{96,80},{112,96},{1... | collective-permute-start | bytes 835592 | tf_op jit(solution)/shard_map/ppermute | solution.py:20
  72.0 11.6 %collective-permute-done.1 = f32[32,2176]{1,0:T(8,128)S(1)} collective-permute-done((f32[32,2176]{1,0:T(8,128)S(1)}, f32[32,2176]{1,0:T(8,128)S(1)}, u32[]{:S(2)}, u32[]{:S(2)}) %collective-permute-start.1) | collective-permute-done | bytes 278560 | tf_op jit(solution)/shard_map/ppermute | solution.py:20
  83.6 0.7 slice_bitcast_fusion
  84.3 0.6 slice_reduce_fusion
  (5 shorter events, 0.0 us)
Async XLA Ops:
  2.3 14.6 %collective-permute-start = (f32[32,2176]{1,0:T(8,128)S(1)}, f32[32,2176]{1,0:T(8,128)S(1)}, u32[]{:S(2)}, u32[]{:S(2)}) collective-permute-start(f32[32,2176]{1,0:T(8,128)S(1)} %pad_maximum_fusion), channel_id=1, source_target_pairs={{0,16},{16,32},{32,48},{48,64},{64,80},{80,96},{96,112},{112,128},... | collective-permute-start | bytes 835592 | tf_op jit(solution)/shard_map/ppermute | solution.py:20
  17.8 8.4 %copy-start.6 = (s32[1,1,16,2]{2,3,1,0:T(2,128)S(1)}, s32[1,1,16,2]{2,3,1,0:T(2,128)}, u32[]{:S(2)}) copy-start(s32[1,1,16,2]{2,3,1,0:T(2,128)} %param.17) | copy-start | bytes 388
  18.5 22.2 %copy-start = (f32[1,1,16,2,128,128]{5,4,3,2,1,0:T(8,128)S(1)}, f32[1,1,16,2,128,128]{5,4,3,2,1,0:T(8,128)}, u32[]{:S(2)}) copy-start(f32[1,1,16,2,128,128]{5,4,3,2,1,0:T(8,128)} %param.16) | copy-start | bytes 6291460
  18.5 22.2 %copy-start.1 = (f32[1,1,2048]{2,1,0:T(1,128)S(1)}, f32[1,1,2048]{2,1,0:T(1,128)}, u32[]{:S(2)}) copy-start(f32[1,1,2048]{2,1,0:T(1,128)} %param.11) | copy-start | bytes 24580
  18.6 22.2 %copy-start.2 = (f32[1,1,2048]{2,1,0:T(1,128)S(1)}, f32[1,1,2048]{2,1,0:T(1,128)}, u32[]{:S(2)}) copy-start(f32[1,1,2048]{2,1,0:T(1,128)} %param.12) | copy-start | bytes 24580
  18.6 22.2 %copy-start.3 = (f32[1,1,2048]{2,1,0:T(1,128)S(1)}, f32[1,1,2048]{2,1,0:T(1,128)}, u32[]{:S(2)}) copy-start(f32[1,1,2048]{2,1,0:T(1,128)} %param.13) | copy-start | bytes 24580
  18.6 22.2 %copy-start.4 = (f32[1,1,2048]{2,1,0:T(1,128)S(1)}, f32[1,1,2048]{2,1,0:T(1,128)}, u32[]{:S(2)}) copy-start(f32[1,1,2048]{2,1,0:T(1,128)} %param.14) | copy-start | bytes 24580
  18.6 22.2 %copy-start.5 = (f32[1,1,2048]{2,1,0:T(1,128)S(1)}, f32[1,1,2048]{2,1,0:T(1,128)}, u32[]{:S(2)}) copy-start(f32[1,1,2048]{2,1,0:T(1,128)} %param.15) | copy-start | bytes 24580
  19.5 21.0 %all-to-all-start = ((f32[16,4,2048]{2,1,0:T(4,128)}), f32[16,4,2048]{2,1,0:T(4,128)S(1)}, u32[]{:S(2)}, u32[]{:S(2)}) async-start(f32[16,4,2048]{2,1,0:T(4,128)} %reshape.52), calls=%async_computation | async-start | bytes 1048576 | tf_op jit(solution)/shard_map/all_to_all | solution.py:147
  47.5 21.2 %all-to-all-start.1 = ((f32[16,4,2176]{2,1,0:T(4,128)}), f32[16,4,2176]{2,1,0:T(4,128)S(1)}, u32[]{:S(2)}, u32[]{:S(2)}) async-start(f32[16,4,2176]{2,1,0:T(4,128)} %reshape.54), calls=%async_computation.1 | async-start | bytes 1114112 | tf_op jit(solution)/shard_map/all_to_all | solution.py:151
  69.6 14.0 %collective-permute-start.1 = (f32[32,2176]{1,0:T(8,128)S(1)}, f32[32,2176]{1,0:T(8,128)S(1)}, u32[]{:S(2)}, u32[]{:S(2)}) collective-permute-start(f32[32,2176]{1,0:T(8,128)S(1)} %gather_fusion.1), channel_id=1, source_target_pairs={{0,496},{16,0},{32,16},{48,32},{64,48},{80,64},{96,80},{112,96},{1... | collective-permute-start | bytes 835592 | tf_op jit(solution)/shard_map/ppermute | solution.py:20

commit v6 on v5

--- a/solution.py
+++ b/solution.py
@@ -97,12 +97,13 @@
         value = value + jnp.sum(term, axis=1, keepdims=True)
         pn = p_s[n]
         cross = cross + jnp.sum(pn * rows, axis=1, keepdims=True)
-        out_ref[:, s] = pn
+        out_ref[:, :, s] = pn.reshape(out_ref.shape[0], out_ref.shape[1], BS)
     icpt = (value - cross) / width
-    out_ref[:, width:] = jnp.broadcast_to(icpt, (rows_n, BS))
+    out_ref[:, :, width:] = jnp.broadcast_to(icpt, (rows_n, BS)).reshape(out_ref.shape[0], out_ref.shape[1], BS)
 
 
-def solve_block(rows, inflow, unit_cost, curvature, target, release_cap, block_values, block_cols):
+def solve_block(rows, inflow, unit_cost, curvature, target, release_cap, block_values, block_cols,
+                groups):
     count, width = rows.shape
     nblk, kblk = block_values.shape[0], block_values.shape[1]
     vec = lambda a: a.reshape(1, width)
@@ -114,7 +115,7 @@
     flops = 2 * count * nblk * kblk * BS * BS * (2 * ITERS) * 3
     return pl.pallas_call(
         functools.partial(solve_kernel, nblk, kblk),
-        out_shape=jax.ShapeDtypeStruct((count, width + BS), jnp.float32),
+        out_shape=jax.ShapeDtypeStruct((groups, count // groups, width + BS), jnp.float32),
         in_specs=[pl.BlockSpec(memory_space=pltpu.SMEM)] + [vspec] * 7,
         out_specs=vspec,
         scratch_shapes=scratch,
@@ -143,13 +144,13 @@
     slot_ids = dest * capacity + ranked
     hit = slot_ids[None, :] == jnp.arange(slots, dtype=jnp.int32)[:, None]
     source = jnp.sum(jnp.where(hit, jnp.arange(tr_rows, dtype=jnp.int32)[None, :], 0), axis=1)
-    packed = jnp.take(rows, source, axis=0, mode="clip")
-    arrived = lax.all_to_all(packed.reshape(states, capacity, width), "markov", 0, 0, tiled=True)
+    packed = jnp.take(rows, source.reshape(states, capacity), axis=0, mode="clip")
+    arrived = lax.all_to_all(packed, "markov", 0, 0, tiled=True)
     solved = solve_block(arrived.reshape(slots, width), inflow.reshape(width),
                          unit_cost.reshape(width), curvature.reshape(width), target.reshape(width),
-                         release_cap.reshape(width), block_values[0, 0], block_cols[0, 0])
-    back = lax.all_to_all(solved.reshape(states, capacity, -1), "markov", 0, 0, tiled=True)
-    mine = jnp.take(back.reshape(slots, -1), slot_ids, axis=0, mode="clip")
+                         release_cap.reshape(width), block_values[0, 0], block_cols[0, 0], states)
+    back = lax.all_to_all(solved, "markov", 0, 0, tiled=True)
+    mine = back.at[dest, ranked].get(mode="clip")
     mine = shifted(mine, "week", -1)
     return (mine[:, :width].reshape(1, 1, tr_rows, width),
             mine[:, width].reshape(1, 1, tr_rows))

time: 85.3 us -> 85.1 us (level)
  blocking collectives: 0 us -> 19.6 us
  waiting for transfers between devices: 47.6 us -> 31.2 us
  starting transfers between devices: 22.9 us -> 20.3 us
    all_to_all x0 -> x1, blocking collectives: none -> 19.6 us  [on_device(): back = lax.all_to_all(solved, 'markov', 0, 0, tiled=True)]
    all_to_all x2 -> x1, waiting for transfers between devices: 31.8 us -> 14.2 us  [on_device(): arrived = lax.all_to_all(packed, 'markov', 0, 0, tiled=True)]
    all_to_all x2 -> x1, starting transfers between devices: 10.1 us -> 6.57 us  [on_device(): arrived = lax.all_to_all(packed, 'markov', 0, 0, tiled=True)]
    reshape x3 -> x0, local copies, waits for them, and re-layouts: 2.07 us -> none  [the longest x1 0.95 us: on_device(): solved.reshape(states, capacity, -1)]
    gather x2 -> x3, local copies, waits for them, and re-layouts: 1.43 us -> 2.68 us  [the longest x2 1.69 us: on_device(): jnp.take(rows, source.reshape(states, capacity), axis=0, mode='clip')]
    ppermute x2, waiting for transfers between devices: 15.8 us -> 17 us  [shifted(): return lax.ppermute(value, axis, pairs)]
    ppermute x2, starting transfers between devices: 12.8 us -> 13.7 us  [shifted(): return lax.ppermute(value, axis, pairs)]
  transfers between devices with their start and end apart: 4 -> 3, of which waited for: 4 -> 3; matrix products, arithmetic and copies ran while one was open for 0% -> 0% of each run, Pallas kernels for 0% -> 0%
where the time goes in v6:
time: 85.1 us; the launch traced here: 84.8 us
  waiting for transfers between devices  31.2 us (37%)
  starting transfers between devices  20.3 us (24%)
  blocking collectives  19.6 us (23%)
  Pallas kernels  5.87 us (7%)
  local copies, waits for them, and re-layouts  4.69 us (6%)
  other arithmetic  2.28 us (3%)
    all_to_all x1, blocking collectives, on_device(): back = lax.all_to_all(solved, 'markov', 0, 0, tiled=True)  19.6 us
    ppermute x2, waiting for transfers between devices, shifted(): return lax.ppermute(value, axis, pairs)  17 us
    all_to_all x1, waiting for transfers between devices, on_device(): arrived = lax.all_to_all(packed, 'markov', 0, 0, tiled=True)  14.2 us
    ppermute x2, starting transfers between devices, shifted(): return lax.ppermute(value, axis, pairs)  13.7 us
    all_to_all x1, starting transfers between devices, on_device(): arrived = lax.all_to_all(packed, 'markov', 0, 0, tiled=True)  6.57 us
    pallas_call x1, Pallas kernels, solve_block(): pl.pallas_call(functools.partial(solve_kernel, nblk, kblk), out_shape=jax...  5.87 us
  transfers between devices with their start and end apart: 3, of which 3 were waited for; matrix products, arithmetic and copies ran while one was open for 0% of the time, Pallas kernels for 0%

profile of v6, /device:TPU:57, one launch (start us, length us, event | category | flops | bytes accessed | tf_op | source)
XLA Modules:
  0.0 84.8 jit_solution(10781408082156775819)
XLA Ops:
  0.6 0.7 convert_bitcast_fusion
  1.3 0.1 broadcast_in_dim.17
  1.4 1.0 %pad_maximum_fusion = f32[32,2176]{1,0:T(8,128)S(1)} fusion(f32[32,128]{1,0:T(8,128)S(1)} %broadcast_in_dim.17, f32[32,2048]{1,0:T(8,128)} %bitcast.24), kind=kLoop, calls=%fused_computation.2 | loop fusion | flops 69632 | bytes 557056 | tf_op jit(solution)/shard_map/concatenate | solution.py:140
  2.3 10.4 %collective-permute-start = (f32[32,2176]{1,0:T(8,128)S(1)}, f32[32,2176]{1,0:T(8,128)S(1)}, u32[]{:S(2)}, u32[]{:S(2)}) collective-permute-start(f32[32,2176]{1,0:T(8,128)S(1)} %pad_maximum_fusion), channel_id=1, source_target_pairs={{0,16},{16,32},{32,48},{48,64},{64,80},{80,96},{96,112},{112,128},... | collective-permute-start | bytes 835592 | tf_op jit(solution)/shard_map/ppermute | solution.py:20
  12.7 4.2 %collective-permute-done = f32[32,2176]{1,0:T(8,128)S(1)} collective-permute-done((f32[32,2176]{1,0:T(8,128)S(1)}, f32[32,2176]{1,0:T(8,128)S(1)}, u32[]{:S(2)}, u32[]{:S(2)}) %collective-permute-start) | collective-permute-done | bytes 278560 | tf_op jit(solution)/shard_map/ppermute | solution.py:20
  17.0 0.1 fusion.7
  17.1 0.1 fusion.6
  17.2 0.1 reduce_window_sum.11
  17.2 0.2 select_reduce_fusion.1
  17.4 0.1 copy.20
  17.5 0.1 copy.21
  17.6 0.1 fusion.3
  17.7 0.1 select_reduce_fusion
  17.8 0.0 copy-start.6
  17.9 0.8 gather_fusion
  18.6 0.0 copy-start
  18.6 0.0 copy-start.1
  18.6 0.0 copy-start.2
  18.7 0.0 copy-start.3
  18.7 0.0 copy-start.4
  18.7 0.0 copy-start.5
  18.7 0.9 %reshape.59 = f32[16,4,2048]{2,1,0:T(4,128)} reshape(f32[64,2048]{1,0:T(8,128)S(1)} %gather_fusion) | data formatting | bytes 1048576 | tf_op jit(solution)/shard_map/jit(_take)/gather | solution.py:147
  19.6 6.6 %all-to-all-start = ((f32[16,4,2048]{2,1,0:T(4,128)}), f32[16,4,2048]{2,1,0:T(4,128)S(1)}, u32[]{:S(2)}, u32[]{:S(2)}) async-start(f32[16,4,2048]{2,1,0:T(4,128)} %reshape.59), calls=%async_computation | async-start | bytes 1048576 | tf_op jit(solution)/shard_map/all_to_all | solution.py:148
  26.2 0.0 copy-done.6
  26.2 0.1 copy.19
  26.3 0.1 reshape_squeeze.6.cols_ref
  26.4 14.2 %all-to-all-done = f32[16,4,2048]{2,1,0:T(4,128)S(1)} async-done(((f32[16,4,2048]{2,1,0:T(4,128)}), f32[16,4,2048]{2,1,0:T(4,128)S(1)}, u32[]{:S(2)}, u32[]{:S(2)}) %all-to-all-start) | async-done | bytes 524320 | tf_op jit(solution)/shard_map/all_to_all | solution.py:148
  40.6 0.2 reshape.56.rows_ref
  40.8 0.0 copy-done
  40.8 0.0 copy-done.1
  40.8 0.0 copy-done.2
  40.8 0.0 copy-done.3
  40.8 0.0 copy-done.4
  40.8 0.0 copy-done.5
  40.8 5.9 %sddp_solve.1 = f32[16,4,2176]{2,1,0:T(4,128)S(1)} custom-call(s32[32]{0:T(128)S(1)} %reshape_squeeze.6.cols_ref, f32[64,2048]{1,0:T(8,128)S(1)} %reshape.56.rows_ref, f32[1,2048]{1,0:T(1,128)S(1)} %bitcast.19, f32[1,2048]{1,0:T(1,128)S(1)} %bitcast.20, f32[1,2048]{1,0:T(1,128)S(1)} %bitcast.21, f32[1,2048]{1,0:T(1,128)S(1)} %bitcast.22, ...), custom_call_target="tpu_custom_call" | custom-call | flops 1610612736 | bytes 3670016 | tf_op jit(solution)/shard_map/sddp_solve/pallas_call | solution.py:116
  46.7 19.6 %all_to_all.10 = f32[16,4,2176]{2,1,0:T(4,128)S(1)} all-to-all(f32[16,4,2176]{2,1,0:T(4,128)S(1)} %sddp_solve.1), channel_id=1, replica_groups=mesh['week'=32,'markov'=16] {'markov'}, dimensions={0} | all-to-all | bytes 1114112 | tf_op jit(solution)/shard_map/all_to_all | solution.py:152
  66.3 1.0 %gather_fusion.1 = f32[32,2176]{1,0:T(8,128)S(1)} fusion(f32[16,4,2176]{2,1,0:T(4,128)S(1)} %all_to_all.10, s32[32]{0:T(128)S(1)} %get-tuple-element.2), kind=kCustom, calls=%fused_computation.1 | custom fusion | bytes 557312 | tf_op jit(solution)/shard_map/gather | solution.py:153
  67.3 3.3 %collective-permute-start.1 = (f32[32,2176]{1,0:T(8,128)S(1)}, f32[32,2176]{1,0:T(8,128)S(1)}, u32[]{:S(2)}, u32[]{:S(2)}) collective-permute-start(f32[32,2176]{1,0:T(8,128)S(1)} %gather_fusion.1), channel_id=1, source_target_pairs={{0,496},{16,0},{32,16},{48,32},{64,48},{80,64},{96,80},{112,96},{1... | collective-permute-start | bytes 835592 | tf_op jit(solution)/shard_map/ppermute | solution.py:20
  70.6 12.8 %collective-permute-done.1 = f32[32,2176]{1,0:T(8,128)S(1)} collective-permute-done((f32[32,2176]{1,0:T(8,128)S(1)}, f32[32,2176]{1,0:T(8,128)S(1)}, u32[]{:S(2)}, u32[]{:S(2)}) %collective-permute-start.1) | collective-permute-done | bytes 278560 | tf_op jit(solution)/shard_map/ppermute | solution.py:20
  83.4 0.6 slice_reduce_fusion
  84.0 0.7 slice_bitcast_fusion
  (4 shorter events, 0.0 us)
Async XLA Ops:
  2.3 14.6 %collective-permute-start = (f32[32,2176]{1,0:T(8,128)S(1)}, f32[32,2176]{1,0:T(8,128)S(1)}, u32[]{:S(2)}, u32[]{:S(2)}) collective-permute-start(f32[32,2176]{1,0:T(8,128)S(1)} %pad_maximum_fusion), channel_id=1, source_target_pairs={{0,16},{16,32},{32,48},{48,64},{64,80},{80,96},{96,112},{112,128},... | collective-permute-start | bytes 835592 | tf_op jit(solution)/shard_map/ppermute | solution.py:20
  17.8 8.4 %copy-start.6 = (s32[1,1,16,2]{2,3,1,0:T(2,128)S(1)}, s32[1,1,16,2]{2,3,1,0:T(2,128)}, u32[]{:S(2)}) copy-start(s32[1,1,16,2]{2,3,1,0:T(2,128)} %param.17) | copy-start | bytes 388
  18.6 22.2 %copy-start = (f32[1,1,16,2,128,128]{5,4,3,2,1,0:T(8,128)S(1)}, f32[1,1,16,2,128,128]{5,4,3,2,1,0:T(8,128)}, u32[]{:S(2)}) copy-start(f32[1,1,16,2,128,128]{5,4,3,2,1,0:T(8,128)} %param.16) | copy-start | bytes 6291460
  18.6 22.2 %copy-start.1 = (f32[1,1,2048]{2,1,0:T(1,128)S(1)}, f32[1,1,2048]{2,1,0:T(1,128)}, u32[]{:S(2)}) copy-start(f32[1,1,2048]{2,1,0:T(1,128)} %param.11) | copy-start | bytes 24580
  18.6 22.2 %copy-start.2 = (f32[1,1,2048]{2,1,0:T(1,128)S(1)}, f32[1,1,2048]{2,1,0:T(1,128)}, u32[]{:S(2)}) copy-start(f32[1,1,2048]{2,1,0:T(1,128)} %param.12) | copy-start | bytes 24580
  18.7 22.2 %copy-start.3 = (f32[1,1,2048]{2,1,0:T(1,128)S(1)}, f32[1,1,2048]{2,1,0:T(1,128)}, u32[]{:S(2)}) copy-start(f32[1,1,2048]{2,1,0:T(1,128)} %param.13) | copy-start | bytes 24580
  18.7 22.2 %copy-start.4 = (f32[1,1,2048]{2,1,0:T(1,128)S(1)}, f32[1,1,2048]{2,1,0:T(1,128)}, u32[]{:S(2)}) copy-start(f32[1,1,2048]{2,1,0:T(1,128)} %param.14) | copy-start | bytes 24580
  18.7 22.2 %copy-start.5 = (f32[1,1,2048]{2,1,0:T(1,128)S(1)}, f32[1,1,2048]{2,1,0:T(1,128)}, u32[]{:S(2)}) copy-start(f32[1,1,2048]{2,1,0:T(1,128)} %param.15) | copy-start | bytes 24580
  19.6 21.0 %all-to-all-start = ((f32[16,4,2048]{2,1,0:T(4,128)}), f32[16,4,2048]{2,1,0:T(4,128)S(1)}, u32[]{:S(2)}, u32[]{:S(2)}) async-start(f32[16,4,2048]{2,1,0:T(4,128)} %reshape.59), calls=%async_computation | async-start | bytes 1048576 | tf_op jit(solution)/shard_map/all_to_all | solution.py:148
  67.3 16.1 %collective-permute-start.1 = (f32[32,2176]{1,0:T(8,128)S(1)}, f32[32,2176]{1,0:T(8,128)S(1)}, u32[]{:S(2)}, u32[]{:S(2)}) collective-permute-start(f32[32,2176]{1,0:T(8,128)S(1)} %gather_fusion.1), channel_id=1, source_target_pairs={{0,496},{16,0},{32,16},{48,32},{64,48},{80,64},{96,80},{112,96},{1... | collective-permute-start | bytes 835592 | tf_op jit(solution)/shard_map/ppermute | solution.py:20

commit v7 on v6

--- a/solution.py
+++ b/solution.py
@@ -136,9 +136,7 @@
     slots = states * capacity
     own_rows = trial_states.reshape(tr_rows, width)
     own_dest = successor.reshape(tr_rows)
-    tag = jnp.broadcast_to(own_dest.astype(jnp.float32)[:, None], (tr_rows, BS))
-    sent = shifted(jnp.concatenate([own_rows, tag], axis=1), "week", 1)
-    rows, dest = sent[:, :width], sent[:, width].astype(jnp.int32)
+    rows, dest = shifted((own_rows, own_dest), "week", 1)
     marked = (dest[:, None] == jnp.arange(states, dtype=jnp.int32)[None, :]).astype(jnp.int32)
     ranked = jnp.sum(jnp.cumsum(marked, axis=0) * marked, axis=1) - 1
     slot_ids = dest * capacity + ranked

time: 85.1 us -> 85.8 us (level)
  blocking collectives: 19.6 us -> 0 us
  waiting for transfers between devices: 31.2 us -> 47.8 us
  starting transfers between devices: 20.3 us -> 25.2 us
  other arithmetic: 2.28 us -> 0.42 us
    all_to_all x1 -> x0, blocking collectives: 19.6 us -> none  [on_device(): back = lax.all_to_all(solved, 'markov', 0, 0, tiled=True)]
    all_to_all x0 -> x1, waiting for transfers between devices: none -> 17.4 us  [on_device(): back = lax.all_to_all(solved, 'markov', 0, 0, tiled=True)]
    all_to_all x0 -> x1, starting transfers between devices: none -> 3.58 us  [on_device(): back = lax.all_to_all(solved, 'markov', 0, 0, tiled=True)]
    ppermute x2 -> x3, waiting for transfers between devices: 17 us -> 15.3 us  [shifted(): return lax.ppermute(value, axis, pairs)]
    ppermute x2 -> x3, starting transfers between devices: 13.7 us -> 15 us  [shifted(): return lax.ppermute(value, axis, pairs)]
    concatenate x1 -> x0, other arithmetic: 0.97 us -> none  [on_device(): sent = shifted(jnp.concatenate([own_rows, tag], axis=1), 'week', 1)]
    all_to_all x1, waiting for transfers between devices: 14.2 us -> 15.2 us  [on_device(): arrived = lax.all_to_all(packed, 'markov', 0, 0, tiled=True)]
  transfers between devices with their start and end apart: 3 -> 5, of which waited for: 3 -> 4; matrix products, arithmetic and copies ran while one was open for 0% -> 1% of each run, Pallas kernels for 0% -> 0%
where the time goes in v7:
time: 85.8 us; the launch traced here: 85.4 us
  waiting for transfers between devices  47.8 us (56%)
  starting transfers between devices  25.2 us (29%)
  Pallas kernels  6.71 us (8%)
  local copies, waits for them, and re-layouts  4.42 us (5%)
    all_to_all x1, waiting for transfers between devices, on_device(): back = lax.all_to_all(solved, 'markov', 0, 0, tiled=True)  17.4 us
    ppermute x3, waiting for transfers between devices, shifted(): return lax.ppermute(value, axis, pairs)  15.3 us
    all_to_all x1, waiting for transfers between devices, on_device(): arrived = lax.all_to_all(packed, 'markov', 0, 0, tiled=True)  15.2 us
    ppermute x3, starting transfers between devices, shifted(): return lax.ppermute(value, axis, pairs)  15 us
    pallas_call x1, Pallas kernels, solve_block(): pl.pallas_call(functools.partial(solve_kernel, nblk, kblk), out_shape=jax...  6.71 us
    all_to_all x1, starting transfers between devices, on_device(): arrived = lax.all_to_all(packed, 'markov', 0, 0, tiled=True)  6.65 us
    all_to_all x1, starting transfers between devices, on_device(): back = lax.all_to_all(solved, 'markov', 0, 0, tiled=True)  3.58 us
  transfers between devices with their start and end apart: 5, of which 4 were waited for; matrix products, arithmetic and copies ran while one was open for 1% of the time, Pallas kernels for 0%

profile of v7, /device:TPU:57, one launch (start us, length us, event | category | flops | bytes accessed | tf_op | source)
XLA Modules:
  0.0 85.4 jit_solution(13979662373026786130)
XLA Ops:
  0.6 10.4 %collective-permute-start.1 = (s32[32]{0:T(128)}, s32[32]{0:T(128)S(1)}, u32[]{:S(2)}, u32[]{:S(2)}) collective-permute-start(s32[32]{0:T(128)} %bitcast.41), channel_id=1, source_target_pairs={{0,16},{16,32},{32,48},{48,64},{64,80},{80,96},{96,112},{112,128},... | collective-permute-start | bytes 392 | tf_op jit(solution)/shard_map/ppermute | solution.py:20
  11.0 1.9 %collective-permute-start = (f32[32,2048]{1,0:T(8,128)}, f32[32,2048]{1,0:T(8,128)S(1)}, u32[]{:S(2)}, u32[]{:S(2)}) collective-permute-start(f32[32,2048]{1,0:T(8,128)} %bitcast.40), channel_id=1, source_target_pairs={{0,16},{16,32},{32,48},{48,64},{64,80},{80,96},{96,112},{112,128},... | collective-permute-start | bytes 786440 | tf_op jit(solution)/shard_map/ppermute | solution.py:20
  13.0 0.0 collective-permute-done.1
  13.0 0.1 fusion
  13.0 0.1 reduce_window_sum.11
  13.1 0.2 select_reduce_fusion.1
  13.3 0.1 select_reduce_fusion
  13.4 3.8 %collective-permute-done = f32[32,2048]{1,0:T(8,128)S(1)} collective-permute-done((f32[32,2048]{1,0:T(8,128)}, f32[32,2048]{1,0:T(8,128)S(1)}, u32[]{:S(2)}, u32[]{:S(2)}) %collective-permute-start) | collective-permute-done | bytes 262176 | tf_op jit(solution)/shard_map/ppermute | solution.py:20
  17.2 0.0 copy-start.6
  17.2 0.8 gather_fusion
  17.9 0.0 copy-start
  17.9 0.0 copy-start.1
  17.9 0.0 copy-start.2
  18.0 0.0 copy-start.3
  18.0 0.0 copy-start.4
  18.0 0.0 copy-start.5
  18.0 0.9 %reshape.45 = f32[16,4,2048]{2,1,0:T(4,128)} reshape(f32[64,2048]{1,0:T(8,128)S(1)} %gather_fusion) | data formatting | bytes 1048576 | tf_op jit(solution)/shard_map/jit(_take)/gather | solution.py:145
  18.9 6.7 %all-to-all-start = ((f32[16,4,2048]{2,1,0:T(4,128)}), f32[16,4,2048]{2,1,0:T(4,128)S(1)}, u32[]{:S(2)}, u32[]{:S(2)}) async-start(f32[16,4,2048]{2,1,0:T(4,128)} %reshape.45), calls=%async_computation | async-start | bytes 1048576 | tf_op jit(solution)/shard_map/all_to_all | solution.py:146
  25.6 0.0 copy-done.6
  25.6 0.1 copy.13
  25.7 0.1 reshape_squeeze.6.cols_ref
  25.8 15.2 %all-to-all-done = f32[16,4,2048]{2,1,0:T(4,128)S(1)} async-done(((f32[16,4,2048]{2,1,0:T(4,128)}), f32[16,4,2048]{2,1,0:T(4,128)S(1)}, u32[]{:S(2)}, u32[]{:S(2)}) %all-to-all-start) | async-done | bytes 524320 | tf_op jit(solution)/shard_map/all_to_all | solution.py:146
  41.0 0.2 reshape.42.rows_ref
  41.1 0.0 copy-done
  41.2 0.0 copy-done.1
  41.2 0.0 copy-done.2
  41.2 0.0 copy-done.3
  41.2 0.0 copy-done.4
  41.2 0.0 copy-done.5
  41.2 6.7 %sddp_solve.1 = f32[16,4,2176]{2,1,0:T(4,128)} custom-call(s32[32]{0:T(128)S(1)} %reshape_squeeze.6.cols_ref, f32[64,2048]{1,0:T(8,128)S(1)} %reshape.42.rows_ref, f32[1,2048]{1,0:T(1,128)S(1)} %bitcast.34, f32[1,2048]{1,0:T(1,128)S(1)} %bitcast.35, f32[1,2048]{1,0:T(1,128)S(1)} %bitcast.36, f32[1,2048]{1,0:T(1,128)S(1)} %bitcast.37, ...), custom_call_target="tpu_custom_call" | custom-call | flops 1610612736 | bytes 3670016 | tf_op jit(solution)/shard_map/sddp_solve/pallas_call | solution.py:116
  47.9 3.6 %all-to-all-start.1 = ((f32[16,4,2176]{2,1,0:T(4,128)}), f32[16,4,2176]{2,1,0:T(4,128)S(1)}, u32[]{:S(2)}, u32[]{:S(2)}) async-start(f32[16,4,2176]{2,1,0:T(4,128)} %sddp_solve.1), calls=%async_computation.1 | async-start | bytes 1114112 | tf_op jit(solution)/shard_map/all_to_all | solution.py:150
  51.5 17.4 %all-to-all-done.1 = f32[16,4,2176]{2,1,0:T(4,128)S(1)} async-done(((f32[16,4,2176]{2,1,0:T(4,128)}), f32[16,4,2176]{2,1,0:T(4,128)S(1)}, u32[]{:S(2)}, u32[]{:S(2)}) %all-to-all-start.1) | async-done | bytes 557088 | tf_op jit(solution)/shard_map/all_to_all | solution.py:150
  68.9 1.0 %gather_fusion.1 = f32[32,2176]{1,0:T(8,128)S(1)} fusion(f32[16,4,2176]{2,1,0:T(4,128)S(1)} %all-to-all-done.1, s32[32]{0:T(128)S(1)} %fusion.6), kind=kCustom, calls=%fused_computation.1 | custom fusion | bytes 557312 | tf_op jit(solution)/shard_map/gather | solution.py:151
  69.9 2.6 %collective-permute-start.2 = (f32[32,2176]{1,0:T(8,128)S(1)}, f32[32,2176]{1,0:T(8,128)S(1)}, u32[]{:S(2)}, u32[]{:S(2)}) collective-permute-start(f32[32,2176]{1,0:T(8,128)S(1)} %gather_fusion.1), channel_id=1, source_target_pairs={{0,496},{16,0},{32,16},{48,32},{64,48},{80,64},{96,80},{112,96},{1... | collective-permute-start | bytes 835592 | tf_op jit(solution)/shard_map/ppermute | solution.py:20
  72.5 11.5 %collective-permute-done.2 = f32[32,2176]{1,0:T(8,128)S(1)} collective-permute-done((f32[32,2176]{1,0:T(8,128)S(1)}, f32[32,2176]{1,0:T(8,128)S(1)}, u32[]{:S(2)}, u32[]{:S(2)}) %collective-permute-start.2) | collective-permute-done | bytes 278560 | tf_op jit(solution)/shard_map/ppermute | solution.py:20
  84.1 0.6 slice_reduce_fusion
  84.7 0.7 slice_bitcast_fusion
  (3 shorter events, 0.0 us)
Async XLA Ops:
  0.6 12.3 %collective-permute-start.1 = (s32[32]{0:T(128)}, s32[32]{0:T(128)S(1)}, u32[]{:S(2)}, u32[]{:S(2)}) collective-permute-start(s32[32]{0:T(128)} %bitcast.41), channel_id=1, source_target_pairs={{0,16},{16,32},{32,48},{48,64},{64,80},{80,96},{96,112},{112,128},... | collective-permute-start | bytes 392 | tf_op jit(solution)/shard_map/ppermute | solution.py:20
  11.0 6.1 %collective-permute-start = (f32[32,2048]{1,0:T(8,128)}, f32[32,2048]{1,0:T(8,128)S(1)}, u32[]{:S(2)}, u32[]{:S(2)}) collective-permute-start(f32[32,2048]{1,0:T(8,128)} %bitcast.40), channel_id=1, source_target_pairs={{0,16},{16,32},{32,48},{48,64},{64,80},{80,96},{96,112},{112,128},... | collective-permute-start | bytes 786440 | tf_op jit(solution)/shard_map/ppermute | solution.py:20
  17.2 8.4 %copy-start.6 = (s32[1,1,16,2]{2,3,1,0:T(2,128)S(1)}, s32[1,1,16,2]{2,3,1,0:T(2,128)}, u32[]{:S(2)}) copy-start(s32[1,1,16,2]{2,3,1,0:T(2,128)} %param.17) | copy-start | bytes 388
  17.9 23.2 %copy-start = (f32[1,1,16,2,128,128]{5,4,3,2,1,0:T(8,128)S(1)}, f32[1,1,16,2,128,128]{5,4,3,2,1,0:T(8,128)}, u32[]{:S(2)}) copy-start(f32[1,1,16,2,128,128]{5,4,3,2,1,0:T(8,128)} %param.16) | copy-start | bytes 6291460
  17.9 23.2 %copy-start.1 = (f32[1,1,2048]{2,1,0:T(1,128)S(1)}, f32[1,1,2048]{2,1,0:T(1,128)}, u32[]{:S(2)}) copy-start(f32[1,1,2048]{2,1,0:T(1,128)} %param.11) | copy-start | bytes 24580
  17.9 23.2 %copy-start.2 = (f32[1,1,2048]{2,1,0:T(1,128)S(1)}, f32[1,1,2048]{2,1,0:T(1,128)}, u32[]{:S(2)}) copy-start(f32[1,1,2048]{2,1,0:T(1,128)} %param.12) | copy-start | bytes 24580
  18.0 23.2 %copy-start.3 = (f32[1,1,2048]{2,1,0:T(1,128)S(1)}, f32[1,1,2048]{2,1,0:T(1,128)}, u32[]{:S(2)}) copy-start(f32[1,1,2048]{2,1,0:T(1,128)} %param.13) | copy-start | bytes 24580
  18.0 23.2 %copy-start.4 = (f32[1,1,2048]{2,1,0:T(1,128)S(1)}, f32[1,1,2048]{2,1,0:T(1,128)}, u32[]{:S(2)}) copy-start(f32[1,1,2048]{2,1,0:T(1,128)} %param.14) | copy-start | bytes 24580
  18.0 23.2 %copy-start.5 = (f32[1,1,2048]{2,1,0:T(1,128)S(1)}, f32[1,1,2048]{2,1,0:T(1,128)}, u32[]{:S(2)}) copy-start(f32[1,1,2048]{2,1,0:T(1,128)} %param.15) | copy-start | bytes 24580
  18.9 22.0 %all-to-all-start = ((f32[16,4,2048]{2,1,0:T(4,128)}), f32[16,4,2048]{2,1,0:T(4,128)S(1)}, u32[]{:S(2)}, u32[]{:S(2)}) async-start(f32[16,4,2048]{2,1,0:T(4,128)} %reshape.45), calls=%async_computation | async-start | bytes 1048576 | tf_op jit(solution)/shard_map/all_to_all | solution.py:146
  47.9 21.0 %all-to-all-start.1 = ((f32[16,4,2176]{2,1,0:T(4,128)}), f32[16,4,2176]{2,1,0:T(4,128)S(1)}, u32[]{:S(2)}, u32[]{:S(2)}) async-start(f32[16,4,2176]{2,1,0:T(4,128)} %sddp_solve.1), calls=%async_computation.1 | async-start | bytes 1114112 | tf_op jit(solution)/shard_map/all_to_all | solution.py:150
  69.9 14.2 %collective-permute-start.2 = (f32[32,2176]{1,0:T(8,128)S(1)}, f32[32,2176]{1,0:T(8,128)S(1)}, u32[]{:S(2)}, u32[]{:S(2)}) collective-permute-start(f32[32,2176]{1,0:T(8,128)S(1)} %gather_fusion.1), channel_id=1, source_target_pairs={{0,496},{16,0},{32,16},{48,32},{64,48},{80,64},{96,80},{112,96},{1... | collective-permute-start | bytes 835592 | tf_op jit(solution)/shard_map/ppermute | solution.py:20

commit v8 on v6

--- a/solution.py
+++ b/solution.py
@@ -127,6 +127,25 @@
       vec(release_cap), block_values)
 
 
+def pack_kernel(states, capacity, source_ref, rows_ref, out_ref):
+    for i in range(states):
+        for j in range(capacity):
+            src = source_ref[i * capacity + j]
+            out_ref[i, pl.ds(j, 1), :] = rows_ref[pl.ds(src, 1), :]
+
+
+def pack_slots(rows, source, states, capacity):
+    width = rows.shape[1]
+    return pl.pallas_call(
+        functools.partial(pack_kernel, states, capacity),
+        out_shape=jax.ShapeDtypeStruct((states, capacity, width), jnp.float32),
+        in_specs=[pl.BlockSpec(memory_space=pltpu.SMEM), pl.BlockSpec(memory_space=pltpu.VMEM)],
+        out_specs=pl.BlockSpec(memory_space=pltpu.VMEM),
+        cost_estimate=pl.CostEstimate(flops=0, transcendentals=0, bytes_accessed=12 * rows.size),
+        name="sddp_pack",
+    )(source, rows)
+
+
 def on_device(trial_states, successor, inflow, unit_cost, curvature, target, release_cap,
               block_values, block_cols):
     states = lax.axis_size("markov")
@@ -144,7 +163,7 @@
     slot_ids = dest * capacity + ranked
     hit = slot_ids[None, :] == jnp.arange(slots, dtype=jnp.int32)[:, None]
     source = jnp.sum(jnp.where(hit, jnp.arange(tr_rows, dtype=jnp.int32)[None, :], 0), axis=1)
-    packed = jnp.take(rows, source.reshape(states, capacity), axis=0, mode="clip")
+    packed = pack_slots(rows, source, states, capacity)
     arrived = lax.all_to_all(packed, "markov", 0, 0, tiled=True)
     solved = solve_block(arrived.reshape(slots, width), inflow.reshape(width),
                          unit_cost.reshape(width), curvature.reshape(width), target.reshape(width),

time: 85.1 us -> 86.7 us (1.019)
  Pallas kernels: 5.87 us -> 7.87 us
  local copies, waits for them, and re-layouts: 4.69 us -> 3.68 us
    pallas_call x0 -> x1, Pallas kernels: none -> 1.89 us  [pack_slots(): pl.pallas_call(functools.partial(pack_kernel, states, capacity), out_shap...]
    gather x2 -> x0, local copies, waits for them, and re-layouts: 1.69 us -> none  [on_device(): jnp.take(rows, source.reshape(states, capacity), axis=0, mode='clip')]
where the time goes in v8:
time: 86.7 us; the launch traced here: 86.3 us
  waiting for transfers between devices  31.2 us (36%)
  starting transfers between devices  20.3 us (23%)
  blocking collectives  19.6 us (23%)
  Pallas kernels  7.87 us (9%)
  local copies, waits for them, and re-layouts  3.68 us (4%)
  other arithmetic  2.92 us (3%)
    all_to_all x1, blocking collectives, on_device(): back = lax.all_to_all(solved, 'markov', 0, 0, tiled=True)  19.6 us
    ppermute x2, waiting for transfers between devices, shifted(): return lax.ppermute(value, axis, pairs)  17 us
    all_to_all x1, waiting for transfers between devices, on_device(): arrived = lax.all_to_all(packed, 'markov', 0, 0, tiled=True)  14.2 us
    ppermute x2, starting transfers between devices, shifted(): return lax.ppermute(value, axis, pairs)  13.7 us
    all_to_all x1, starting transfers between devices, on_device(): arrived = lax.all_to_all(packed, 'markov', 0, 0, tiled=True)  6.57 us
    pallas_call x1, Pallas kernels, solve_block(): pl.pallas_call(functools.partial(solve_kernel, nblk, kblk), out_shape=jax...  5.98 us
    pallas_call x1, Pallas kernels, pack_slots(): pl.pallas_call(functools.partial(pack_kernel, states, capacity), out_shap...  1.89 us
  transfers between devices with their start and end apart: 3, of which 3 were waited for; matrix products, arithmetic and copies ran while one was open for 0% of the time, Pallas kernels for 0%

profile of v8, /device:TPU:57, one launch (start us, length us, event | category | flops | bytes accessed | tf_op | source)
XLA Modules:
  0.0 86.3 jit_solution(4584159258751871562)
XLA Ops:
  0.6 0.0 copy-start.6
  0.6 0.7 convert_bitcast_fusion
  1.3 0.0 copy-start
  1.3 0.0 copy-start.1
  1.3 0.0 copy-start.2
  1.3 0.0 copy-start.3
  1.3 0.0 copy-start.4
  1.3 0.0 copy-start.5
  1.3 0.1 broadcast_in_dim.10
  1.4 1.1 %pad_maximum_fusion = f32[32,2176]{1,0:T(8,128)S(1)} fusion(f32[32,128]{1,0:T(8,128)S(1)} %broadcast_in_dim.10, f32[32,2048]{1,0:T(8,128)} %bitcast.24), kind=kLoop, calls=%fused_computation.1 | loop fusion | flops 69632 | bytes 557056 | tf_op jit(solution)/shard_map/concatenate | solution.py:159
  2.5 10.4 %collective-permute-start = (f32[32,2176]{1,0:T(8,128)S(1)}, f32[32,2176]{1,0:T(8,128)S(1)}, u32[]{:S(2)}, u32[]{:S(2)}) collective-permute-start(f32[32,2176]{1,0:T(8,128)S(1)} %pad_maximum_fusion), channel_id=1, source_target_pairs={{0,16},{16,32},{32,48},{48,64},{64,80},{80,96},{96,112},{112,128},... | collective-permute-start | bytes 835592 | tf_op jit(solution)/shard_map/ppermute | solution.py:20
  12.9 4.2 %collective-permute-done = f32[32,2176]{1,0:T(8,128)S(1)} collective-permute-done((f32[32,2176]{1,0:T(8,128)S(1)}, f32[32,2176]{1,0:T(8,128)S(1)}, u32[]{:S(2)}, u32[]{:S(2)}) %collective-permute-start) | collective-permute-done | bytes 278560 | tf_op jit(solution)/shard_map/ppermute | solution.py:20
  17.2 0.1 fusion.7
  17.3 0.1 fusion.6
  17.3 0.1 reduce_window_sum.11
  17.4 0.2 select_reduce_fusion.1
  17.6 0.1 copy.20
  17.7 0.1 copy.21
  17.8 0.1 fusion.3
  17.9 0.6 select_reduce_fusion.source_ref
  18.5 0.7 slice.19.rows_ref
  19.2 1.9 %sddp_pack.1 = f32[16,4,2048]{2,1,0:T(4,128)} custom-call(s32[64]{0:T(128)} %select_reduce_fusion.source_ref, f32[32,2048]{1,0:T(8,128)} %slice.19.rows_ref), custom_call_target="tpu_custom_call" | custom-call | bytes 786432 | tf_op jit(solution)/shard_map/sddp_pack/pallas_call | solution.py:139
  21.1 6.6 %all-to-all-start = ((f32[16,4,2048]{2,1,0:T(4,128)}), f32[16,4,2048]{2,1,0:T(4,128)S(1)}, u32[]{:S(2)}, u32[]{:S(2)}) async-start(f32[16,4,2048]{2,1,0:T(4,128)} %sddp_pack.1), calls=%async_computation | async-start | bytes 1048576 | tf_op jit(solution)/shard_map/all_to_all | solution.py:167
  27.7 0.0 copy-done.6
  27.7 0.1 copy.19
  27.8 0.1 reshape_squeeze.6.cols_ref
  27.9 14.2 %all-to-all-done = f32[16,4,2048]{2,1,0:T(4,128)S(1)} async-done(((f32[16,4,2048]{2,1,0:T(4,128)}), f32[16,4,2048]{2,1,0:T(4,128)S(1)}, u32[]{:S(2)}, u32[]{:S(2)}) %all-to-all-start) | async-done | bytes 524320 | tf_op jit(solution)/shard_map/all_to_all | solution.py:167
  42.1 0.2 reshape.54.rows_ref
  42.3 0.0 copy-done
  42.3 0.0 copy-done.1
  42.3 0.0 copy-done.2
  42.3 0.0 copy-done.3
  42.3 0.0 copy-done.4
  42.3 0.0 copy-done.5
  42.3 6.0 %sddp_solve.1 = f32[16,4,2176]{2,1,0:T(4,128)S(1)} custom-call(s32[32]{0:T(128)S(1)} %reshape_squeeze.6.cols_ref, f32[64,2048]{1,0:T(8,128)S(1)} %reshape.54.rows_ref, f32[1,2048]{1,0:T(1,128)S(1)} %bitcast.19, f32[1,2048]{1,0:T(1,128)S(1)} %bitcast.20, f32[1,2048]{1,0:T(1,128)S(1)} %bitcast.21, f32[1,2048]{1,0:T(1,128)S(1)} %bitcast.22, ...), custom_call_target="tpu_custom_call" | custom-call | flops 1610612736 | bytes 3670016 | tf_op jit(solution)/shard_map/sddp_solve/pallas_call | solution.py:116
  48.3 19.6 %all_to_all.10 = f32[16,4,2176]{2,1,0:T(4,128)S(1)} all-to-all(f32[16,4,2176]{2,1,0:T(4,128)S(1)} %sddp_solve.1), channel_id=1, replica_groups=mesh['week'=32,'markov'=16] {'markov'}, dimensions={0} | all-to-all | bytes 1114112 | tf_op jit(solution)/shard_map/all_to_all | solution.py:171
  67.9 1.0 %gather_fusion = f32[32,2176]{1,0:T(8,128)S(1)} fusion(f32[16,4,2176]{2,1,0:T(4,128)S(1)} %all_to_all.10, s32[32]{0:T(128)S(1)} %get-tuple-element.2), kind=kCustom, calls=%fused_computation | custom fusion | bytes 557312 | tf_op jit(solution)/shard_map/gather | solution.py:172
  68.9 3.3 %collective-permute-start.1 = (f32[32,2176]{1,0:T(8,128)S(1)}, f32[32,2176]{1,0:T(8,128)S(1)}, u32[]{:S(2)}, u32[]{:S(2)}) collective-permute-start(f32[32,2176]{1,0:T(8,128)S(1)} %gather_fusion), channel_id=1, source_target_pairs={{0,496},{16,0},{32,16},{48,32},{64,48},{80,64},{96,80},{112,96},{1... | collective-permute-start | bytes 835592 | tf_op jit(solution)/shard_map/ppermute | solution.py:20
  72.3 12.7 %collective-permute-done.1 = f32[32,2176]{1,0:T(8,128)S(1)} collective-permute-done((f32[32,2176]{1,0:T(8,128)S(1)}, f32[32,2176]{1,0:T(8,128)S(1)}, u32[]{:S(2)}, u32[]{:S(2)}) %collective-permute-start.1) | collective-permute-done | bytes 278560 | tf_op jit(solution)/shard_map/ppermute | solution.py:20
  85.0 0.6 slice_reduce_fusion
  85.6 0.7 slice_bitcast_fusion
  (2 shorter events, 0.0 us)
Async XLA Ops:
  0.6 27.1 %copy-start.6 = (s32[1,1,16,2]{2,3,1,0:T(2,128)S(1)}, s32[1,1,16,2]{2,3,1,0:T(2,128)}, u32[]{:S(2)}) copy-start(s32[1,1,16,2]{2,3,1,0:T(2,128)} %param.17) | copy-start | bytes 388
  1.3 41.0 %copy-start = (f32[1,1,16,2,128,128]{5,4,3,2,1,0:T(8,128)S(1)}, f32[1,1,16,2,128,128]{5,4,3,2,1,0:T(8,128)}, u32[]{:S(2)}) copy-start(f32[1,1,16,2,128,128]{5,4,3,2,1,0:T(8,128)} %param.16) | copy-start | bytes 6291460
  1.3 41.0 %copy-start.1 = (f32[1,1,2048]{2,1,0:T(1,128)S(1)}, f32[1,1,2048]{2,1,0:T(1,128)}, u32[]{:S(2)}) copy-start(f32[1,1,2048]{2,1,0:T(1,128)} %param.11) | copy-start | bytes 24580
  1.3 41.0 %copy-start.2 = (f32[1,1,2048]{2,1,0:T(1,128)S(1)}, f32[1,1,2048]{2,1,0:T(1,128)}, u32[]{:S(2)}) copy-start(f32[1,1,2048]{2,1,0:T(1,128)} %param.12) | copy-start | bytes 24580
  1.3 41.0 %copy-start.3 = (f32[1,1,2048]{2,1,0:T(1,128)S(1)}, f32[1,1,2048]{2,1,0:T(1,128)}, u32[]{:S(2)}) copy-start(f32[1,1,2048]{2,1,0:T(1,128)} %param.13) | copy-start | bytes 24580
  1.3 41.0 %copy-start.4 = (f32[1,1,2048]{2,1,0:T(1,128)S(1)}, f32[1,1,2048]{2,1,0:T(1,128)}, u32[]{:S(2)}) copy-start(f32[1,1,2048]{2,1,0:T(1,128)} %param.14) | copy-start | bytes 24580
  1.3 41.0 %copy-start.5 = (f32[1,1,2048]{2,1,0:T(1,128)S(1)}, f32[1,1,2048]{2,1,0:T(1,128)}, u32[]{:S(2)}) copy-start(f32[1,1,2048]{2,1,0:T(1,128)} %param.15) | copy-start | bytes 24580
  2.5 14.6 %collective-permute-start = (f32[32,2176]{1,0:T(8,128)S(1)}, f32[32,2176]{1,0:T(8,128)S(1)}, u32[]{:S(2)}, u32[]{:S(2)}) collective-permute-start(f32[32,2176]{1,0:T(8,128)S(1)} %pad_maximum_fusion), channel_id=1, source_target_pairs={{0,16},{16,32},{32,48},{48,64},{64,80},{80,96},{96,112},{112,128},... | collective-permute-start | bytes 835592 | tf_op jit(solution)/shard_map/ppermute | solution.py:20
  21.1 21.0 %all-to-all-start = ((f32[16,4,2048]{2,1,0:T(4,128)}), f32[16,4,2048]{2,1,0:T(4,128)S(1)}, u32[]{:S(2)}, u32[]{:S(2)}) async-start(f32[16,4,2048]{2,1,0:T(4,128)} %sddp_pack.1), calls=%async_computation | async-start | bytes 1048576 | tf_op jit(solution)/shard_map/all_to_all | solution.py:167
  68.9 16.1 %collective-permute-start.1 = (f32[32,2176]{1,0:T(8,128)S(1)}, f32[32,2176]{1,0:T(8,128)S(1)}, u32[]{:S(2)}, u32[]{:S(2)}) collective-permute-start(f32[32,2176]{1,0:T(8,128)S(1)} %gather_fusion), channel_id=1, source_target_pairs={{0,496},{16,0},{32,16},{48,32},{64,48},{80,64},{96,80},{112,96},{1... | collective-permute-start | bytes 835592 | tf_op jit(solution)/shard_map/ppermute | solution.py:20

commit v9 on v6

--- a/solution.py
+++ b/solution.py
@@ -35,7 +35,7 @@
 
 
 def solve_kernel(nblk, kblk, cols_ref, rows_ref, xi_ref, c_ref, q_ref, g_ref, h_ref, bv_ref,
-                 out_ref, base_s, p_s, u_s, v_s, acc_s, fh, fl, ah, al):
+                 out_ref, base_s, p_s, u_s, v_s, acc_s, spread_s, fh, fl, ah, al):
     width = nblk * BS
     rows_n = rows_ref.shape[0]
 
@@ -73,32 +73,32 @@
                 av = v_s[n] + mixed_fwd(v_s, n)
                 p_s[n] = (p_s[n] + dual_step * (base_s[n] - av)) * shrink
         for n in range(nblk):
-            acc_s[n] = jnp.zeros(acc_s.shape[1:], jnp.float32)
+            spread_s[n] = mm(p_s[n], ah[n], al[n])
         for n in range(nblk):
-            r = mm(p_s[n], ah[n], al[n])
+            acc_s[n] = p_s[n]
+        for n in range(nblk):
             for k in range(kblk):
                 c = col(n, k)
-                acc_s[c] = acc_s[c] + r[:, k * BS:(k + 1) * BS]
+                acc_s[c] = acc_s[c] + spread_s[n, :, k * BS:(k + 1) * BS]
         for n in range(nblk):
             s = lanes(n)
             u_old = u_s[n]
-            fresh = jnp.clip(u_old + primal_step * (p_s[n] + acc_s[n] - c_ref[:, s]), 0.0, h_ref[:, s])
+            fresh = jnp.clip(u_old + primal_step * (acc_s[n] - c_ref[:, s]), 0.0, h_ref[:, s])
             v_s[n] = 2.0 * fresh - u_old
             u_s[n] = fresh
 
-    value = jnp.zeros((rows_n, 1), jnp.float32)
-    cross = jnp.zeros((rows_n, 1), jnp.float32)
+    value = jnp.zeros((rows_n, BS), jnp.float32)
+    cross = jnp.zeros((rows_n, BS), jnp.float32)
     for n in range(nblk):
         s = lanes(n)
         rows = rows_ref[:, s]
         un = u_s[n]
         gap = rows + xi_ref[:, s] - (un + mixed_fwd(u_s, n)) - g_ref[:, s]
-        term = c_ref[:, s] * un + 0.5 * q_ref[:, s] * gap * gap
-        value = value + jnp.sum(term, axis=1, keepdims=True)
+        value = value + (c_ref[:, s] * un + 0.5 * q_ref[:, s] * gap * gap)
         pn = p_s[n]
-        cross = cross + jnp.sum(pn * rows, axis=1, keepdims=True)
+        cross = cross + pn * rows
         out_ref[:, :, s] = pn.reshape(out_ref.shape[0], out_ref.shape[1], BS)
-    icpt = (value - cross) / width
+    icpt = (jnp.sum(value, axis=1, keepdims=True) - jnp.sum(cross, axis=1, keepdims=True)) / width
     out_ref[:, :, width:] = jnp.broadcast_to(icpt, (rows_n, BS)).reshape(out_ref.shape[0], out_ref.shape[1], BS)
 
 
@@ -109,7 +109,7 @@
     vec = lambda a: a.reshape(1, width)
     vspec = pl.BlockSpec(memory_space=pltpu.VMEM)
     field = pltpu.VMEM((nblk, count, BS), jnp.float32)
-    scratch = [field] * 5
+    scratch = [field] * 5 + [pltpu.VMEM((nblk, count, kblk * BS), jnp.float32)]
     scratch += [pltpu.VMEM((nblk, kblk * BS, BS), jnp.bfloat16)] * 2
     scratch += [pltpu.VMEM((nblk, BS, kblk * BS), jnp.bfloat16)] * 2
     flops = 2 * count * nblk * kblk * BS * BS * (2 * ITERS) * 3

time: 85.1 us -> 84.8 us (level)
  no operation moved by 1% of the time
where the time goes in v9:
time: 84.8 us; the launch traced here: 84.5 us
  waiting for transfers between devices  31.2 us (37%)
  starting transfers between devices  20.3 us (24%)
  blocking collectives  19.5 us (23%)
  Pallas kernels  5.62 us (7%)
  local copies, waits for them, and re-layouts  4.69 us (6%)
  other arithmetic  2.28 us (3%)
    all_to_all x1, blocking collectives, on_device(): back = lax.all_to_all(solved, 'markov', 0, 0, tiled=True)  19.5 us
    ppermute x2, waiting for transfers between devices, shifted(): return lax.ppermute(value, axis, pairs)  17 us
    all_to_all x1, waiting for transfers between devices, on_device(): arrived = lax.all_to_all(packed, 'markov', 0, 0, tiled=True)  14.2 us
    ppermute x2, starting transfers between devices, shifted(): return lax.ppermute(value, axis, pairs)  13.8 us
    all_to_all x1, starting transfers between devices, on_device(): arrived = lax.all_to_all(packed, 'markov', 0, 0, tiled=True)  6.57 us
    pallas_call x1, Pallas kernels, solve_block(): pl.pallas_call(functools.partial(solve_kernel, nblk, kblk), out_shape=jax...  5.62 us
  transfers between devices with their start and end apart: 3, of which 3 were waited for; matrix products, arithmetic and copies ran while one was open for 0% of the time, Pallas kernels for 0%

profile of v9, /device:TPU:57, one launch (start us, length us, event | category | flops | bytes accessed | tf_op | source)
XLA Modules:
  0.0 84.5 jit_solution(2259487581420051593)
XLA Ops:
  0.6 0.7 convert_bitcast_fusion
  1.3 0.1 broadcast_in_dim.17
  1.4 1.0 %pad_maximum_fusion = f32[32,2176]{1,0:T(8,128)S(1)} fusion(f32[32,128]{1,0:T(8,128)S(1)} %broadcast_in_dim.17, f32[32,2048]{1,0:T(8,128)} %bitcast.24), kind=kLoop, calls=%fused_computation.2 | loop fusion | flops 69632 | bytes 557056 | tf_op jit(solution)/shard_map/concatenate | solution.py:140
  2.3 10.4 %collective-permute-start = (f32[32,2176]{1,0:T(8,128)S(1)}, f32[32,2176]{1,0:T(8,128)S(1)}, u32[]{:S(2)}, u32[]{:S(2)}) collective-permute-start(f32[32,2176]{1,0:T(8,128)S(1)} %pad_maximum_fusion), channel_id=1, source_target_pairs={{0,16},{16,32},{32,48},{48,64},{64,80},{80,96},{96,112},{112,128},... | collective-permute-start | bytes 835592 | tf_op jit(solution)/shard_map/ppermute | solution.py:20
  12.7 4.2 %collective-permute-done = f32[32,2176]{1,0:T(8,128)S(1)} collective-permute-done((f32[32,2176]{1,0:T(8,128)S(1)}, f32[32,2176]{1,0:T(8,128)S(1)}, u32[]{:S(2)}, u32[]{:S(2)}) %collective-permute-start) | collective-permute-done | bytes 278560 | tf_op jit(solution)/shard_map/ppermute | solution.py:20
  17.0 0.1 fusion.7
  17.1 0.1 fusion.6
  17.2 0.1 reduce_window_sum.11
  17.2 0.2 select_reduce_fusion.1
  17.4 0.1 copy.20
  17.5 0.1 copy.21
  17.6 0.1 fusion.3
  17.7 0.1 select_reduce_fusion
  17.8 0.0 copy-start.6
  17.9 0.8 gather_fusion
  18.6 0.0 copy-start
  18.6 0.0 copy-start.1
  18.6 0.0 copy-start.2
  18.7 0.0 copy-start.3
  18.7 0.0 copy-start.4
  18.7 0.0 copy-start.5
  18.7 0.9 %reshape.59 = f32[16,4,2048]{2,1,0:T(4,128)} reshape(f32[64,2048]{1,0:T(8,128)S(1)} %gather_fusion) | data formatting | bytes 1048576 | tf_op jit(solution)/shard_map/jit(_take)/gather | solution.py:147
  19.6 6.6 %all-to-all-start = ((f32[16,4,2048]{2,1,0:T(4,128)}), f32[16,4,2048]{2,1,0:T(4,128)S(1)}, u32[]{:S(2)}, u32[]{:S(2)}) async-start(f32[16,4,2048]{2,1,0:T(4,128)} %reshape.59), calls=%async_computation | async-start | bytes 1048576 | tf_op jit(solution)/shard_map/all_to_all | solution.py:148
  26.2 0.0 copy-done.6
  26.2 0.1 copy.19
  26.3 0.1 reshape_squeeze.6.cols_ref
  26.4 14.2 %all-to-all-done = f32[16,4,2048]{2,1,0:T(4,128)S(1)} async-done(((f32[16,4,2048]{2,1,0:T(4,128)}), f32[16,4,2048]{2,1,0:T(4,128)S(1)}, u32[]{:S(2)}, u32[]{:S(2)}) %all-to-all-start) | async-done | bytes 524320 | tf_op jit(solution)/shard_map/all_to_all | solution.py:148
  40.6 0.2 reshape.56.rows_ref
  40.8 0.0 copy-done
  40.8 0.0 copy-done.1
  40.8 0.0 copy-done.2
  40.8 0.0 copy-done.3
  40.8 0.0 copy-done.4
  40.8 0.0 copy-done.5
  40.8 5.6 %sddp_solve.1 = f32[16,4,2176]{2,1,0:T(4,128)S(1)} custom-call(s32[32]{0:T(128)S(1)} %reshape_squeeze.6.cols_ref, f32[64,2048]{1,0:T(8,128)S(1)} %reshape.56.rows_ref, f32[1,2048]{1,0:T(1,128)S(1)} %bitcast.19, f32[1,2048]{1,0:T(1,128)S(1)} %bitcast.20, f32[1,2048]{1,0:T(1,128)S(1)} %bitcast.21, f32[1,2048]{1,0:T(1,128)S(1)} %bitcast.22, ...), custom_call_target="tpu_custom_call" | custom-call | flops 1610612736 | bytes 3670016 | tf_op jit(solution)/shard_map/sddp_solve/pallas_call | solution.py:116
  46.5 19.5 %all_to_all.10 = f32[16,4,2176]{2,1,0:T(4,128)S(1)} all-to-all(f32[16,4,2176]{2,1,0:T(4,128)S(1)} %sddp_solve.1), channel_id=1, replica_groups=mesh['week'=32,'markov'=16] {'markov'}, dimensions={0} | all-to-all | bytes 1114112 | tf_op jit(solution)/shard_map/all_to_all | solution.py:152
  66.0 1.0 %gather_fusion.1 = f32[32,2176]{1,0:T(8,128)S(1)} fusion(f32[16,4,2176]{2,1,0:T(4,128)S(1)} %all_to_all.10, s32[32]{0:T(128)S(1)} %get-tuple-element.2), kind=kCustom, calls=%fused_computation.1 | custom fusion | bytes 557312 | tf_op jit(solution)/shard_map/gather | solution.py:153
  67.0 3.4 %collective-permute-start.1 = (f32[32,2176]{1,0:T(8,128)S(1)}, f32[32,2176]{1,0:T(8,128)S(1)}, u32[]{:S(2)}, u32[]{:S(2)}) collective-permute-start(f32[32,2176]{1,0:T(8,128)S(1)} %gather_fusion.1), channel_id=1, source_target_pairs={{0,496},{16,0},{32,16},{48,32},{64,48},{80,64},{96,80},{112,96},{1... | collective-permute-start | bytes 835592 | tf_op jit(solution)/shard_map/ppermute | solution.py:20
  70.4 12.8 %collective-permute-done.1 = f32[32,2176]{1,0:T(8,128)S(1)} collective-permute-done((f32[32,2176]{1,0:T(8,128)S(1)}, f32[32,2176]{1,0:T(8,128)S(1)}, u32[]{:S(2)}, u32[]{:S(2)}) %collective-permute-start.1) | collective-permute-done | bytes 278560 | tf_op jit(solution)/shard_map/ppermute | solution.py:20
  83.1 0.6 slice_reduce_fusion
  83.7 0.7 slice_bitcast_fusion
  (4 shorter events, 0.0 us)
Async XLA Ops:
  2.3 14.6 %collective-permute-start = (f32[32,2176]{1,0:T(8,128)S(1)}, f32[32,2176]{1,0:T(8,128)S(1)}, u32[]{:S(2)}, u32[]{:S(2)}) collective-permute-start(f32[32,2176]{1,0:T(8,128)S(1)} %pad_maximum_fusion), channel_id=1, source_target_pairs={{0,16},{16,32},{32,48},{48,64},{64,80},{80,96},{96,112},{112,128},... | collective-permute-start | bytes 835592 | tf_op jit(solution)/shard_map/ppermute | solution.py:20
  17.8 8.4 %copy-start.6 = (s32[1,1,16,2]{2,3,1,0:T(2,128)S(1)}, s32[1,1,16,2]{2,3,1,0:T(2,128)}, u32[]{:S(2)}) copy-start(s32[1,1,16,2]{2,3,1,0:T(2,128)} %param.17) | copy-start | bytes 388
  18.6 22.2 %copy-start = (f32[1,1,16,2,128,128]{5,4,3,2,1,0:T(8,128)S(1)}, f32[1,1,16,2,128,128]{5,4,3,2,1,0:T(8,128)}, u32[]{:S(2)}) copy-start(f32[1,1,16,2,128,128]{5,4,3,2,1,0:T(8,128)} %param.16) | copy-start | bytes 6291460
  18.6 22.2 %copy-start.1 = (f32[1,1,2048]{2,1,0:T(1,128)S(1)}, f32[1,1,2048]{2,1,0:T(1,128)}, u32[]{:S(2)}) copy-start(f32[1,1,2048]{2,1,0:T(1,128)} %param.11) | copy-start | bytes 24580
  18.6 22.2 %copy-start.2 = (f32[1,1,2048]{2,1,0:T(1,128)S(1)}, f32[1,1,2048]{2,1,0:T(1,128)}, u32[]{:S(2)}) copy-start(f32[1,1,2048]{2,1,0:T(1,128)} %param.12) | copy-start | bytes 24580
  18.7 22.2 %copy-start.3 = (f32[1,1,2048]{2,1,0:T(1,128)S(1)}, f32[1,1,2048]{2,1,0:T(1,128)}, u32[]{:S(2)}) copy-start(f32[1,1,2048]{2,1,0:T(1,128)} %param.13) | copy-start | bytes 24580
  18.7 22.2 %copy-start.4 = (f32[1,1,2048]{2,1,0:T(1,128)S(1)}, f32[1,1,2048]{2,1,0:T(1,128)}, u32[]{:S(2)}) copy-start(f32[1,1,2048]{2,1,0:T(1,128)} %param.14) | copy-start | bytes 24580
  18.7 22.2 %copy-start.5 = (f32[1,1,2048]{2,1,0:T(1,128)S(1)}, f32[1,1,2048]{2,1,0:T(1,128)}, u32[]{:S(2)}) copy-start(f32[1,1,2048]{2,1,0:T(1,128)} %param.15) | copy-start | bytes 24580
  19.6 21.0 %all-to-all-start = ((f32[16,4,2048]{2,1,0:T(4,128)}), f32[16,4,2048]{2,1,0:T(4,128)S(1)}, u32[]{:S(2)}, u32[]{:S(2)}) async-start(f32[16,4,2048]{2,1,0:T(4,128)} %reshape.59), calls=%async_computation | async-start | bytes 1048576 | tf_op jit(solution)/shard_map/all_to_all | solution.py:148
  67.0 16.1 %collective-permute-start.1 = (f32[32,2176]{1,0:T(8,128)S(1)}, f32[32,2176]{1,0:T(8,128)S(1)}, u32[]{:S(2)}, u32[]{:S(2)}) collective-permute-start(f32[32,2176]{1,0:T(8,128)S(1)} %gather_fusion.1), channel_id=1, source_target_pairs={{0,496},{16,0},{32,16},{48,32},{64,48},{80,64},{96,80},{112,96},{1... | collective-permute-start | bytes 835592 | tf_op jit(solution)/shard_map/ppermute | solution.py:20

commit v10 on v9

--- a/solution.py
+++ b/solution.py
@@ -29,13 +29,13 @@
     return hi, (x - hi.astype(jnp.float32)).astype(jnp.bfloat16)
 
 
-def mm(x, wh, wl):
+def mm(x, w3):
     xh, xl = split(x)
-    return dotb(xh, wh) + dotb(xl, wh) + dotb(xh, wl)
+    return dotb(jnp.concatenate([xh, xl, xh], axis=1), w3)
 
 
 def solve_kernel(nblk, kblk, cols_ref, rows_ref, xi_ref, c_ref, q_ref, g_ref, h_ref, bv_ref,
-                 out_ref, base_s, p_s, u_s, v_s, acc_s, spread_s, fh, fl, ah, al):
+                 out_ref, base_s, p_s, u_s, v_s, acc_s, spread_s, fw, aw):
     width = nblk * BS
     rows_n = rows_ref.shape[0]
 
@@ -47,15 +47,13 @@
 
     for n in range(nblk):
         hi, lo = split(jnp.concatenate([bv_ref[n, k].T for k in range(kblk)], axis=0))
-        fh[n] = hi
-        fl[n] = lo
+        fw[n] = jnp.concatenate([hi, hi, lo], axis=0)
         hi, lo = split(jnp.concatenate([bv_ref[n, k] for k in range(kblk)], axis=1))
-        ah[n] = hi
-        al[n] = lo
+        aw[n] = jnp.concatenate([hi, hi, lo], axis=0)
 
     def mixed_fwd(field_s, n):
         x = jnp.concatenate([field_s[col(n, k)] for k in range(kblk)], axis=1)
-        return mm(x, fh[n], fl[n])
+        return mm(x, fw[n])
 
     for n in range(nblk):
         s = lanes(n)
@@ -73,7 +71,7 @@
                 av = v_s[n] + mixed_fwd(v_s, n)
                 p_s[n] = (p_s[n] + dual_step * (base_s[n] - av)) * shrink
         for n in range(nblk):
-            spread_s[n] = mm(p_s[n], ah[n], al[n])
+            spread_s[n] = mm(p_s[n], aw[n])
         for n in range(nblk):
             acc_s[n] = p_s[n]
         for n in range(nblk):
@@ -110,8 +108,8 @@
     vspec = pl.BlockSpec(memory_space=pltpu.VMEM)
     field = pltpu.VMEM((nblk, count, BS), jnp.float32)
     scratch = [field] * 5 + [pltpu.VMEM((nblk, count, kblk * BS), jnp.float32)]
-    scratch += [pltpu.VMEM((nblk, kblk * BS, BS), jnp.bfloat16)] * 2
-    scratch += [pltpu.VMEM((nblk, BS, kblk * BS), jnp.bfloat16)] * 2
+    scratch += [pltpu.VMEM((nblk, 3 * kblk * BS, BS), jnp.bfloat16)]
+    scratch += [pltpu.VMEM((nblk, 3 * BS, kblk * BS), jnp.bfloat16)]
     flops = 2 * count * nblk * kblk * BS * BS * (2 * ITERS) * 3
     return pl.pallas_call(
         functools.partial(solve_kernel, nblk, kblk),

time: 84.8 us -> 85.2 us (level)
  no operation moved by 1% of the time
where the time goes in v10:
time: 85.2 us; the launch traced here: 84.9 us
  waiting for transfers between devices  31.2 us (37%)
  starting transfers between devices  20.3 us (24%)
  blocking collectives  19.6 us (23%)
  Pallas kernels  6.02 us (7%)
  local copies, waits for them, and re-layouts  4.69 us (6%)
  other arithmetic  2.28 us (3%)
    all_to_all x1, blocking collectives, on_device(): back = lax.all_to_all(solved, 'markov', 0, 0, tiled=True)  19.6 us
    ppermute x2, waiting for transfers between devices, shifted(): return lax.ppermute(value, axis, pairs)  16.9 us
    all_to_all x1, waiting for transfers between devices, on_device(): arrived = lax.all_to_all(packed, 'markov', 0, 0, tiled=True)  14.2 us
    ppermute x2, starting transfers between devices, shifted(): return lax.ppermute(value, axis, pairs)  13.7 us
    all_to_all x1, starting transfers between devices, on_device(): arrived = lax.all_to_all(packed, 'markov', 0, 0, tiled=True)  6.57 us
    pallas_call x1, Pallas kernels, solve_block(): pl.pallas_call(functools.partial(solve_kernel, nblk, kblk), out_shape=jax...  6.02 us
  transfers between devices with their start and end apart: 3, of which 3 were waited for; matrix products, arithmetic and copies ran while one was open for 0% of the time, Pallas kernels for 0%

profile of v10, /device:TPU:57, one launch (start us, length us, event | category | flops | bytes accessed | tf_op | source)
XLA Modules:
  0.0 84.9 jit_solution(4399015344075868811)
XLA Ops:
  0.6 0.7 convert_bitcast_fusion
  1.3 0.1 broadcast_in_dim.17
  1.4 1.0 %pad_maximum_fusion = f32[32,2176]{1,0:T(8,128)S(1)} fusion(f32[32,128]{1,0:T(8,128)S(1)} %broadcast_in_dim.17, f32[32,2048]{1,0:T(8,128)} %bitcast.24), kind=kLoop, calls=%fused_computation.2 | loop fusion | flops 69632 | bytes 557056 | tf_op jit(solution)/shard_map/concatenate | solution.py:138
  2.3 10.4 %collective-permute-start = (f32[32,2176]{1,0:T(8,128)S(1)}, f32[32,2176]{1,0:T(8,128)S(1)}, u32[]{:S(2)}, u32[]{:S(2)}) collective-permute-start(f32[32,2176]{1,0:T(8,128)S(1)} %pad_maximum_fusion), channel_id=1, source_target_pairs={{0,16},{16,32},{32,48},{48,64},{64,80},{80,96},{96,112},{112,128},... | collective-permute-start | bytes 835592 | tf_op jit(solution)/shard_map/ppermute | solution.py:20
  12.7 4.2 %collective-permute-done = f32[32,2176]{1,0:T(8,128)S(1)} collective-permute-done((f32[32,2176]{1,0:T(8,128)S(1)}, f32[32,2176]{1,0:T(8,128)S(1)}, u32[]{:S(2)}, u32[]{:S(2)}) %collective-permute-start) | collective-permute-done | bytes 278560 | tf_op jit(solution)/shard_map/ppermute | solution.py:20
  17.0 0.1 fusion.7
  17.1 0.1 fusion.6
  17.2 0.1 reduce_window_sum.11
  17.2 0.2 select_reduce_fusion.1
  17.4 0.1 copy.20
  17.5 0.1 copy.21
  17.6 0.1 fusion.3
  17.7 0.1 select_reduce_fusion
  17.8 0.0 copy-start.6
  17.9 0.8 gather_fusion
  18.6 0.0 copy-start
  18.6 0.0 copy-start.1
  18.6 0.0 copy-start.2
  18.7 0.0 copy-start.3
  18.7 0.0 copy-start.4
  18.7 0.0 copy-start.5
  18.7 0.9 %reshape.59 = f32[16,4,2048]{2,1,0:T(4,128)} reshape(f32[64,2048]{1,0:T(8,128)S(1)} %gather_fusion) | data formatting | bytes 1048576 | tf_op jit(solution)/shard_map/jit(_take)/gather | solution.py:145
  19.6 6.6 %all-to-all-start = ((f32[16,4,2048]{2,1,0:T(4,128)}), f32[16,4,2048]{2,1,0:T(4,128)S(1)}, u32[]{:S(2)}, u32[]{:S(2)}) async-start(f32[16,4,2048]{2,1,0:T(4,128)} %reshape.59), calls=%async_computation | async-start | bytes 1048576 | tf_op jit(solution)/shard_map/all_to_all | solution.py:146
  26.2 0.0 copy-done.6
  26.2 0.1 copy.19
  26.3 0.1 reshape_squeeze.6.cols_ref
  26.4 14.2 %all-to-all-done = f32[16,4,2048]{2,1,0:T(4,128)S(1)} async-done(((f32[16,4,2048]{2,1,0:T(4,128)}), f32[16,4,2048]{2,1,0:T(4,128)S(1)}, u32[]{:S(2)}, u32[]{:S(2)}) %all-to-all-start) | async-done | bytes 524320 | tf_op jit(solution)/shard_map/all_to_all | solution.py:146
  40.6 0.2 reshape.56.rows_ref
  40.8 0.0 copy-done
  40.8 0.0 copy-done.1
  40.8 0.0 copy-done.2
  40.8 0.0 copy-done.3
  40.8 0.0 copy-done.4
  40.8 0.0 copy-done.5
  40.8 6.0 %sddp_solve.1 = f32[16,4,2176]{2,1,0:T(4,128)S(1)} custom-call(s32[32]{0:T(128)S(1)} %reshape_squeeze.6.cols_ref, f32[64,2048]{1,0:T(8,128)S(1)} %reshape.56.rows_ref, f32[1,2048]{1,0:T(1,128)S(1)} %bitcast.19, f32[1,2048]{1,0:T(1,128)S(1)} %bitcast.20, f32[1,2048]{1,0:T(1,128)S(1)} %bitcast.21, f32[1,2048]{1,0:T(1,128)S(1)} %bitcast.22, ...), custom_call_target="tpu_custom_call" | custom-call | flops 1610612736 | bytes 3670016 | tf_op jit(solution)/shard_map/sddp_solve/pallas_call | solution.py:114
  46.9 19.6 %all_to_all.10 = f32[16,4,2176]{2,1,0:T(4,128)S(1)} all-to-all(f32[16,4,2176]{2,1,0:T(4,128)S(1)} %sddp_solve.1), channel_id=1, replica_groups=mesh['week'=32,'markov'=16] {'markov'}, dimensions={0} | all-to-all | bytes 1114112 | tf_op jit(solution)/shard_map/all_to_all | solution.py:150
  66.5 1.0 %gather_fusion.1 = f32[32,2176]{1,0:T(8,128)S(1)} fusion(f32[16,4,2176]{2,1,0:T(4,128)S(1)} %all_to_all.10, s32[32]{0:T(128)S(1)} %get-tuple-element.2), kind=kCustom, calls=%fused_computation.1 | custom fusion | bytes 557312 | tf_op jit(solution)/shard_map/gather | solution.py:151
  67.5 3.3 %collective-permute-start.1 = (f32[32,2176]{1,0:T(8,128)S(1)}, f32[32,2176]{1,0:T(8,128)S(1)}, u32[]{:S(2)}, u32[]{:S(2)}) collective-permute-start(f32[32,2176]{1,0:T(8,128)S(1)} %gather_fusion.1), channel_id=1, source_target_pairs={{0,496},{16,0},{32,16},{48,32},{64,48},{80,64},{96,80},{112,96},{1... | collective-permute-start | bytes 835592 | tf_op jit(solution)/shard_map/ppermute | solution.py:20
  70.8 12.7 %collective-permute-done.1 = f32[32,2176]{1,0:T(8,128)S(1)} collective-permute-done((f32[32,2176]{1,0:T(8,128)S(1)}, f32[32,2176]{1,0:T(8,128)S(1)}, u32[]{:S(2)}, u32[]{:S(2)}) %collective-permute-start.1) | collective-permute-done | bytes 278560 | tf_op jit(solution)/shard_map/ppermute | solution.py:20
  83.5 0.6 slice_reduce_fusion
  84.2 0.7 slice_bitcast_fusion
  (4 shorter events, 0.0 us)
Async XLA Ops:
  2.3 14.6 %collective-permute-start = (f32[32,2176]{1,0:T(8,128)S(1)}, f32[32,2176]{1,0:T(8,128)S(1)}, u32[]{:S(2)}, u32[]{:S(2)}) collective-permute-start(f32[32,2176]{1,0:T(8,128)S(1)} %pad_maximum_fusion), channel_id=1, source_target_pairs={{0,16},{16,32},{32,48},{48,64},{64,80},{80,96},{96,112},{112,128},... | collective-permute-start | bytes 835592 | tf_op jit(solution)/shard_map/ppermute | solution.py:20
  17.8 8.4 %copy-start.6 = (s32[1,1,16,2]{2,3,1,0:T(2,128)S(1)}, s32[1,1,16,2]{2,3,1,0:T(2,128)}, u32[]{:S(2)}) copy-start(s32[1,1,16,2]{2,3,1,0:T(2,128)} %param.17) | copy-start | bytes 388
  18.6 22.2 %copy-start = (f32[1,1,16,2,128,128]{5,4,3,2,1,0:T(8,128)S(1)}, f32[1,1,16,2,128,128]{5,4,3,2,1,0:T(8,128)}, u32[]{:S(2)}) copy-start(f32[1,1,16,2,128,128]{5,4,3,2,1,0:T(8,128)} %param.16) | copy-start | bytes 6291460
  18.6 22.2 %copy-start.1 = (f32[1,1,2048]{2,1,0:T(1,128)S(1)}, f32[1,1,2048]{2,1,0:T(1,128)}, u32[]{:S(2)}) copy-start(f32[1,1,2048]{2,1,0:T(1,128)} %param.11) | copy-start | bytes 24580
  18.6 22.2 %copy-start.2 = (f32[1,1,2048]{2,1,0:T(1,128)S(1)}, f32[1,1,2048]{2,1,0:T(1,128)}, u32[]{:S(2)}) copy-start(f32[1,1,2048]{2,1,0:T(1,128)} %param.12) | copy-start | bytes 24580
  18.7 22.2 %copy-start.3 = (f32[1,1,2048]{2,1,0:T(1,128)S(1)}, f32[1,1,2048]{2,1,0:T(1,128)}, u32[]{:S(2)}) copy-start(f32[1,1,2048]{2,1,0:T(1,128)} %param.13) | copy-start | bytes 24580
  18.7 22.2 %copy-start.4 = (f32[1,1,2048]{2,1,0:T(1,128)S(1)}, f32[1,1,2048]{2,1,0:T(1,128)}, u32[]{:S(2)}) copy-start(f32[1,1,2048]{2,1,0:T(1,128)} %param.14) | copy-start | bytes 24580
  18.7 22.2 %copy-start.5 = (f32[1,1,2048]{2,1,0:T(1,128)S(1)}, f32[1,1,2048]{2,1,0:T(1,128)}, u32[]{:S(2)}) copy-start(f32[1,1,2048]{2,1,0:T(1,128)} %param.15) | copy-start | bytes 24580
  19.6 21.0 %all-to-all-start = ((f32[16,4,2048]{2,1,0:T(4,128)}), f32[16,4,2048]{2,1,0:T(4,128)S(1)}, u32[]{:S(2)}, u32[]{:S(2)}) async-start(f32[16,4,2048]{2,1,0:T(4,128)} %reshape.59), calls=%async_computation | async-start | bytes 1048576 | tf_op jit(solution)/shard_map/all_to_all | solution.py:146
  67.5 16.1 %collective-permute-start.1 = (f32[32,2176]{1,0:T(8,128)S(1)}, f32[32,2176]{1,0:T(8,128)S(1)}, u32[]{:S(2)}, u32[]{:S(2)}) collective-permute-start(f32[32,2176]{1,0:T(8,128)S(1)} %gather_fusion.1), channel_id=1, source_target_pairs={{0,496},{16,0},{32,16},{48,32},{64,48},{80,64},{96,80},{112,96},{1... | collective-permute-start | bytes 835592 | tf_op jit(solution)/shard_map/ppermute | solution.py:20

commit v11 on v9

--- a/solution.py
+++ b/solution.py
@@ -35,7 +35,7 @@
 
 
 def solve_kernel(nblk, kblk, cols_ref, rows_ref, xi_ref, c_ref, q_ref, g_ref, h_ref, bv_ref,
-                 out_ref, base_s, p_s, u_s, v_s, acc_s, spread_s, fh, fl, ah, al):
+                 out_ref, base_s, p_s, u_s, v_s, acc_s, spread_s, xh_s, xl_s, fh, fl, ah, al):
     width = nblk * BS
     rows_n = rows_ref.shape[0]
 
@@ -53,9 +53,10 @@
         ah[n] = hi
         al[n] = lo
 
-    def mixed_fwd(field_s, n):
-        x = jnp.concatenate([field_s[col(n, k)] for k in range(kblk)], axis=1)
-        return mm(x, fh[n], fl[n])
+    def mixed_fwd(n):
+        xh = jnp.concatenate([xh_s[col(n, k)] for k in range(kblk)], axis=1)
+        xl = jnp.concatenate([xl_s[col(n, k)] for k in range(kblk)], axis=1)
+        return dotb(xh, fh[n]) + dotb(xl, fh[n]) + dotb(xh, fl[n])
 
     for n in range(nblk):
         s = lanes(n)
@@ -70,7 +71,7 @@
             if sweep == 0:
                 p_s[n] = (dual_step * base_s[n]) * shrink
             else:
-                av = v_s[n] + mixed_fwd(v_s, n)
+                av = v_s[n] + mixed_fwd(n)
                 p_s[n] = (p_s[n] + dual_step * (base_s[n] - av)) * shrink
         for n in range(nblk):
             spread_s[n] = mm(p_s[n], ah[n], al[n])
@@ -84,8 +85,12 @@
             s = lanes(n)
             u_old = u_s[n]
             fresh = jnp.clip(u_old + primal_step * (acc_s[n] - c_ref[:, s]), 0.0, h_ref[:, s])
-            v_s[n] = 2.0 * fresh - u_old
+            v = 2.0 * fresh - u_old
+            v_s[n] = v
             u_s[n] = fresh
+            hi, lo = split(fresh if sweep == ITERS - 1 else v)
+            xh_s[n] = hi
+            xl_s[n] = lo
 
     value = jnp.zeros((rows_n, BS), jnp.float32)
     cross = jnp.zeros((rows_n, BS), jnp.float32)
@@ -93,7 +98,7 @@
         s = lanes(n)
         rows = rows_ref[:, s]
         un = u_s[n]
-        gap = rows + xi_ref[:, s] - (un + mixed_fwd(u_s, n)) - g_ref[:, s]
+        gap = rows + xi_ref[:, s] - (un + mixed_fwd(n)) - g_ref[:, s]
         value = value + (c_ref[:, s] * un + 0.5 * q_ref[:, s] * gap * gap)
         pn = p_s[n]
         cross = cross + pn * rows
@@ -110,6 +115,7 @@
     vspec = pl.BlockSpec(memory_space=pltpu.VMEM)
     field = pltpu.VMEM((nblk, count, BS), jnp.float32)
     scratch = [field] * 5 + [pltpu.VMEM((nblk, count, kblk * BS), jnp.float32)]
+    scratch += [pltpu.VMEM((nblk, count, BS), jnp.bfloat16)] * 2
     scratch += [pltpu.VMEM((nblk, kblk * BS, BS), jnp.bfloat16)] * 2
     scratch += [pltpu.VMEM((nblk, BS, kblk * BS), jnp.bfloat16)] * 2
     flops = 2 * count * nblk * kblk * BS * BS * (2 * ITERS) * 3

time: 84.8 us -> 85 us (level)
  no operation moved by 1% of the time
where the time goes in v11:
time: 85 us; the launch traced here: 84.7 us
  waiting for transfers between devices  31.2 us (37%)
  starting transfers between devices  20.3 us (24%)
  blocking collectives  19.6 us (23%)
  Pallas kernels  5.81 us (7%)
  local copies, waits for them, and re-layouts  4.69 us (6%)
  other arithmetic  2.28 us (3%)
    all_to_all x1, blocking collectives, on_device(): back = lax.all_to_all(solved, 'markov', 0, 0, tiled=True)  19.6 us
    ppermute x2, waiting for transfers between devices, shifted(): return lax.ppermute(value, axis, pairs)  17 us
    all_to_all x1, waiting for transfers between devices, on_device(): arrived = lax.all_to_all(packed, 'markov', 0, 0, tiled=True)  14.2 us
    ppermute x2, starting transfers between devices, shifted(): return lax.ppermute(value, axis, pairs)  13.7 us
    all_to_all x1, starting transfers between devices, on_device(): arrived = lax.all_to_all(packed, 'markov', 0, 0, tiled=True)  6.57 us
    pallas_call x1, Pallas kernels, solve_block(): pl.pallas_call(functools.partial(solve_kernel, nblk, kblk), out_shape=jax...  5.81 us
  transfers between devices with their start and end apart: 3, of which 3 were waited for; matrix products, arithmetic and copies ran while one was open for 0% of the time, Pallas kernels for 0%

profile of v11, /device:TPU:57, one launch (start us, length us, event | category | flops | bytes accessed | tf_op | source)
XLA Modules:
  0.0 84.7 jit_solution(12071654026610429978)
XLA Ops:
  0.6 0.7 convert_bitcast_fusion
  1.3 0.1 broadcast_in_dim.17
  1.4 1.0 %pad_maximum_fusion = f32[32,2176]{1,0:T(8,128)S(1)} fusion(f32[32,128]{1,0:T(8,128)S(1)} %broadcast_in_dim.17, f32[32,2048]{1,0:T(8,128)} %bitcast.24), kind=kLoop, calls=%fused_computation.2 | loop fusion | flops 69632 | bytes 557056 | tf_op jit(solution)/shard_map/concatenate | solution.py:146
  2.3 10.4 %collective-permute-start = (f32[32,2176]{1,0:T(8,128)S(1)}, f32[32,2176]{1,0:T(8,128)S(1)}, u32[]{:S(2)}, u32[]{:S(2)}) collective-permute-start(f32[32,2176]{1,0:T(8,128)S(1)} %pad_maximum_fusion), channel_id=1, source_target_pairs={{0,16},{16,32},{32,48},{48,64},{64,80},{80,96},{96,112},{112,128},... | collective-permute-start | bytes 835592 | tf_op jit(solution)/shard_map/ppermute | solution.py:20
  12.7 4.2 %collective-permute-done = f32[32,2176]{1,0:T(8,128)S(1)} collective-permute-done((f32[32,2176]{1,0:T(8,128)S(1)}, f32[32,2176]{1,0:T(8,128)S(1)}, u32[]{:S(2)}, u32[]{:S(2)}) %collective-permute-start) | collective-permute-done | bytes 278560 | tf_op jit(solution)/shard_map/ppermute | solution.py:20
  17.0 0.1 fusion.7
  17.1 0.1 fusion.6
  17.2 0.1 reduce_window_sum.11
  17.2 0.2 select_reduce_fusion.1
  17.4 0.1 copy.20
  17.5 0.1 copy.21
  17.6 0.1 fusion.3
  17.7 0.1 select_reduce_fusion
  17.8 0.0 copy-start.6
  17.9 0.8 gather_fusion
  18.6 0.0 copy-start
  18.6 0.0 copy-start.1
  18.6 0.0 copy-start.2
  18.7 0.0 copy-start.3
  18.7 0.0 copy-start.4
  18.7 0.0 copy-start.5
  18.7 0.9 %reshape.59 = f32[16,4,2048]{2,1,0:T(4,128)} reshape(f32[64,2048]{1,0:T(8,128)S(1)} %gather_fusion) | data formatting | bytes 1048576 | tf_op jit(solution)/shard_map/jit(_take)/gather | solution.py:153
  19.6 6.6 %all-to-all-start = ((f32[16,4,2048]{2,1,0:T(4,128)}), f32[16,4,2048]{2,1,0:T(4,128)S(1)}, u32[]{:S(2)}, u32[]{:S(2)}) async-start(f32[16,4,2048]{2,1,0:T(4,128)} %reshape.59), calls=%async_computation | async-start | bytes 1048576 | tf_op jit(solution)/shard_map/all_to_all | solution.py:154
  26.2 0.0 copy-done.6
  26.2 0.1 copy.19
  26.3 0.1 reshape_squeeze.6.cols_ref
  26.4 14.2 %all-to-all-done = f32[16,4,2048]{2,1,0:T(4,128)S(1)} async-done(((f32[16,4,2048]{2,1,0:T(4,128)}), f32[16,4,2048]{2,1,0:T(4,128)S(1)}, u32[]{:S(2)}, u32[]{:S(2)}) %all-to-all-start) | async-done | bytes 524320 | tf_op jit(solution)/shard_map/all_to_all | solution.py:154
  40.6 0.2 reshape.56.rows_ref
  40.8 0.0 copy-done
  40.8 0.0 copy-done.1
  40.8 0.0 copy-done.2
  40.8 0.0 copy-done.3
  40.8 0.0 copy-done.4
  40.8 0.0 copy-done.5
  40.8 5.8 %sddp_solve.1 = f32[16,4,2176]{2,1,0:T(4,128)S(1)} custom-call(s32[32]{0:T(128)S(1)} %reshape_squeeze.6.cols_ref, f32[64,2048]{1,0:T(8,128)S(1)} %reshape.56.rows_ref, f32[1,2048]{1,0:T(1,128)S(1)} %bitcast.19, f32[1,2048]{1,0:T(1,128)S(1)} %bitcast.20, f32[1,2048]{1,0:T(1,128)S(1)} %bitcast.21, f32[1,2048]{1,0:T(1,128)S(1)} %bitcast.22, ...), custom_call_target="tpu_custom_call" | custom-call | flops 1610612736 | bytes 3670016 | tf_op jit(solution)/shard_map/sddp_solve/pallas_call | solution.py:122
  46.7 19.6 %all_to_all.10 = f32[16,4,2176]{2,1,0:T(4,128)S(1)} all-to-all(f32[16,4,2176]{2,1,0:T(4,128)S(1)} %sddp_solve.1), channel_id=1, replica_groups=mesh['week'=32,'markov'=16] {'markov'}, dimensions={0} | all-to-all | bytes 1114112 | tf_op jit(solution)/shard_map/all_to_all | solution.py:158
  66.3 1.0 %gather_fusion.1 = f32[32,2176]{1,0:T(8,128)S(1)} fusion(f32[16,4,2176]{2,1,0:T(4,128)S(1)} %all_to_all.10, s32[32]{0:T(128)S(1)} %get-tuple-element.2), kind=kCustom, calls=%fused_computation.1 | custom fusion | bytes 557312 | tf_op jit(solution)/shard_map/gather | solution.py:159
  67.3 3.3 %collective-permute-start.1 = (f32[32,2176]{1,0:T(8,128)S(1)}, f32[32,2176]{1,0:T(8,128)S(1)}, u32[]{:S(2)}, u32[]{:S(2)}) collective-permute-start(f32[32,2176]{1,0:T(8,128)S(1)} %gather_fusion.1), channel_id=1, source_target_pairs={{0,496},{16,0},{32,16},{48,32},{64,48},{80,64},{96,80},{112,96},{1... | collective-permute-start | bytes 835592 | tf_op jit(solution)/shard_map/ppermute | solution.py:20
  70.6 12.7 %collective-permute-done.1 = f32[32,2176]{1,0:T(8,128)S(1)} collective-permute-done((f32[32,2176]{1,0:T(8,128)S(1)}, f32[32,2176]{1,0:T(8,128)S(1)}, u32[]{:S(2)}, u32[]{:S(2)}) %collective-permute-start.1) | collective-permute-done | bytes 278560 | tf_op jit(solution)/shard_map/ppermute | solution.py:20
  83.3 0.6 slice_reduce_fusion
  84.0 0.7 slice_bitcast_fusion
  (4 shorter events, 0.0 us)
Async XLA Ops:
  2.3 14.6 %collective-permute-start = (f32[32,2176]{1,0:T(8,128)S(1)}, f32[32,2176]{1,0:T(8,128)S(1)}, u32[]{:S(2)}, u32[]{:S(2)}) collective-permute-start(f32[32,2176]{1,0:T(8,128)S(1)} %pad_maximum_fusion), channel_id=1, source_target_pairs={{0,16},{16,32},{32,48},{48,64},{64,80},{80,96},{96,112},{112,128},... | collective-permute-start | bytes 835592 | tf_op jit(solution)/shard_map/ppermute | solution.py:20
  17.8 8.4 %copy-start.6 = (s32[1,1,16,2]{2,3,1,0:T(2,128)S(1)}, s32[1,1,16,2]{2,3,1,0:T(2,128)}, u32[]{:S(2)}) copy-start(s32[1,1,16,2]{2,3,1,0:T(2,128)} %param.17) | copy-start | bytes 388
  18.6 22.2 %copy-start = (f32[1,1,16,2,128,128]{5,4,3,2,1,0:T(8,128)S(1)}, f32[1,1,16,2,128,128]{5,4,3,2,1,0:T(8,128)}, u32[]{:S(2)}) copy-start(f32[1,1,16,2,128,128]{5,4,3,2,1,0:T(8,128)} %param.16) | copy-start | bytes 6291460
  18.6 22.2 %copy-start.1 = (f32[1,1,2048]{2,1,0:T(1,128)S(1)}, f32[1,1,2048]{2,1,0:T(1,128)}, u32[]{:S(2)}) copy-start(f32[1,1,2048]{2,1,0:T(1,128)} %param.11) | copy-start | bytes 24580
  18.6 22.2 %copy-start.2 = (f32[1,1,2048]{2,1,0:T(1,128)S(1)}, f32[1,1,2048]{2,1,0:T(1,128)}, u32[]{:S(2)}) copy-start(f32[1,1,2048]{2,1,0:T(1,128)} %param.12) | copy-start | bytes 24580
  18.7 22.2 %copy-start.3 = (f32[1,1,2048]{2,1,0:T(1,128)S(1)}, f32[1,1,2048]{2,1,0:T(1,128)}, u32[]{:S(2)}) copy-start(f32[1,1,2048]{2,1,0:T(1,128)} %param.13) | copy-start | bytes 24580
  18.7 22.2 %copy-start.4 = (f32[1,1,2048]{2,1,0:T(1,128)S(1)}, f32[1,1,2048]{2,1,0:T(1,128)}, u32[]{:S(2)}) copy-start(f32[1,1,2048]{2,1,0:T(1,128)} %param.14) | copy-start | bytes 24580
  18.7 22.2 %copy-start.5 = (f32[1,1,2048]{2,1,0:T(1,128)S(1)}, f32[1,1,2048]{2,1,0:T(1,128)}, u32[]{:S(2)}) copy-start(f32[1,1,2048]{2,1,0:T(1,128)} %param.15) | copy-start | bytes 24580
  19.6 21.0 %all-to-all-start = ((f32[16,4,2048]{2,1,0:T(4,128)}), f32[16,4,2048]{2,1,0:T(4,128)S(1)}, u32[]{:S(2)}, u32[]{:S(2)}) async-start(f32[16,4,2048]{2,1,0:T(4,128)} %reshape.59), calls=%async_computation | async-start | bytes 1048576 | tf_op jit(solution)/shard_map/all_to_all | solution.py:154
  67.3 16.1 %collective-permute-start.1 = (f32[32,2176]{1,0:T(8,128)S(1)}, f32[32,2176]{1,0:T(8,128)S(1)}, u32[]{:S(2)}, u32[]{:S(2)}) collective-permute-start(f32[32,2176]{1,0:T(8,128)S(1)} %gather_fusion.1), channel_id=1, source_target_pairs={{0,496},{16,0},{32,16},{48,32},{64,48},{80,64},{96,80},{112,96},{1... | collective-permute-start | bytes 835592 | tf_op jit(solution)/shard_map/ppermute | solution.py:20

commit v12 on v9

--- a/solution.py
+++ b/solution.py
@@ -35,7 +35,7 @@
 
 
 def solve_kernel(nblk, kblk, cols_ref, rows_ref, xi_ref, c_ref, q_ref, g_ref, h_ref, bv_ref,
-                 out_ref, base_s, p_s, u_s, v_s, acc_s, spread_s, fh, fl, ah, al):
+                 out_ref, base_s, p_s, u_s, v_s, acc_s, spread_s, shrink_s, fh, fl, ah, al):
     width = nblk * BS
     rows_n = rows_ref.shape[0]
 
@@ -62,11 +62,13 @@
         base_s[n] = rows_ref[:, s] + xi_ref[:, s] - g_ref[:, s]
         u_s[n] = jnp.zeros(u_s.shape[1:], jnp.float32)
 
+    for n in range(nblk):
+        q = q_ref[:, lanes(n)]
+        shrink_s[n] = q / (q + dual_step)
+
     for sweep in range(ITERS):
         for n in range(nblk):
-            s = lanes(n)
-            q = q_ref[:, s]
-            shrink = q / (q + dual_step)
+            shrink = shrink_s[n]
             if sweep == 0:
                 p_s[n] = (dual_step * base_s[n]) * shrink
             else:
@@ -110,6 +112,7 @@
     vspec = pl.BlockSpec(memory_space=pltpu.VMEM)
     field = pltpu.VMEM((nblk, count, BS), jnp.float32)
     scratch = [field] * 5 + [pltpu.VMEM((nblk, count, kblk * BS), jnp.float32)]
+    scratch += [pltpu.VMEM((nblk, 1, BS), jnp.float32)]
     scratch += [pltpu.VMEM((nblk, kblk * BS, BS), jnp.bfloat16)] * 2
     scratch += [pltpu.VMEM((nblk, BS, kblk * BS), jnp.bfloat16)] * 2
     flops = 2 * count * nblk * kblk * BS * BS * (2 * ITERS) * 3

time: 84.8 us -> 84.7 us (level)
  no operation moved by 1% of the time
where the time goes in v12:
time: 84.7 us; the launch traced here: 84.4 us
  waiting for transfers between devices  31.2 us (37%)
  starting transfers between devices  20.3 us (24%)
  blocking collectives  19.5 us (23%)
  Pallas kernels  5.53 us (7%)
  local copies, waits for them, and re-layouts  4.69 us (6%)
  other arithmetic  2.28 us (3%)
    all_to_all x1, blocking collectives, on_device(): back = lax.all_to_all(solved, 'markov', 0, 0, tiled=True)  19.5 us
    ppermute x2, waiting for transfers between devices, shifted(): return lax.ppermute(value, axis, pairs)  17 us
    all_to_all x1, waiting for transfers between devices, on_device(): arrived = lax.all_to_all(packed, 'markov', 0, 0, tiled=True)  14.2 us
    ppermute x2, starting transfers between devices, shifted(): return lax.ppermute(value, axis, pairs)  13.8 us
    all_to_all x1, starting transfers between devices, on_device(): arrived = lax.all_to_all(packed, 'markov', 0, 0, tiled=True)  6.57 us
    pallas_call x1, Pallas kernels, solve_block(): pl.pallas_call(functools.partial(solve_kernel, nblk, kblk), out_shape=jax...  5.53 us
  transfers between devices with their start and end apart: 3, of which 3 were waited for; matrix products, arithmetic and copies ran while one was open for 0% of the time, Pallas kernels for 0%

profile of v12, /device:TPU:57, one launch (start us, length us, event | category | flops | bytes accessed | tf_op | source)
XLA Modules:
  0.0 84.4 jit_solution(1323140807191762963)
XLA Ops:
  0.6 0.7 convert_bitcast_fusion
  1.3 0.1 broadcast_in_dim.17
  1.4 1.0 %pad_maximum_fusion = f32[32,2176]{1,0:T(8,128)S(1)} fusion(f32[32,128]{1,0:T(8,128)S(1)} %broadcast_in_dim.17, f32[32,2048]{1,0:T(8,128)} %bitcast.24), kind=kLoop, calls=%fused_computation.2 | loop fusion | flops 69632 | bytes 557056 | tf_op jit(solution)/shard_map/concatenate | solution.py:143
  2.3 10.4 %collective-permute-start = (f32[32,2176]{1,0:T(8,128)S(1)}, f32[32,2176]{1,0:T(8,128)S(1)}, u32[]{:S(2)}, u32[]{:S(2)}) collective-permute-start(f32[32,2176]{1,0:T(8,128)S(1)} %pad_maximum_fusion), channel_id=1, source_target_pairs={{0,16},{16,32},{32,48},{48,64},{64,80},{80,96},{96,112},{112,128},... | collective-permute-start | bytes 835592 | tf_op jit(solution)/shard_map/ppermute | solution.py:20
  12.7 4.2 %collective-permute-done = f32[32,2176]{1,0:T(8,128)S(1)} collective-permute-done((f32[32,2176]{1,0:T(8,128)S(1)}, f32[32,2176]{1,0:T(8,128)S(1)}, u32[]{:S(2)}, u32[]{:S(2)}) %collective-permute-start) | collective-permute-done | bytes 278560 | tf_op jit(solution)/shard_map/ppermute | solution.py:20
  17.0 0.1 fusion.7
  17.1 0.1 fusion.6
  17.2 0.1 reduce_window_sum.11
  17.2 0.2 select_reduce_fusion.1
  17.4 0.1 copy.20
  17.5 0.1 copy.21
  17.6 0.1 fusion.3
  17.7 0.1 select_reduce_fusion
  17.8 0.0 copy-start.6
  17.9 0.8 gather_fusion
  18.6 0.0 copy-start
  18.6 0.0 copy-start.1
  18.6 0.0 copy-start.2
  18.7 0.0 copy-start.3
  18.7 0.0 copy-start.4
  18.7 0.0 copy-start.5
  18.7 0.9 %reshape.59 = f32[16,4,2048]{2,1,0:T(4,128)} reshape(f32[64,2048]{1,0:T(8,128)S(1)} %gather_fusion) | data formatting | bytes 1048576 | tf_op jit(solution)/shard_map/jit(_take)/gather | solution.py:150
  19.6 6.6 %all-to-all-start = ((f32[16,4,2048]{2,1,0:T(4,128)}), f32[16,4,2048]{2,1,0:T(4,128)S(1)}, u32[]{:S(2)}, u32[]{:S(2)}) async-start(f32[16,4,2048]{2,1,0:T(4,128)} %reshape.59), calls=%async_computation | async-start | bytes 1048576 | tf_op jit(solution)/shard_map/all_to_all | solution.py:151
  26.2 0.0 copy-done.6
  26.2 0.1 copy.19
  26.3 0.1 reshape_squeeze.6.cols_ref
  26.4 14.2 %all-to-all-done = f32[16,4,2048]{2,1,0:T(4,128)S(1)} async-done(((f32[16,4,2048]{2,1,0:T(4,128)}), f32[16,4,2048]{2,1,0:T(4,128)S(1)}, u32[]{:S(2)}, u32[]{:S(2)}) %all-to-all-start) | async-done | bytes 524320 | tf_op jit(solution)/shard_map/all_to_all | solution.py:151
  40.6 0.2 reshape.56.rows_ref
  40.8 0.0 copy-done
  40.8 0.0 copy-done.1
  40.8 0.0 copy-done.2
  40.8 0.0 copy-done.3
  40.8 0.0 copy-done.4
  40.8 0.0 copy-done.5
  40.8 5.5 %sddp_solve.1 = f32[16,4,2176]{2,1,0:T(4,128)S(1)} custom-call(s32[32]{0:T(128)S(1)} %reshape_squeeze.6.cols_ref, f32[64,2048]{1,0:T(8,128)S(1)} %reshape.56.rows_ref, f32[1,2048]{1,0:T(1,128)S(1)} %bitcast.19, f32[1,2048]{1,0:T(1,128)S(1)} %bitcast.20, f32[1,2048]{1,0:T(1,128)S(1)} %bitcast.21, f32[1,2048]{1,0:T(1,128)S(1)} %bitcast.22, ...), custom_call_target="tpu_custom_call" | custom-call | flops 1610612736 | bytes 3670016 | tf_op jit(solution)/shard_map/sddp_solve/pallas_call | solution.py:119
  46.4 19.5 %all_to_all.10 = f32[16,4,2176]{2,1,0:T(4,128)S(1)} all-to-all(f32[16,4,2176]{2,1,0:T(4,128)S(1)} %sddp_solve.1), channel_id=1, replica_groups=mesh['week'=32,'markov'=16] {'markov'}, dimensions={0} | all-to-all | bytes 1114112 | tf_op jit(solution)/shard_map/all_to_all | solution.py:155
  65.9 1.0 %gather_fusion.1 = f32[32,2176]{1,0:T(8,128)S(1)} fusion(f32[16,4,2176]{2,1,0:T(4,128)S(1)} %all_to_all.10, s32[32]{0:T(128)S(1)} %get-tuple-element.2), kind=kCustom, calls=%fused_computation.1 | custom fusion | bytes 557312 | tf_op jit(solution)/shard_map/gather | solution.py:156
  66.9 3.4 %collective-permute-start.1 = (f32[32,2176]{1,0:T(8,128)S(1)}, f32[32,2176]{1,0:T(8,128)S(1)}, u32[]{:S(2)}, u32[]{:S(2)}) collective-permute-start(f32[32,2176]{1,0:T(8,128)S(1)} %gather_fusion.1), channel_id=1, source_target_pairs={{0,496},{16,0},{32,16},{48,32},{64,48},{80,64},{96,80},{112,96},{1... | collective-permute-start | bytes 835592 | tf_op jit(solution)/shard_map/ppermute | solution.py:20
  70.3 12.8 %collective-permute-done.1 = f32[32,2176]{1,0:T(8,128)S(1)} collective-permute-done((f32[32,2176]{1,0:T(8,128)S(1)}, f32[32,2176]{1,0:T(8,128)S(1)}, u32[]{:S(2)}, u32[]{:S(2)}) %collective-permute-start.1) | collective-permute-done | bytes 278560 | tf_op jit(solution)/shard_map/ppermute | solution.py:20
  83.1 0.6 slice_reduce_fusion
  83.7 0.7 slice_bitcast_fusion
  (4 shorter events, 0.0 us)
Async XLA Ops:
  2.3 14.6 %collective-permute-start = (f32[32,2176]{1,0:T(8,128)S(1)}, f32[32,2176]{1,0:T(8,128)S(1)}, u32[]{:S(2)}, u32[]{:S(2)}) collective-permute-start(f32[32,2176]{1,0:T(8,128)S(1)} %pad_maximum_fusion), channel_id=1, source_target_pairs={{0,16},{16,32},{32,48},{48,64},{64,80},{80,96},{96,112},{112,128},... | collective-permute-start | bytes 835592 | tf_op jit(solution)/shard_map/ppermute | solution.py:20
  17.8 8.4 %copy-start.6 = (s32[1,1,16,2]{2,3,1,0:T(2,128)S(1)}, s32[1,1,16,2]{2,3,1,0:T(2,128)}, u32[]{:S(2)}) copy-start(s32[1,1,16,2]{2,3,1,0:T(2,128)} %param.17) | copy-start | bytes 388
  18.6 22.2 %copy-start = (f32[1,1,16,2,128,128]{5,4,3,2,1,0:T(8,128)S(1)}, f32[1,1,16,2,128,128]{5,4,3,2,1,0:T(8,128)}, u32[]{:S(2)}) copy-start(f32[1,1,16,2,128,128]{5,4,3,2,1,0:T(8,128)} %param.16) | copy-start | bytes 6291460
  18.6 22.2 %copy-start.1 = (f32[1,1,2048]{2,1,0:T(1,128)S(1)}, f32[1,1,2048]{2,1,0:T(1,128)}, u32[]{:S(2)}) copy-start(f32[1,1,2048]{2,1,0:T(1,128)} %param.11) | copy-start | bytes 24580
  18.6 22.2 %copy-start.2 = (f32[1,1,2048]{2,1,0:T(1,128)S(1)}, f32[1,1,2048]{2,1,0:T(1,128)}, u32[]{:S(2)}) copy-start(f32[1,1,2048]{2,1,0:T(1,128)} %param.12) | copy-start | bytes 24580
  18.7 22.2 %copy-start.3 = (f32[1,1,2048]{2,1,0:T(1,128)S(1)}, f32[1,1,2048]{2,1,0:T(1,128)}, u32[]{:S(2)}) copy-start(f32[1,1,2048]{2,1,0:T(1,128)} %param.13) | copy-start | bytes 24580
  18.7 22.2 %copy-start.4 = (f32[1,1,2048]{2,1,0:T(1,128)S(1)}, f32[1,1,2048]{2,1,0:T(1,128)}, u32[]{:S(2)}) copy-start(f32[1,1,2048]{2,1,0:T(1,128)} %param.14) | copy-start | bytes 24580
  18.7 22.2 %copy-start.5 = (f32[1,1,2048]{2,1,0:T(1,128)S(1)}, f32[1,1,2048]{2,1,0:T(1,128)}, u32[]{:S(2)}) copy-start(f32[1,1,2048]{2,1,0:T(1,128)} %param.15) | copy-start | bytes 24580
  19.6 21.0 %all-to-all-start = ((f32[16,4,2048]{2,1,0:T(4,128)}), f32[16,4,2048]{2,1,0:T(4,128)S(1)}, u32[]{:S(2)}, u32[]{:S(2)}) async-start(f32[16,4,2048]{2,1,0:T(4,128)} %reshape.59), calls=%async_computation | async-start | bytes 1048576 | tf_op jit(solution)/shard_map/all_to_all | solution.py:151
  66.9 16.1 %collective-permute-start.1 = (f32[32,2176]{1,0:T(8,128)S(1)}, f32[32,2176]{1,0:T(8,128)S(1)}, u32[]{:S(2)}, u32[]{:S(2)}) collective-permute-start(f32[32,2176]{1,0:T(8,128)S(1)} %gather_fusion.1), channel_id=1, source_target_pairs={{0,496},{16,0},{32,16},{48,32},{64,48},{80,64},{96,80},{112,96},{1... | collective-permute-start | bytes 835592 | tf_op jit(solution)/shard_map/ppermute | solution.py:20
